TPU v7x, 32 devices: a whole 2x2x4 slice. The times are simulated.
32 devices in a mesh: subtree: 4 (over y, core), tile: 8 (over z, x).
Axes of the slice: x: 2, y: 2, z: 4, core: 2. Of those that a mesh axis runs over, the one named last changes fastest.
Arguments:
- interface_stiffness: float32 [4, 4096, 4096], P('subtree', 'tile'), may hold values from -3 to 3
- lower_factor: bfloat16 [4, 4096, 512], P('subtree', 'tile'), may hold values from -0.25 to 0.25
- upper_factor: bfloat16 [4, 512, 4096], P('subtree', None, 'tile'), may hold values from -6 to 6
- modes: bfloat16 [4096, 256], P('tile'), may hold values from -0.09375 to 0.09375
- gyro_rows: int32 [512], replicated, may hold values from 0 to 4095, as said below
- gyro_coupling: float32 [512, 512], replicated, may hold values from -24 to 24
- spin_softening: float32 [512], replicated, may hold values from 0.5 to 8
- speed_index: int32 [2], replicated, may hold values from 0 to 63
Outputs:
- schur: float32 [4096, 4096], P('tile', 'subtree')
- campbell: float32 [2, 256, 256], P(None, 'tile', 'subtree')
Inputs may be any that keep to these rules, and one draw needn't show every extreme that they name: `gyro_rows`: distinct interface degrees of freedom, in whole aligned blocks of 8 consecutive ones.
All inputs are finite; a program needn't handle non-finite values.
Results may differ from a plain program's by a relative error of at most 0.0003.
Values may be sent and summed in bfloat16 or wider, within the bound.
No kernel may reach another device: no remote copies, remote signals or barrier semaphores. Data moves between devices by JAX's collectives and lax.ppermute only.
A program may use at most 64 MiB of HBM per device.

v0:
```python
import jax
import jax.numpy as jnp
from jax import lax
from jax.sharding import PartitionSpec as P

SPEED_STEPS = 64


OMEGA_TOP = 2.0


def partner(block, axis, distance):
    count = lax.axis_size(axis)
    route = []
    for low in range(count):
        high = low | 1 << distance
        if high != low and high < count:
            route += [(low, high), (high, low)]
    return lax.ppermute(block, axis, route)


def shards(
    interface_stiffness,
    lower_factor,
    upper_factor,
    modes,
    gyro_rows,
    gyro_coupling,
    spin_softening,
    speed_index,
):
    tile_count = lax.axis_size("tile")
    branch_count = lax.axis_size("subtree")
    tile_pos = lax.axis_index("tile")
    branch_pos = lax.axis_index("subtree")
    mode_count = modes.shape[1]
    mode_cols = mode_count // branch_count
    mode_rows_dev = mode_count // tile_count
    coupled = jnp.einsum(
        "lrk,lkn->rn",
        lower_factor,
        lax.all_gather(upper_factor, "tile", axis=2, tiled=True),
        preferred_element_type=jnp.float32,
    )
    schur_rows = jnp.sum(interface_stiffness, axis=0) - coupled
    full_width = schur_rows.shape[1]
    own_width = full_width // branch_count
    own_first = branch_pos * own_width
    schur_part = schur_rows
    for level_bit in range(branch_count.bit_length() - 1):
        schur_part = schur_part + partner(schur_part, "subtree", level_bit)
    schur_out = lax.dynamic_slice_in_dim(schur_part, own_first, own_width, 1)
    col_first = branch_pos * mode_cols
    segment = lax.all_gather(modes, "tile", axis=0, tiled=True)
    row_count = segment.shape[0]
    wanted = lax.dynamic_slice_in_dim(segment, col_first, mode_cols, 1).astype(jnp.float32)
    response = jnp.dot(
        schur_part, wanted, precision=lax.Precision.HIGHEST, preferred_element_type=jnp.float32
    )
    inside = (gyro_rows >= 0) & (gyro_rows < row_count)
    taken = jnp.take(segment, jnp.clip(gyro_rows, 0, row_count - 1), axis=0).astype(jnp.float32)
    picked = jnp.where(inside[:, None], taken, jnp.float32(0.0))
    response, picked = (response, picked)
    local_modes = modes.astype(jnp.float32)
    partial_value = jnp.einsum(
        "rm,rc->mc",
        local_modes,
        response,
        precision=lax.Precision.HIGHEST,
        preferred_element_type=jnp.float32,
    )
    stiff_block = lax.psum_scatter(partial_value, "tile", scatter_dimension=0, tiled=True)
    skew_part = 0.5 * (gyro_coupling - gyro_coupling.T)
    left_modes = lax.dynamic_slice_in_dim(picked, tile_pos * mode_rows_dev, mode_rows_dev, 1)
    right_modes = lax.dynamic_slice_in_dim(picked, branch_pos * mode_cols, mode_cols, 1)
    turned = jnp.dot(
        skew_part, right_modes, precision=lax.Precision.HIGHEST, preferred_element_type=jnp.float32
    )
    gyro_block = jnp.einsum(
        "gm,gc->mc",
        left_modes,
        turned,
        precision=lax.Precision.HIGHEST,
        preferred_element_type=jnp.float32,
    )
    spin_block = jnp.einsum(
        "gm,gc->mc",
        left_modes,
        spin_softening[:, None] * right_modes,
        precision=lax.Precision.HIGHEST,
        preferred_element_type=jnp.float32,
    )
    speeds_omega = OMEGA_TOP * (speed_index.astype(jnp.float32) + 1.0) / SPEED_STEPS
    campbell = (
        stiff_block[None]
        + speeds_omega[:, None, None] * gyro_block[None]
        - (speeds_omega * speeds_omega)[:, None, None] * spin_block[None]
    )
    return (schur_out, campbell)


def solution(mesh):
    placed = (
        P("subtree", "tile", None),
        P("subtree", "tile", None),
        P("subtree", None, "tile"),
        P("tile", None),
        P(),
        P(),
        P(),
        P(),
    )
    return jax.shard_map(
        shards,
        mesh=mesh,
        in_specs=placed,
        out_specs=(P("tile", "subtree"), P(None, "tile", "subtree")),
        check_vma=False,
    )
```

profile of v0, /device:TPU:0, one launch (start us, length us, event | category | flops | bytes accessed | tf_op | source)
XLA Modules:
  0.0 391.6 jit_solution(2700897672948704366)
XLA Ops:
  7.2 0.0 copy-start
  7.2 0.0 all-gather.3.cloned.1.call-start
  7.2 0.7 all-gather.3.cloned.1.call-update
  7.9 0.0 all-gather.5.cloned.1.call-start
  8.0 79.8 %all-gather.3.cloned.1.call-done = bf16[1,512,4096]{2,1,0:T(8,128)(2,1)} async-done(((bf16[1,512,512]{2,1,0:T(8,128)(2,1)}), bf16[1,512,4096]{2,1,0:T(8,128)(2,1)}) %all-gather.3.cloned.1.call-update) | async-done | bytes 4194320 | tf_op jit(solution)/shard_map/all_gather | solution.py:42
  87.8 0.0 copy-done
  87.8 7.0 %bitcast_subtract_fusion = f32[512,4096]{1,0:T(8,128)S(1)} fusion(f32[1,512,4096]{2,1,0:T(8,128)} %param.8, bf16[1,512,4096]{2,1,0:T(8,128)(2,1)} %all-gather.3.cloned.1.call-done, bf16[1,512,512]{2,1,0:T(8,128)(2,1)S(1)} %copy-done), kind=kOutput, calls=%fused_computation.1 | convolution fusion | flops 2149580800 | bytes 21495808 | tf_op jit(solution)/shard_map/lrk,lkn->rn/dot_general | solution.py:39
  94.8 0.0 copy-start.1
  94.8 3.2 copy-done.1
  98.1 0.1 collective-permute-start
  98.2 13.3 %collective-permute-done = f32[512,4096]{1,0:T(8,128)} collective-permute-done((f32[512,4096]{1,0:T(8,128)S(1)}, f32[512,4096]{1,0:T(8,128)}, u32[]{:S(2)}, u32[]{:S(2)}) %collective-permute-start) | collective-permute-done | bytes 8388640 | tf_op jit(solution)/shard_map/ppermute | solution.py:19
  111.4 11.1 %add.35 = f32[512,4096]{1,0:T(8,128)} add(f32[512,4096]{1,0:T(8,128)} %copy-done.1, f32[512,4096]{1,0:T(8,128)} %collective-permute-done) | non-fusion elementwise | flops 2097152 | bytes 25165824 | tf_op jit(solution)/shard_map/add | solution.py:51
  122.6 1.5 collective-permute-start.1
  124.1 0.0 all-gather.5.cloned.1.call-update
  124.1 0.0 reduce-scatter.4.cloned.1.call-start
  124.1 0.0 copy-done.3
  124.2 0.3 copy.13
  124.6 46.2 %all-gather.5.cloned.1.call-done = bf16[4096,256]{1,0:T(8,128)(2,1)} async-done(((bf16[512,256]{1,0:T(8,128)(2,1)}), bf16[4096,256]{1,0:T(8,128)(2,1)}) %all-gather.5.cloned.1.call-update) | async-done | bytes 2097168 | tf_op jit(solution)/shard_map/all_gather | solution.py:54
  170.8 3.4 gather_fusion
  174.2 0.2 convert_select_fusion
  174.4 0.8 fusion.8
  175.3 1.1 fusion.2
  176.4 0.7 fusion.13
  177.0 128.3 %collective-permute-done.1 = f32[512,4096]{1,0:T(8,128)} collective-permute-done((f32[512,4096]{1,0:T(8,128)}, f32[512,4096]{1,0:T(8,128)}, u32[]{:S(2)}, u32[]{:S(2)}) %collective-permute-start.1) | collective-permute-done | bytes 8388640 | tf_op jit(solution)/shard_map/ppermute | solution.py:19
  305.4 11.1 %add.36 = f32[512,4096]{1,0:T(8,128)} add(f32[512,4096]{1,0:T(8,128)} %add.35, f32[512,4096]{1,0:T(8,128)} %collective-permute-done.1) | non-fusion elementwise | flops 2097152 | bytes 25165824 | tf_op jit(solution)/shard_map/add | solution.py:51
  316.5 6.7 %fusion.4 = f32[512,64]{1,0:T(8,128)S(1)} fusion(f32[512,4096]{1,0:T(8,128)} %add.36, bf16[4096,256]{1,0:T(8,128)(2,1)S(1)} %copy-done.2, s32[]{:T(128)S(6)} %select_n.24), kind=kOutput, calls=%fused_computation.7 | convolution fusion | flops 1610612736 | bytes 9568260 | tf_op jit(solution)/shard_map/dot_general | solution.py:57
  323.3 0.4 convolution_bitcast_fusion
  323.6 0.8 copy.14
  324.4 0.0 reduce-scatter.4.cloned.1.call-update
  324.4 3.2 constant_dynamic-slice_fusion
  327.6 56.0 %reduce-scatter.4.cloned.1.call-done = f32[32,64]{1,0:T(8,128)} async-done(((f32[256,64]{1,0:T(8,128)}), f32[32,64]{1,0:T(8,128)}) %reduce-scatter.4.cloned.1.call-update) | async-done | bytes 8208 | tf_op jit(solution)/shard_map/reduce_scatter | solution.py:72
  383.6 1.4 multiply_subtract_fusion
  (15 shorter events, 0.1 us)
Async XLA Ops:
  7.2 80.6 %copy-start = (bf16[1,512,512]{2,1,0:T(8,128)(2,1)S(1)}, bf16[1,512,512]{2,1,0:T(8,128)(2,1)}, u32[]{:S(2)}) copy-start(bf16[1,512,512]{2,1,0:T(8,128)(2,1)} %param.9) | copy-start | bytes 1572868
  7.2 80.6 %all-gather.3.cloned.1.call-start = ((), (), s32[]{:S(2)}) async-start(), calls=%async_computation.1 | async-start | bytes 4718592 | tf_op jit(solution)/shard_map/all_gather | solution.py:42
  7.9 162.9 %all-gather.5.cloned.1.call-start = ((), (), s32[]{:S(2)}) async-start(), calls=%async_computation.2 | async-start | bytes 2359296 | tf_op jit(solution)/shard_map/all_gather | solution.py:54
  94.8 3.2 copy-start.1
  98.1 26.1 %copy-start.3 = (f32[512,512]{1,0:T(8,128)S(1)}, f32[512,512]{1,0:T(8,128)}, u32[]{:S(2)}) copy-start(f32[512,512]{1,0:T(8,128)} %param.13) | copy-start | bytes 3145732
  98.1 26.4 %copy-start.5 = (s32[512]{0:T(512)S(1)}, s32[512]{0:T(512)}, u32[]{:S(2)}) copy-start(s32[512]{0:T(512)} %param.12) | copy-start | bytes 6148
  98.1 26.5 %copy-start.7 = (s32[2]{0:T(128)S(1)}, s32[2]{0:T(128)}, u32[]{:S(2)}) copy-start(s32[2]{0:T(128)} %param.15) | copy-start | bytes 28
  98.1 76.4 %copy-start.6 = (f32[512]{0:T(512)S(1)}, f32[512]{0:T(512)}, u32[]{:S(2)}) copy-start(f32[512]{0:T(512)} %param.14) | copy-start | bytes 6148
  98.1 13.4 %collective-permute-start = (f32[512,4096]{1,0:T(8,128)S(1)}, f32[512,4096]{1,0:T(8,128)}, u32[]{:S(2)}, u32[]{:S(2)}) collective-permute-start(f32[512,4096]{1,0:T(8,128)S(1)} %bitcast_subtract_fusion), channel_id=1, source_target_pairs={{0,8},{8,0},{16,24},{24,16},{1,9},{9,1},{17,25},{25,17},{2,10},{10... | collective-permute-start | bytes 25165832 | tf_op jit(solution)/shard_map/ppermute | solution.py:19
  122.6 182.8 %collective-permute-start.1 = (f32[512,4096]{1,0:T(8,128)}, f32[512,4096]{1,0:T(8,128)}, u32[]{:S(2)}, u32[]{:S(2)}) collective-permute-start(f32[512,4096]{1,0:T(8,128)} %add.35), channel_id=1, source_target_pairs={{0,16},{16,0},{8,24},{24,8},{1,17},{17,1},{9,25},{25,9},{2,18},{18... | collective-permute-start | bytes 25165832 | tf_op jit(solution)/shard_map/ppermute | solution.py:19
  124.1 259.5 %reduce-scatter.4.cloned.1.call-start = ((), (), s32[]{:S(2)}) async-start(), calls=%async_computation.3 | async-start | bytes 147456 | tf_op jit(solution)/shard_map/reduce_scatter | solution.py:72
  177.0 139.5 %copy-start.2 = (bf16[4096,256]{1,0:T(8,128)(2,1)S(1)}, bf16[4096,256]{1,0:T(8,128)(2,1)}, u32[]{:S(2)}) copy-start(bf16[4096,256]{1,0:T(8,128)(2,1)} %all-gather.5.cloned.1.call-done) | copy-start | bytes 6291460
  316.5 6.7 %copy-start.4 = (bf16[512,256]{1,0:T(8,128)(2,1)S(1)}, bf16[512,256]{1,0:T(8,128)(2,1)}, u32[]{:S(2)}) copy-start(bf16[512,256]{1,0:T(8,128)(2,1)} %param.11) | copy-start | bytes 786436
Sparse Core Ops, SparseCore 0:
  10.1 77.7 all-gather.2
  124.2 46.5 all-gather.4
  324.5 59.0 reduce-scatter.3
where the time goes:
time: 392 us
  waiting for transfers between devices  324 us (83%)
  other arithmetic  23.9 us (6%)
  matrix products  16.7 us (4%)
  between operations  13.9 us (4%)
  local copies, waits for them, and re-layouts  10.9 us (3%)
    ppermute x2, waiting for transfers between devices, partner(): return lax.ppermute(block, axis, route)  142 us
    all_gather x1, waiting for transfers between devices, shards(): lax.all_gather(upper_factor, 'tile', axis=2, tiled=True)  79.8 us
    reduce_scatter x1, waiting for transfers between devices, shards(): lax.psum_scatter(partial_value, 'tile', scatter_dimension=0, tiled=True)  56 us
    all_gather x1, waiting for transfers between devices, shards(): segment = lax.all_gather(modes, 'tile', axis=0, tiled=True)  46.2 us
    add x2, other arithmetic, shards(): schur_part = schur_part + partner(schur_part, 'subtree', level_bit)  22.3 us
  transfers between devices with their start and end apart: 5, of which 5 were waited for; matrix products, arithmetic and copies ran while one was open for 2% of the time, Pallas kernels for 0%

commit v1 on v0

v1 whole, which is shorter than its diff:
```python
import jax
import jax.numpy as jnp
from jax import lax
from jax.sharding import PartitionSpec as P

SPEED_STEPS = 64


OMEGA_TOP = 2.0

SHARE_SCALE = 32.0


def omegas(speed_index):
    return OMEGA_TOP * (speed_index.astype(jnp.float32) + 1.0) / SPEED_STEPS


def combine(stiff_block, gyro_block, spin_block, speed_index):
    speeds_omega = omegas(speed_index)
    return (
        stiff_block[None]
        + speeds_omega[:, None, None] * gyro_block[None]
        - (speeds_omega * speeds_omega)[:, None, None] * spin_block[None]
    )


def gyro_parts(picked, gyro_coupling, spin_softening, left_first, left_count, right_first, right_count):
    skew_part = 0.5 * (gyro_coupling - gyro_coupling.T)
    left_modes = lax.dynamic_slice_in_dim(picked, left_first, left_count, 1)
    right_modes = lax.dynamic_slice_in_dim(picked, right_first, right_count, 1)
    turned = jnp.dot(
        skew_part, right_modes, precision=lax.Precision.HIGHEST, preferred_element_type=jnp.float32
    )
    gyro_block = jnp.einsum(
        "gm,gc->mc",
        left_modes,
        turned,
        precision=lax.Precision.HIGHEST,
        preferred_element_type=jnp.float32,
    )
    spin_block = jnp.einsum(
        "gm,gc->mc",
        left_modes,
        spin_softening[:, None] * right_modes,
        precision=lax.Precision.HIGHEST,
        preferred_element_type=jnp.float32,
    )
    return gyro_block, spin_block


def partner(block, axis, distance):
    count = lax.axis_size(axis)
    route = []
    for low in range(count):
        high = low | 1 << distance
        if high != low and high < count:
            route += [(low, high), (high, low)]
    return lax.ppermute(block, axis, route)


def shards_any(
    interface_stiffness,
    lower_factor,
    upper_factor,
    modes,
    gyro_rows,
    gyro_coupling,
    spin_softening,
    speed_index,
):
    tile_count = lax.axis_size("tile")
    branch_count = lax.axis_size("subtree")
    tile_pos = lax.axis_index("tile")
    branch_pos = lax.axis_index("subtree")
    mode_count = modes.shape[1]
    mode_cols = mode_count // branch_count
    mode_rows_dev = mode_count // tile_count
    coupled = jnp.einsum(
        "lrk,lkn->rn",
        lower_factor,
        lax.all_gather(upper_factor, "tile", axis=2, tiled=True),
        preferred_element_type=jnp.float32,
    )
    schur_part = jnp.sum(interface_stiffness, axis=0) - coupled
    own_width = schur_part.shape[1] // branch_count
    for level_bit in range(branch_count.bit_length() - 1):
        schur_part = schur_part + partner(schur_part, "subtree", level_bit)
    schur_out = lax.dynamic_slice_in_dim(schur_part, branch_pos * own_width, own_width, 1)
    segment = lax.all_gather(modes, "tile", axis=0, tiled=True)
    wanted = lax.dynamic_slice_in_dim(segment, branch_pos * mode_cols, mode_cols, 1)
    response = jnp.dot(
        schur_part,
        wanted.astype(jnp.float32),
        precision=lax.Precision.HIGHEST,
        preferred_element_type=jnp.float32,
    )
    partial_value = jnp.einsum(
        "rm,rc->mc",
        modes.astype(jnp.float32),
        response,
        precision=lax.Precision.HIGHEST,
        preferred_element_type=jnp.float32,
    )
    stiff_block = lax.psum_scatter(partial_value, "tile", scatter_dimension=0, tiled=True)
    picked = jnp.take(segment, gyro_rows, axis=0, mode="clip").astype(jnp.float32)
    gyro_block, spin_block = gyro_parts(
        picked,
        gyro_coupling,
        spin_softening,
        tile_pos * mode_rows_dev,
        mode_rows_dev,
        branch_pos * mode_cols,
        mode_cols,
    )
    return (schur_out, combine(stiff_block, gyro_block, spin_block, speed_index))


def shards_ring(
    interface_stiffness,
    lower_factor,
    upper_factor,
    modes,
    gyro_rows,
    gyro_coupling,
    spin_softening,
    speed_index,
):
    f32 = jnp.float32
    tiles = lax.axis_size("tile")
    branches = lax.axis_size("subtree")
    tile = lax.axis_index("tile")
    branch = lax.axis_index("subtree")
    z, x = tile // 2, tile % 2
    y, core = branch // 2, branch % 2
    stiffness = interface_stiffness[0]
    lower = lower_factor[0]
    upper = upper_factor[0]
    rows, width = stiffness.shape
    depth, cols = upper.shape
    mode_count = modes.shape[1]

    def gray(i):
        return i ^ (i >> 1)

    def over_z(block):
        step = [(gray(p) * 2 + a, gray((p + 1) % 4) * 2 + a) for p in range(4) for a in range(2)]
        return lax.ppermute(block, "tile", step)

    def over_x(block):
        return lax.ppermute(block, "tile", [(i, i ^ 1) for i in range(tiles)])

    def over_y(block):
        return lax.ppermute(block, "subtree", [(i, i ^ 2) for i in range(branches)])

    def over_core(block):
        return lax.ppermute(block, "subtree", [(i, i ^ 1) for i in range(branches)])

    from_z = [gray((gray(z) - k) % 4) for k in range(4)]
    from_x = [x, 1 - x]

    chunk = modes.shape[0] // branches
    mine = lax.dynamic_slice_in_dim(modes, branch * chunk, chunk, 0)
    mode_z = [mine]
    for _ in range(3):
        mode_z.append(over_z(mode_z[-1]))
    mode_own = jnp.stack(mode_z)
    mode_other = over_x(mode_own)
    quarter = jnp.zeros((4, 2, chunk, mode_count), modes.dtype)
    for k in range(4):
        for j, source in enumerate((mode_own, mode_other)):
            quarter = lax.dynamic_update_slice(
                quarter, source[k][None, None], (from_z[k], from_x[j], 0, 0)
            )
    quarter = quarter.reshape(tiles, chunk, mode_count)
    across = over_y(quarter)
    half = jnp.stack(
        [jnp.where(y == 0, quarter, across), jnp.where(y == 0, across, quarter)], axis=1
    )
    beside = over_core(half)
    all_modes = jnp.stack(
        [jnp.where(core == 0, half, beside), jnp.where(core == 0, beside, half)], axis=2
    ).reshape(tiles * modes.shape[0], mode_count)

    z1, x0 = lax.optimization_barrier((over_z(upper), over_x(upper)))
    z2, x1 = lax.optimization_barrier((over_z(z1), over_x(z1)))
    z3, x2 = lax.optimization_barrier((over_z(z2), over_x(z2)))
    cut = depth // 2
    x3_low, x3_high = over_x(z3[:cut]), over_z(x2[cut:])

    def first_col(k, j):
        return (from_z[k] * 2 + from_x[j]) * cols

    def share(k, j, product):
        return lax.dynamic_slice_in_dim(stiffness, first_col(k, j), cols, 1) - product

    def times(left, right):
        return jnp.dot(left, right, preferred_element_type=f32)

    parts = [
        [share(k, 0, times(lower, block)) for k, block in enumerate((upper, z1, z2, z3))],
        [share(k, 1, times(lower, block)) for k, block in enumerate((x0, x1, x2))],
    ]
    parts[1].append(share(3, 1, times(lower[:, :cut], x3_low) + times(lower[:, cut:], x3_high)))

    response = jnp.zeros((rows, mode_count), f32)
    for j in range(2):
        for k in range(4):
            block_modes = lax.dynamic_slice_in_dim(all_modes, first_col(k, j), cols, 0)
            response = response + jnp.dot(
                parts[j][k],
                block_modes.astype(f32),
                precision=lax.Precision.HIGH,
                preferred_element_type=f32,
            )
    reduced = jnp.einsum(
        "rm,rc->mc",
        modes.astype(f32),
        response,
        precision=lax.Precision.HIGH,
        preferred_element_type=f32,
    )
    mode_rows = mode_count // tiles
    mode_cols = mode_count // branches
    pieces = reduced.reshape(tiles, mode_rows, branches, mode_cols).transpose(2, 0, 1, 3)
    pieces = pieces.reshape(branches * tiles, mode_rows, mode_cols)
    pieces = lax.all_to_all(pieces, ("subtree", "tile"), 0, 0)
    stiff_block = jnp.sum(pieces, axis=0)

    final = []
    keep_first = [from_z[k] % 2 == core for k in range(2)]
    kept_z = [jnp.where(keep_first[k], from_z[k], from_z[k + 2]) for k in range(2)]
    stays = kept_z[0] // 2 == y
    for j in range(2):
        both = []
        for k in range(2):
            kept = jnp.where(keep_first[k], parts[j][k], parts[j][k + 2])
            sent = jnp.where(keep_first[k], parts[j][k + 2], parts[j][k])
            both.append(kept + over_core(sent))
        sent = jnp.where(stays, both[1], both[0])
        arrived = over_y((sent * SHARE_SCALE).astype(jnp.float16))
        final.append(
            jnp.where(stays, both[0], both[1]) + arrived.astype(f32) * (1.0 / SHARE_SCALE)
        )
    schur_out = jnp.concatenate(
        [jnp.where(x == 0, final[0], final[1]), jnp.where(x == 0, final[1], final[0])], axis=1
    )

    picked = jnp.take(all_modes, gyro_rows, axis=0, mode="clip").astype(f32)
    gyro_block, spin_block = gyro_parts(
        picked,
        gyro_coupling,
        spin_softening,
        tile * mode_rows,
        mode_rows,
        branch * mode_cols,
        mode_cols,
    )
    return (schur_out, combine(stiff_block, gyro_block, spin_block, speed_index))


def solution(mesh):
    placed = (
        P("subtree", "tile", None),
        P("subtree", "tile", None),
        P("subtree", None, "tile"),
        P("tile", None),
        P(),
        P(),
        P(),
        P(),
    )
    ring = (mesh.shape["subtree"], mesh.shape["tile"]) == (4, 8)
    return jax.shard_map(
        shards_ring if ring else shards_any,
        mesh=mesh,
        in_specs=placed,
        out_specs=(P("tile", "subtree"), P(None, "tile", "subtree")),
        check_vma=False,
    )
```

time: 392 us -> 159 us (0.41)
  waiting for transfers between devices: 324 us -> 48.6 us
  local copies, waits for them, and re-layouts: 10.9 us -> 42.7 us
  starting transfers between devices: 1.67 us -> 27.8 us
  between operations: 13.9 us -> 1.29 us
  other arithmetic: 23.9 us -> 14.4 us
  matrix products: 16.7 us -> 22.9 us
    all_gather x2 -> x0, waiting for transfers between devices: 126 us -> none  [the longest x1 79.8 us: shards(): lax.all_gather(upper_factor, 'tile', axis=2, tiled=True)]
    ppermute x2 -> x20, waiting for transfers between devices: 142 us -> 48.6 us  [the longest x3 21.2 us: over_y(): return lax.ppermute(block, 'subtree', [(i, i ^ 2) for i in range(branches)])]
    reduce_scatter x1 -> x0, waiting for transfers between devices: 56 us -> none  [shards(): lax.psum_scatter(partial_value, 'tile', scatter_dimension=0, tiled=True)]
    add x2 -> x0, other arithmetic: 22.3 us -> none  [shards(): schur_part = schur_part + partner(schur_part, 'subtree', level_bit)]
    ppermute x2 -> x20, starting transfers between devices: 1.56 us -> 22.9 us  [the longest x7 14.1 us: over_z(): return lax.ppermute(block, 'tile', step)]
    dynamic_slice x1 -> x9, local copies, waits for them, and re-layouts: 3.17 us -> 24.2 us  [share(): lax.dynamic_slice_in_dim(stiffness, first_col(k, j), cols, 1) - product]
    convert_element_type x0 -> x2, other arithmetic: none -> 7.54 us  [shards_ring(): arrived = over_y((sent * SHARE_SCALE).astype(jnp.float16))]
    dot_general x6 -> x21, matrix products: 16.7 us -> 22.9 us  [the longest x9 11.9 us: times(): return jnp.dot(left, right, preferred_element_type=f32)]
  transfers between devices with their start and end apart: 5 -> 21, of which waited for: 5 -> 9; matrix products, arithmetic and copies ran while one was open for 2% -> 46% of each run, Pallas kernels for 0% -> 0%
where the time goes in v1:
time: 159 us; the launch traced here: 158 us
  waiting for transfers between devices  48.6 us (31%)
  local copies, waits for them, and re-layouts  42.7 us (27%)
  starting transfers between devices  27.8 us (17%)
  matrix products  22.9 us (14%)
  other arithmetic  14.4 us (9%)
    dynamic_slice x9, local copies, waits for them, and re-layouts, share(): lax.dynamic_slice_in_dim(stiffness, first_col(k, j), cols, 1) - product  24.2 us
    ppermute x3, waiting for transfers between devices, over_y(): return lax.ppermute(block, 'subtree', [(i, i ^ 2) for i in range(branches)])  21.2 us
    ppermute x7, waiting for transfers between devices, over_z(): return lax.ppermute(block, 'tile', step)  20.4 us
    ppermute x7, starting transfers between devices, over_z(): return lax.ppermute(block, 'tile', step)  14.1 us
    dot_general x9, matrix products, times(): return jnp.dot(left, right, preferred_element_type=f32)  11.9 us
    unnamed x58, local copies, waits for them, and re-layouts  8.14 us
    convert_element_type x2, other arithmetic, shards_ring(): arrived = over_y((sent * SHARE_SCALE).astype(jnp.float16))  7.54 us
    ppermute x5, waiting for transfers between devices, over_x(): return lax.ppermute(block, 'tile', [(i, i ^ 1) for i in range(tiles)])  7.05 us
  transfers between devices with their start and end apart: 21, of which 9 were waited for; matrix products, arithmetic and copies ran while one was open for 46% of the time, Pallas kernels for 0%

profile of v1, /device:TPU:0, one launch (start us, length us, event | category | flops | bytes accessed | tf_op | source)
XLA Modules:
  0.0 157.8 jit_solution(13699134536416580166)
XLA Ops:
  3.0 3.0 %collective-permute-start.14 = (bf16[128,256]{1,0:T(8,128)(2,1)S(1)}, bf16[128,256]{1,0:T(8,128)(2,1)S(1)}, u32[]{:S(2)}, u32[]{:S(2)}) collective-permute-start(bf16[128,256]{1,0:T(8,128)(2,1)S(1)} %get-tuple-element.19), channel_id=1, source_target_pairs={{0,2},{1,3},{2,6},{3,7},{6,4},{7,5},{4,0},{5,1},{8,10},{9,11},{10,... | collective-permute-start | bytes 196616 | tf_op jit(solution)/shard_map/ppermute | solution.py:147
  6.0 2.6 %collective-permute-start = (bf16[512,512]{1,0:T(8,128)(2,1)}, bf16[512,512]{1,0:T(8,128)(2,1)}, u32[]{:S(2)}, u32[]{:S(2)}) collective-permute-start(bf16[512,512]{1,0:T(8,128)(2,1)} %bitcast.153), channel_id=1, source_target_pairs={{0,2},{1,3},{2,6},{3,7},{6,4},{7,5},{4,0},{5,1},{8,10},{9,11},{10,... | collective-permute-start | bytes 1572872 | tf_op jit(solution)/shard_map/ppermute | solution.py:147
  11.1 6.3 %constant_dynamic-slice_fusion.2 = (f32[1,512,512]{2,1,0:T(8,128)}, f32[1,512,512]{2,1,0:T(8,128)}, f32[1,512,512]{2,1,0:T(8,128)}, f32[1,512,512]{2,1,0:T(8,128...) fusion(f32[1,512,4096]{2,1,0:T(8,128)} %param.8, ...), kind=kLoop, calls=%fused_computation.98 | loop fusion | bytes 16777248 | tf_op jit(solution)/shard_map/dynamic_slice | solution.py:194
  18.7 3.2 %collective-permute-done.15 = bf16[128,256]{1,0:T(8,128)(2,1)S(1)} collective-permute-done((bf16[128,256]{1,0:T(8,128)(2,1)S(1)}, bf16[128,256]{1,0:T(8,128)(2,1)S(1)}, u32[]{:S(2)}, u32[]{:S(2)}) %collective-permute-start.15) | collective-permute-done | bytes 65568 | tf_op jit(solution)/shard_map/ppermute | solution.py:147
  23.6 1.7 %convolution_subtract_fusion = f32[512,512]{0,1:T(8,128)S(1)} fusion(f32[1,512,512]{1,2,0:T(8,128)} %copy.22, bf16[1,512,512]{2,1,0:T(8,128)(2,1)S(1)} %copy-done.23, bf16[1,512,512]{2,1,0:T(8,128)(2,1)S(1)} %copy-done), kind=kOutput, calls=%fused_computation.15 | convolution fusion | flops 268697600 | bytes 3145728 | tf_op jit(solution)/shard_map/dot_general | solution.py:197
  25.3 1.8 %collective-permute-done.16 = bf16[128,256]{1,0:T(8,128)(2,1)S(1)} collective-permute-done((bf16[128,256]{1,0:T(8,128)(2,1)S(1)}, bf16[128,256]{1,0:T(8,128)(2,1)S(1)}, u32[]{:S(2)}, u32[]{:S(2)}) %collective-permute-start.16) | collective-permute-done | bytes 65568 | tf_op jit(solution)/shard_map/ppermute | solution.py:147
  27.1 1.9 %collective-permute-start.17 = (bf16[4,128,256]{2,1,0:T(8,128)(2,1)S(1)}, bf16[4,128,256]{2,1,0:T(8,128)(2,1)S(1)}, u32[]{:S(2)}, u32[]{:S(2)}) collective-permute-start(bf16[4,128,256]{2,1,0:T(8,128)(2,1)S(1)} %pad_maximum_fusion.3), channel_id=1, source_target_pairs={{0,1},{1,0},{2,3},{3,2},{4,5},{5,4},{6,7},{7,6},{8,9},{9,8},{10,11... | collective-permute-start | bytes 786440 | tf_op jit(solution)/shard_map/ppermute | solution.py:150
  29.1 2.5 %copy.23 = f32[1,512,512]{1,2,0:T(8,128)} copy(f32[1,512,512]{2,1,0:T(8,128)} %get-tuple-element.31) | data formatting | bytes 2097152 | tf_op jit(solution)/shard_map/dynamic_slice | solution.py:194
  31.7 2.5 %copy.24 = f32[1,512,512]{1,2,0:T(8,128)} copy(f32[1,512,512]{2,1,0:T(8,128)} %get-tuple-element.30) | data formatting | bytes 2097152 | tf_op jit(solution)/shard_map/dynamic_slice | solution.py:194
  34.2 2.5 %copy.25 = f32[1,512,512]{1,2,0:T(8,128)} copy(f32[1,512,512]{2,1,0:T(8,128)} %get-tuple-element.29) | data formatting | bytes 2097152 | tf_op jit(solution)/shard_map/dynamic_slice | solution.py:194
  36.7 2.6 %copy.26 = f32[1,512,512]{1,2,0:T(8,128)} copy(f32[1,512,512]{2,1,0:T(8,128)} %get-tuple-element.28) | data formatting | bytes 2097152 | tf_op jit(solution)/shard_map/dynamic_slice | solution.py:194
  39.3 2.5 %copy.27 = f32[1,512,512]{1,2,0:T(8,128)} copy(f32[1,512,512]{2,1,0:T(8,128)} %get-tuple-element.27) | data formatting | bytes 2097152 | tf_op jit(solution)/shard_map/dynamic_slice | solution.py:194
  41.9 2.5 %copy.28 = f32[1,512,512]{1,2,0:T(8,128)} copy(f32[1,512,512]{2,1,0:T(8,128)} %get-tuple-element.26) | data formatting | bytes 2097152 | tf_op jit(solution)/shard_map/dynamic_slice | solution.py:194
  45.7 2.6 %copy.34 = f32[512,512]{0,1:T(8,128)} copy(f32[512,512]{1,0:T(8,128)} %param.13) | data formatting | bytes 2097152 | tf_op args[5]
  56.8 1.9 %fusion.2 = f32[512,512]{0,1:T(8,128)S(1)} fusion(bf16[512,512]{1,0:T(8,128)(2,1)} %collective-permute-done.1, f32[1,512,512]{1,2,0:T(8,128)S(1)} %copy-done.15, bf16[1,512,512]{2,1,0:T(8,128)(2,1)S(1)} %copy-done), kind=kOutput, calls=%fused_computation.8 | convolution fusion | flops 268697600 | bytes 3145728 | tf_op jit(solution)/shard_map/dot_general | solution.py:197
  58.7 5.6 %collective-permute-done.18 = bf16[8,128,256]{2,1,0:T(8,128)(2,1)S(1)} collective-permute-done((bf16[8,128,256]{2,1,0:T(8,128)(2,1)}, bf16[8,128,256]{2,1,0:T(8,128)(2,1)S(1)}, u32[]{:S(2)}, u32[]{:S(2)}) %collective-permute-start.18) | collective-permute-done | bytes 524320 | tf_op jit(solution)/shard_map/ppermute | solution.py:153
  66.5 2.6 %collective-permute-start.5 = (bf16[512,512]{1,0:T(8,128)(2,1)S(1)}, bf16[512,512]{1,0:T(8,128)(2,1)S(1)}, u32[]{:S(2)}, u32[]{:S(2)}) collective-permute-start(bf16[512,512]{1,0:T(8,128)(2,1)S(1)} %collective-permute-done.2), channel_id=1, source_target_pairs={{0,2},{1,3},{2,6},{3,7},{6,4},{7,5},{4,0},{5,1},{8,10},{9,11},{10,... | collective-permute-start | bytes 1572872 | tf_op jit(solution)/shard_map/ppermute | solution.py:147
  71.6 9.3 %collective-permute-done.5 = bf16[512,512]{1,0:T(8,128)(2,1)S(1)} collective-permute-done((bf16[512,512]{1,0:T(8,128)(2,1)S(1)}, bf16[512,512]{1,0:T(8,128)(2,1)S(1)}, u32[]{:S(2)}, u32[]{:S(2)}) %collective-permute-start.5) | collective-permute-done | bytes 524320 | tf_op jit(solution)/shard_map/ppermute | solution.py:147
  82.6 2.8 %collective-permute-start.11 = (bf16[256,512]{1,0:T(8,128)(2,1)S(1)}, bf16[256,512]{1,0:T(8,128)(2,1)S(1)}, u32[]{:S(2)}, u32[]{:S(2)}) collective-permute-start(bf16[256,512]{1,0:T(8,128)(2,1)S(1)} %slice.26), channel_id=1, source_target_pairs={{0,2},{1,3},{2,6},{3,7},{6,4},{7,5},{4,0},{5,1},{8,10},{9,11},{10,... | collective-permute-start | bytes 786440 | tf_op jit(solution)/shard_map/ppermute | solution.py:147
  87.1 5.3 %collective-permute-done.11 = bf16[256,512]{1,0:T(8,128)(2,1)S(1)} collective-permute-done((bf16[256,512]{1,0:T(8,128)(2,1)S(1)}, bf16[256,512]{1,0:T(8,128)(2,1)S(1)}, u32[]{:S(2)}, u32[]{:S(2)}) %collective-permute-start.11) | collective-permute-done | bytes 262176 | tf_op jit(solution)/shard_map/ppermute | solution.py:147
  93.3 7.0 %collective-permute-done.10 = bf16[256,512]{1,0:T(8,128)(2,1)S(1)} collective-permute-done((bf16[256,512]{1,0:T(8,128)(2,1)S(1)}, bf16[256,512]{1,0:T(8,128)(2,1)S(1)}, u32[]{:S(2)}, u32[]{:S(2)}) %collective-permute-start.10) | collective-permute-done | bytes 262176 | tf_op jit(solution)/shard_map/ppermute | solution.py:150
  110.1 1.9 %gather_fusion = bf16[512,256]{1,0:T(8,128)(2,1)S(1)} fusion(bf16[4096,256]{1,0:T(8,128)(2,1)S(1)} %bitcast.150, s32[1024]{0:T(1024)S(1)} %pad_clamp_fusion), kind=kCustom, calls=%fused_computation | custom fusion | bytes 526336 | tf_op jit(solution)/shard_map/jit(_take)/gather | solution.py:248
  114.9 2.2 %reshape.43 = f32[32,1,2048]{2,1,0:T(1,128)} reshape(f32[32,32,64]{2,1,0:T(8,128)} %bitcast.152) | data formatting | bytes 524288
  117.0 4.9 %all-to-all-start = ((f32[32,1,2048]{2,1,0:T(1,128)}), f32[32,1,2048]{2,1,0:T(1,128)}, u32[]{:S(2)}, u32[]{:S(2)}) async-start(f32[32,1,2048]{2,1,0:T(1,128)} %reshape.43), calls=%async_computation | async-start | bytes 524288 | tf_op jit(solution)/shard_map/all_to_all | solution.py:226
  121.9 1.9 %fusion.9 = f32[512,64]{1,0:T(8,128)S(1)} fusion(f32[512,512]{1,0:T(8,128)S(1)} %copy-done.16, f32[512,512]{0,1:T(8,128)} %copy.34, bf16[512,256]{1,0:T(8,128)(2,1)S(1)} %gather_fusion, s32[]{:T(128)S(6)} %select_n.259), kind=kOutput, calls=%fused_computation.30 | convolution fusion | flops 201850880 | bytes 2359300 | tf_op jit(solution)/shard_map/dot_general | solution.py:31
  123.9 4.0 %multiply_convert_fusion.1 = (f16[512,512]{0,1:T(8,128)(2,1)}, f32[512,512]{0,1:T(8,128)}, f32[512,512]{0,1:T(8,128)}) fusion(pred[]{:T(512)S(6)} %eq.32, f32[512,512]{0,1:T(8,128)} %collective-permute-done.4, f32[512,512]{0,1:T(8,128)} %copy-done.5, f32[512,512]{0,1:T(8,128)} %copy-done.7, pred[]{:T(512)S(6)} %eq.31, f32[512,512]{0,1:T(8,128)} %collective-permute-done.7, ...), kind=kLoop, calls=%fused_computation.38 | loop fusion | flops 1835008 | bytes 8912899 | tf_op jit(solution)/shard_map/convert_element_type | solution.py:240
  129.4 3.6 %multiply_convert_fusion = (f16[512,512]{0,1:T(8,128)(2,1)}, f32[512,512]{0,1:T(8,128)}, f32[512,512]{0,1:T(8,128)}) fusion(pred[]{:T(512)S(6)} %eq.32, f32[512,512]{0,1:T(8,128)} %collective-permute-done.9, f32[512,512]{0,1:T(8,128)S(1)} %fusion.2, f32[512,512]{0,1:T(8,128)S(1)} %copy-done.9, pred[]{:T(512)S(6)} %eq.31, ...), kind=kLoop, calls=%fused_computation.34 | loop fusion | flops 1835008 | bytes 8912899 | tf_op jit(solution)/shard_map/convert_element_type | solution.py:240
  134.9 2.2 %reduce = f32[32,2048]{1,0:T(8,128)S(1)} reduce(f32[32,1,2048]{2,1,0:T(1,128)} %all-to-all-done, f32[]{:T(128)} %broadcast.52), dimensions={1}, to_apply=%all_to_all.3.reduce_sub_computation | reduce | bytes 524292 | tf_op jit(solution)/shard_map/all_to_all | solution.py:226
  138.1 5.0 %collective-permute-done.8 = f16[512,512]{0,1:T(8,128)(2,1)} collective-permute-done((f16[512,512]{0,1:T(8,128)(2,1)}, f16[512,512]{0,1:T(8,128)(2,1)}, u32[]{:S(2)}, u32[]{:S(2)}) %collective-permute-start.8) | collective-permute-done | bytes 524320 | tf_op jit(solution)/shard_map/ppermute | solution.py:153
  143.1 10.6 %collective-permute-done.13 = f16[512,512]{0,1:T(8,128)(2,1)} collective-permute-done((f16[512,512]{0,1:T(8,128)(2,1)}, f16[512,512]{0,1:T(8,128)(2,1)}, u32[]{:S(2)}, u32[]{:S(2)}) %collective-permute-start.13) | collective-permute-done | bytes 524320 | tf_op jit(solution)/shard_map/ppermute | solution.py:153
  153.7 2.1 %broadcast_select_fusion.5 = (f32[512,512]{0,1:T(8,128)S(1)}, f32[512,512]{0,1:T(8,128)S(1)}) fusion(pred[]{:T(512)S(6)} %eq.30, f16[512,512]{0,1:T(8,128)(2,1)} %collective-permute-done.8, f32[512,512]{0,1:T(8,128)S(1)} %copy-done.17, f32[512,512]{0,1:T(8,128)S(1)} %copy-done.18, pred[]{:T(512)S(6)} %eq.32, f16[512,512]{0,1:T(8,128)(2,1)} %collective-permute-done.13, ...), kind=kLoop, calls=%fused_computation.49 | loop fusion | flops 2621440 | bytes 7340034 | tf_op jit(solution)/shard_map/jit(_where)/select_n | solution.py:245
  156.0 1.8 %copy.35 = f32[512,1024]{1,0:T(8,128)} copy(f32[512,1024]{0,1:T(8,128)S(1)} %pad_maximum_fusion) | data formatting | bytes 4194304
  (128 shorter events, 43.5 us)
Async XLA Ops:
  3.0 7.1 %collective-permute-start.14 = (bf16[128,256]{1,0:T(8,128)(2,1)S(1)}, bf16[128,256]{1,0:T(8,128)(2,1)S(1)}, u32[]{:S(2)}, u32[]{:S(2)}) collective-permute-start(bf16[128,256]{1,0:T(8,128)(2,1)S(1)} %get-tuple-element.19), channel_id=1, source_target_pairs={{0,2},{1,3},{2,6},{3,7},{6,4},{7,5},{4,0},{5,1},{8,10},{9,11},{10,... | collective-permute-start | bytes 196616 | tf_op jit(solution)/shard_map/ppermute | solution.py:147
  6.0 48.2 %collective-permute-start = (bf16[512,512]{1,0:T(8,128)(2,1)}, bf16[512,512]{1,0:T(8,128)(2,1)}, u32[]{:S(2)}, u32[]{:S(2)}) collective-permute-start(bf16[512,512]{1,0:T(8,128)(2,1)} %bitcast.153), channel_id=1, source_target_pairs={{0,2},{1,3},{2,6},{3,7},{6,4},{7,5},{4,0},{5,1},{8,10},{9,11},{10,... | collective-permute-start | bytes 1572872 | tf_op jit(solution)/shard_map/ppermute | solution.py:147
  8.6 45.6 %collective-permute-start.1 = (bf16[512,512]{1,0:T(8,128)(2,1)}, bf16[512,512]{1,0:T(8,128)(2,1)}, u32[]{:S(2)}, u32[]{:S(2)}) collective-permute-start(bf16[512,512]{1,0:T(8,128)(2,1)} %bitcast.154), channel_id=1, source_target_pairs={{0,1},{1,0},{2,3},{3,2},{4,5},{5,4},{6,7},{7,6},{8,9},{9,8},{10,11... | collective-permute-start | bytes 1572872 | tf_op jit(solution)/shard_map/ppermute | solution.py:150
  10.1 11.8 %collective-permute-start.15 = (bf16[128,256]{1,0:T(8,128)(2,1)S(1)}, bf16[128,256]{1,0:T(8,128)(2,1)S(1)}, u32[]{:S(2)}, u32[]{:S(2)}) collective-permute-start(bf16[128,256]{1,0:T(8,128)(2,1)S(1)} %collective-permute-done.14), channel_id=1, source_target_pairs={{0,2},{1,3},{2,6},{3,7},{6,4},{7,5},{4,0},{5,1},{8,10},{9,11},{10,... | collective-permute-start | bytes 196616 | tf_op jit(solution)/shard_map/ppermute | solution.py:147
  21.9 5.2 %collective-permute-start.16 = (bf16[128,256]{1,0:T(8,128)(2,1)S(1)}, bf16[128,256]{1,0:T(8,128)(2,1)S(1)}, u32[]{:S(2)}, u32[]{:S(2)}) collective-permute-start(bf16[128,256]{1,0:T(8,128)(2,1)S(1)} %collective-permute-done.15), channel_id=1, source_target_pairs={{0,2},{1,3},{2,6},{3,7},{6,4},{7,5},{4,0},{5,1},{8,10},{9,11},{10,... | collective-permute-start | bytes 196616 | tf_op jit(solution)/shard_map/ppermute | solution.py:147
  25.3 44.3 %copy-start.5 = (f32[512,512]{0,1:T(8,128)}, f32[512,512]{0,1:T(8,128)S(1)}, u32[]{:S(2)}) copy-start(f32[512,512]{0,1:T(8,128)S(1)} %convolution_subtract_fusion) | copy-start | bytes 3145732
  27.1 21.2 %collective-permute-start.17 = (bf16[4,128,256]{2,1,0:T(8,128)(2,1)S(1)}, bf16[4,128,256]{2,1,0:T(8,128)(2,1)S(1)}, u32[]{:S(2)}, u32[]{:S(2)}) collective-permute-start(bf16[4,128,256]{2,1,0:T(8,128)(2,1)S(1)} %pad_maximum_fusion.3), channel_id=1, source_target_pairs={{0,1},{1,0},{2,3},{3,2},{4,5},{5,4},{6,7},{7,6},{8,9},{9,8},{10,11... | collective-permute-start | bytes 786440 | tf_op jit(solution)/shard_map/ppermute | solution.py:150
  52.7 11.7 %collective-permute-start.18 = (bf16[8,128,256]{2,1,0:T(8,128)(2,1)}, bf16[8,128,256]{2,1,0:T(8,128)(2,1)S(1)}, u32[]{:S(2)}, u32[]{:S(2)}) collective-permute-start(bf16[8,128,256]{2,1,0:T(8,128)(2,1)} %bitcast.29), channel_id=1, source_target_pairs={{0,16},{8,24},{16,0},{24,8},{1,17},{9,25},{17,1},{25,9},{2,18},{10... | collective-permute-start | bytes 1572872 | tf_op jit(solution)/shard_map/ppermute | solution.py:153
  54.2 12.3 %collective-permute-start.2 = (bf16[512,512]{1,0:T(8,128)(2,1)}, bf16[512,512]{1,0:T(8,128)(2,1)S(1)}, u32[]{:S(2)}, u32[]{:S(2)}) collective-permute-start(bf16[512,512]{1,0:T(8,128)(2,1)} %collective-permute-done), channel_id=1, source_target_pairs={{0,2},{1,3},{2,6},{3,7},{6,4},{7,5},{4,0},{5,1},{8,10},{9,11},{10,... | collective-permute-start | bytes 1572872 | tf_op jit(solution)/shard_map/ppermute | solution.py:147
  54.7 11.8 %collective-permute-start.3 = (bf16[512,512]{1,0:T(8,128)(2,1)}, bf16[512,512]{1,0:T(8,128)(2,1)S(1)}, u32[]{:S(2)}, u32[]{:S(2)}) collective-permute-start(bf16[512,512]{1,0:T(8,128)(2,1)} %collective-permute-done), channel_id=1, source_target_pairs={{0,1},{1,0},{2,3},{3,2},{4,5},{5,4},{6,7},{7,6},{8,9},{9,8},{10,11... | collective-permute-start | bytes 1572872 | tf_op jit(solution)/shard_map/ppermute | solution.py:150
  56.8 47.3 %copy-start.1 = (f32[512,512]{0,1:T(8,128)}, f32[512,512]{0,1:T(8,128)S(1)}, u32[]{:S(2)}) copy-start(f32[512,512]{0,1:T(8,128)S(1)} %fusion.4) | copy-start | bytes 3145732
  58.7 10.9 %copy-start.22 = (f32[1,512,512]{1,2,0:T(8,128)S(1)}, f32[1,512,512]{1,2,0:T(8,128)}, u32[]{:S(2)}) copy-start(f32[1,512,512]{1,2,0:T(8,128)} %copy.23) | copy-start | bytes 3145732
  65.6 36.1 %collective-permute-start.19 = (bf16[8,2,128,256]{3,2,1,0:T(8,128)(2,1)S(1)}, bf16[8,2,128,256]{3,2,1,0:T(8,128)(2,1)S(1)}, u32[]{:S(2)}, u32[]{:S(2)}) collective-permute-start(bf16[8,2,128,256]{3,2,1,0:T(8,128)(2,1)S(1)} %pad_maximum_fusion.2), channel_id=1, source_target_pairs={{0,8},{8,0},{16,24},{24,16},{1,9},{9,1},{17,25},{25,17},{2,10},{10... | collective-permute-start | bytes 3145736 | tf_op jit(solution)/shard_map/ppermute | solution.py:156
  66.5 14.4 %collective-permute-start.5 = (bf16[512,512]{1,0:T(8,128)(2,1)S(1)}, bf16[512,512]{1,0:T(8,128)(2,1)S(1)}, u32[]{:S(2)}, u32[]{:S(2)}) collective-permute-start(bf16[512,512]{1,0:T(8,128)(2,1)S(1)} %collective-permute-done.2), channel_id=1, source_target_pairs={{0,2},{1,3},{2,6},{3,7},{6,4},{7,5},{4,0},{5,1},{8,10},{9,11},{10,... | collective-permute-start | bytes 1572872 | tf_op jit(solution)/shard_map/ppermute | solution.py:147
  69.1 11.8 %collective-permute-start.6 = (bf16[512,512]{1,0:T(8,128)(2,1)S(1)}, bf16[512,512]{1,0:T(8,128)(2,1)S(1)}, u32[]{:S(2)}, u32[]{:S(2)}) collective-permute-start(bf16[512,512]{1,0:T(8,128)(2,1)S(1)} %collective-permute-done.2), channel_id=1, source_target_pairs={{0,1},{1,0},{2,3},{3,2},{4,5},{5,4},{6,7},{7,6},{8,9},{9,8},{10,11... | collective-permute-start | bytes 1572872 | tf_op jit(solution)/shard_map/ppermute | solution.py:150
  71.1 33.7 %copy-start.7 = (f32[512,512]{0,1:T(8,128)}, f32[512,512]{0,1:T(8,128)S(1)}, u32[]{:S(2)}) copy-start(f32[512,512]{0,1:T(8,128)S(1)} %get-tuple-element.43) | copy-start | bytes 3145732
  71.1 52.8 %collective-permute-start.4 = (f32[512,512]{0,1:T(8,128)}, f32[512,512]{0,1:T(8,128)}, u32[]{:S(2)}, u32[]{:S(2)}) collective-permute-start(f32[512,512]{0,1:T(8,128)} %get-tuple-element.42), channel_id=1, source_target_pairs={{0,8},{8,0},{16,24},{24,16},{1,9},{9,1},{17,25},{25,17},{2,10},{10... | collective-permute-start | bytes 3145736 | tf_op jit(solution)/shard_map/ppermute | solution.py:156
  71.6 35.5 %copy-start.3 = (f32[512,512]{0,1:T(8,128)}, f32[512,512]{0,1:T(8,128)S(1)}, u32[]{:S(2)}) copy-start(f32[512,512]{0,1:T(8,128)S(1)} %fusion) | copy-start | bytes 3145732
  71.6 13.7 %copy-start.20 = (f32[1,512,512]{1,2,0:T(8,128)S(1)}, f32[1,512,512]{1,2,0:T(8,128)}, u32[]{:S(2)}) copy-start(f32[1,512,512]{1,2,0:T(8,128)} %copy.27) | copy-start | bytes 3145732
  82.4 23.1 %copy-start.10 = (f32[512,512]{0,1:T(8,128)}, f32[512,512]{0,1:T(8,128)S(1)}, u32[]{:S(2)}) copy-start(f32[512,512]{0,1:T(8,128)S(1)} %get-tuple-element.45) | copy-start | bytes 3145732
  82.5 41.5 %collective-permute-start.7 = (f32[512,512]{0,1:T(8,128)}, f32[512,512]{0,1:T(8,128)}, u32[]{:S(2)}, u32[]{:S(2)}) collective-permute-start(f32[512,512]{0,1:T(8,128)} %get-tuple-element.44), channel_id=1, source_target_pairs={{0,8},{8,0},{16,24},{24,16},{1,9},{9,1},{17,25},{25,17},{2,10},{10... | collective-permute-start | bytes 3145736 | tf_op jit(solution)/shard_map/ppermute | solution.py:156
  82.6 9.8 %collective-permute-start.11 = (bf16[256,512]{1,0:T(8,128)(2,1)S(1)}, bf16[256,512]{1,0:T(8,128)(2,1)S(1)}, u32[]{:S(2)}, u32[]{:S(2)}) collective-permute-start(bf16[256,512]{1,0:T(8,128)(2,1)S(1)} %slice.26), channel_id=1, source_target_pairs={{0,2},{1,3},{2,6},{3,7},{6,4},{7,5},{4,0},{5,1},{8,10},{9,11},{10,... | collective-permute-start | bytes 786440 | tf_op jit(solution)/shard_map/ppermute | solution.py:147
  86.9 20.9 %copy-start.8 = (f32[512,512]{0,1:T(8,128)}, f32[512,512]{0,1:T(8,128)S(1)}, u32[]{:S(2)}) copy-start(f32[512,512]{0,1:T(8,128)S(1)} %get-tuple-element.47) | copy-start | bytes 3145732
  86.9 13.4 %copy-start.19 = (f32[1,512,512]{1,2,0:T(8,128)S(1)}, f32[1,512,512]{1,2,0:T(8,128)}, u32[]{:S(2)}) copy-start(f32[1,512,512]{1,2,0:T(8,128)} %copy.29) | copy-start | bytes 3145732
  86.9 42.5 %collective-permute-start.9 = (f32[512,512]{0,1:T(8,128)}, f32[512,512]{0,1:T(8,128)}, u32[]{:S(2)}, u32[]{:S(2)}) collective-permute-start(f32[512,512]{0,1:T(8,128)} %get-tuple-element.46), channel_id=1, source_target_pairs={{0,8},{8,0},{16,24},{24,16},{1,9},{9,1},{17,25},{25,17},{2,10},{10... | collective-permute-start | bytes 3145736 | tf_op jit(solution)/shard_map/ppermute | solution.py:156
  92.4 7.9 %collective-permute-start.10 = (bf16[256,512]{1,0:T(8,128)(2,1)S(1)}, bf16[256,512]{1,0:T(8,128)(2,1)S(1)}, u32[]{:S(2)}, u32[]{:S(2)}) collective-permute-start(bf16[256,512]{1,0:T(8,128)(2,1)S(1)} %slice.24), channel_id=1, source_target_pairs={{0,1},{1,0},{2,3},{3,2},{4,5},{5,4},{6,7},{7,6},{8,9},{9,8},{10,11... | collective-permute-start | bytes 786440 | tf_op jit(solution)/shard_map/ppermute | solution.py:150
  101.7 27.7 %collective-permute-start.12 = (f32[512,512]{0,1:T(8,128)}, f32[512,512]{0,1:T(8,128)}, u32[]{:S(2)}, u32[]{:S(2)}) collective-permute-start(f32[512,512]{0,1:T(8,128)} %get-tuple-element.48), channel_id=1, source_target_pairs={{0,8},{8,0},{16,24},{24,16},{1,9},{9,1},{17,25},{25,17},{2,10},{10... | collective-permute-start | bytes 3145736 | tf_op jit(solution)/shard_map/ppermute | solution.py:156
  117.0 17.3 %all-to-all-start = ((f32[32,1,2048]{2,1,0:T(1,128)}), f32[32,1,2048]{2,1,0:T(1,128)}, u32[]{:S(2)}, u32[]{:S(2)}) async-start(f32[32,1,2048]{2,1,0:T(1,128)} %reshape.43), calls=%async_computation | async-start | bytes 524288 | tf_op jit(solution)/shard_map/all_to_all | solution.py:226
  127.9 15.2 %collective-permute-start.8 = (f16[512,512]{0,1:T(8,128)(2,1)}, f16[512,512]{0,1:T(8,128)(2,1)}, u32[]{:S(2)}, u32[]{:S(2)}) collective-permute-start(f16[512,512]{0,1:T(8,128)(2,1)} %get-tuple-element.23), channel_id=1, source_target_pairs={{0,16},{8,24},{16,0},{24,8},{1,17},{9,25},{17,1},{25,9},{2,18},{10... | collective-permute-start | bytes 1572872 | tf_op jit(solution)/shard_map/ppermute | solution.py:153
  133.0 20.7 %copy-start.17 = (f32[512,512]{0,1:T(8,128)S(1)}, f32[512,512]{0,1:T(8,128)}, u32[]{:S(2)}) copy-start(f32[512,512]{0,1:T(8,128)} %get-tuple-element.24) | copy-start | bytes 3145732
  133.0 20.7 %copy-start.18 = (f32[512,512]{0,1:T(8,128)S(1)}, f32[512,512]{0,1:T(8,128)}, u32[]{:S(2)}) copy-start(f32[512,512]{0,1:T(8,128)} %get-tuple-element.25) | copy-start | bytes 3145732
  133.0 20.7 %collective-permute-start.13 = (f16[512,512]{0,1:T(8,128)(2,1)}, f16[512,512]{0,1:T(8,128)(2,1)}, u32[]{:S(2)}, u32[]{:S(2)}) collective-permute-start(f16[512,512]{0,1:T(8,128)(2,1)} %get-tuple-element.20), channel_id=1, source_target_pairs={{0,16},{8,24},{16,0},{24,8},{1,17},{9,25},{17,1},{25,9},{2,18},{10... | collective-permute-start | bytes 1572872 | tf_op jit(solution)/shard_map/ppermute | solution.py:153
  (16 other events, 107.9 us)

commit v2 on v1

--- a/solution.py
+++ b/solution.py
@@ -1,6 +1,8 @@
 import jax
 import jax.numpy as jnp
 from jax import lax
+from jax.experimental import pallas as pl
+from jax.experimental.pallas import tpu as pltpu
 from jax.sharding import PartitionSpec as P
 
 SPEED_STEPS = 64
@@ -115,6 +117,230 @@
     return (schur_out, combine(stiff_block, gyro_block, spin_block, speed_index))
 
 
+def gray(i):
+    return i ^ (i >> 1)
+
+
+def ring_z(place, k):
+    return gray((gray(place[0] >> 1) + (4 - k)) & 3)
+
+
+def block_at(place, j, k):
+    return ring_z(place, k) * 2 + ((place[0] & 1) ^ j)
+
+
+def keeps(place, k):
+    return (ring_z(place, k) & 1) == (place[1] & 1)
+
+
+def stays(place):
+    kept_z = jnp.where(keeps(place, 0), ring_z(place, 0), ring_z(place, 2))
+    return (kept_z >> 1) == (place[1] >> 1)
+
+
+def whole(shape):
+    return pl.BlockSpec(shape, lambda *_: (0,) * len(shape))
+
+
+def call(body, grid, in_specs, out_specs, out_shape, flops, moved, scratch=()):
+    return pl.pallas_call(
+        body,
+        out_shape=out_shape,
+        grid_spec=pltpu.PrefetchScalarGridSpec(
+            num_scalar_prefetch=1,
+            grid=grid,
+            in_specs=in_specs,
+            out_specs=out_specs,
+            scratch_shapes=scratch,
+        ),
+        compiler_params=pltpu.CompilerParams(vmem_limit_bytes=40 << 20),
+        cost_estimate=pl.CostEstimate(flops=flops, bytes_accessed=moved, transcendentals=0),
+    )
+
+
+def mul(left, right):
+    return jnp.dot(left, right, preferred_element_type=jnp.float32)
+
+
+def mul_wide(left, right):
+    high = left.astype(jnp.bfloat16)
+    low = (left - high.astype(jnp.float32)).astype(jnp.bfloat16)
+    return mul(high, right) + mul(low, right)
+
+
+def shares(place, stiffness, lower, blocks, first):
+    rows = stiffness.shape[0]
+    depth, cols = blocks[0][2].shape
+    step = rows // 2
+    steps = rows // step
+    count = len(blocks)
+    pairs = [f for f in first if f is not None]
+
+    def stiff_spec(j, k):
+        return pl.BlockSpec((step, cols), lambda i, at: (i, block_at(at, j, k)))
+
+    tile_spec = pl.BlockSpec((step, cols), lambda i, at: (i, 0))
+    in_specs = [stiff_spec(j, k) for j, k, _ in blocks]
+    in_specs += [pl.BlockSpec((step, depth), lambda i, at: (i, 0))]
+    in_specs += [whole((depth, cols))] * count + [tile_spec] * len(pairs)
+    outs = count + len(pairs)
+
+    def body(at, *refs):
+        stiff = refs[:count]
+        low = refs[count][...]
+        uppers = refs[count + 1 : 2 * count + 1]
+        olds = list(refs[2 * count + 1 : 2 * count + 1 + len(pairs)])
+        outputs = list(refs[2 * count + 1 + len(pairs) :])
+        for n, (j, k, _) in enumerate(blocks):
+            value = stiff[n][...] - mul(low, uppers[n][...])
+            if first[n] is None:
+                outputs.pop(0)[...] = value
+                continue
+            old = olds.pop(0)
+            sent, kept = outputs.pop(0), outputs.pop(0)
+            keep_old = keeps(at, k - 2)
+
+            @pl.when(keep_old)
+            def _():
+                sent[...] = value
+                kept[...] = old[...]
+
+            @pl.when(jnp.logical_not(keep_old))
+            def _():
+                sent[...] = old[...]
+                kept[...] = value
+
+    return call(
+        body,
+        (steps,),
+        in_specs,
+        [tile_spec] * outs,
+        [jax.ShapeDtypeStruct((rows, cols), jnp.float32)] * outs,
+        2 * count * rows * cols * depth,
+        4 * rows * cols * (count + outs),
+    )(place, *[stiffness] * count, lower, *[b[2] for b in blocks], *pairs)
+
+
+def fill_modes(at, target, near, beside, j, k):
+    chunk = near.shape[2]
+    for dist in range(4):
+        source = beside if dist % 2 else near
+        first = pl.multiple_of((at[1] ^ dist) * chunk, chunk)
+        target[pl.ds(first, chunk), :] = source[dist // 2, j * 4 + k]
+
+
+def respond(place, near, beside, plain, pairs):
+    rows, cols = plain[0][2].shape
+    modes_count = near.shape[3]
+    flat = [p[2] for p in plain] + [s for p in pairs for s in p[2:]]
+    step = rows // 2
+    tile_spec = pl.BlockSpec((step, cols), lambda i, at: (i, 0))
+
+    def body(at, near_ref, beside_ref, *refs):
+        share_refs, out, scratch = list(refs[: len(flat)]), refs[len(flat)], refs[len(flat) + 1]
+        total = jnp.zeros((step, modes_count), jnp.float32)
+        order = [(j, k) for j, k, _ in plain]
+        for j, k, _, _ in pairs:
+            keep_old = keeps(at, k)
+            order.append((j, jnp.where(keep_old, k + 2, k)))
+            order.append((j, jnp.where(keep_old, k, k + 2)))
+        for n, (j, k) in enumerate(order):
+            fill_modes(at, scratch.at[n], near_ref, beside_ref, j, k)
+            total += mul_wide(share_refs[n][...], scratch[n])
+        out[...] = total
+
+    return call(
+        body,
+        (rows // step,),
+        [whole(near.shape), whole(beside.shape)] + [tile_spec] * len(flat),
+        pl.BlockSpec((step, modes_count), lambda i, at: (i, 0)),
+        jax.ShapeDtypeStruct((rows, modes_count), jnp.float32),
+        4 * len(flat) * rows * cols * modes_count,
+        4 * len(flat) * rows * cols,
+        [pltpu.VMEM((len(flat), cols, modes_count), jnp.bfloat16)],
+    )(place, near, beside, *flat)
+
+
+def last_share(place, stiffness, lower, low_half, high_half, old, near, beside, response, modes):
+    rows = stiffness.shape[0]
+    cut, cols = low_half.shape
+    depth = lower.shape[1]
+    mode_count = modes.shape[1]
+    branches, tiles = 4, 8
+    group = mode_count // tiles // 2
+
+    def body(at, stiff, low, lo, hi, old_ref, near_ref, beside_ref, resp, mode, sent, kept, pieces, scratch):
+        fill_modes(at, scratch, near_ref, beside_ref, 1, 3)
+        value = stiff[...] - mul(low[:, :cut], lo[...]) - mul(low[:, cut:], hi[...])
+        keep_old = keeps(at, 1)
+
+        @pl.when(keep_old)
+        def _():
+            sent[...] = value
+            kept[...] = old_ref[...]
+
+        @pl.when(jnp.logical_not(keep_old))
+        def _():
+            sent[...] = old_ref[...]
+            kept[...] = value
+
+        total = resp[...] + mul_wide(value, scratch[...])
+        high = total.astype(jnp.bfloat16)
+        rest = (total - high.astype(jnp.float32)).astype(jnp.bfloat16)
+        across = (((0,), (0,)), ((), ()))
+        reduced = lax.dot_general(
+            mode[...], high, across, preferred_element_type=jnp.float32
+        ) + lax.dot_general(mode[...], rest, across, preferred_element_type=jnp.float32)
+        split = reduced.reshape(tiles, 2, group, mode_count)
+        upper = split[:, 0].reshape(tiles * group, mode_count)
+        under = split[:, 1].reshape(tiles * group, mode_count)
+        left = lax.broadcasted_iota(jnp.int32, (tiles * group, 128), 1) < 64
+        for pair in range(branches // 2):
+            u = upper[:, 128 * pair : 128 * pair + 128]
+            v = under[:, 128 * pair : 128 * pair + 128]
+            pieces[2 * pair] = jnp.where(left, u, pltpu.roll(v, 64, 1))
+            pieces[2 * pair + 1] = jnp.where(left, pltpu.roll(u, 64, 1), v)
+
+    share_shape = jax.ShapeDtypeStruct((rows, cols), jnp.float32)
+    return call(
+        body,
+        (1,),
+        [
+            pl.BlockSpec((rows, cols), lambda i, at: (0, block_at(at, 1, 3))),
+            whole(lower.shape),
+            whole(low_half.shape),
+            whole(high_half.shape),
+            whole((rows, cols)),
+            whole(near.shape),
+            whole(beside.shape),
+            whole(response.shape),
+            whole(modes.shape),
+        ],
+        [whole((rows, cols)), whole((rows, cols)), whole((branches, tiles * group, 128))],
+        [share_shape, share_shape, jax.ShapeDtypeStruct((branches, tiles * group, 128), jnp.float32)],
+        2 * rows * cols * (depth + 2 * mode_count),
+        16 * rows * cols,
+        [pltpu.VMEM((cols, mode_count), jnp.bfloat16)],
+    )(place, stiffness, lower, low_half, high_half, old, near, beside, response, modes)
+
+
+def join(place, kept, came):
+    here = stays(place)
+    both = [kept[n] + came[n] for n in range(2)]
+    sent = jnp.where(here, both[1], both[0])
+    return (sent * SHARE_SCALE).astype(jnp.float16), jnp.where(here, both[0], both[1])
+
+
+def finish(place, own, came):
+    first, second = (
+        mine + other.astype(jnp.float32) * (1.0 / SHARE_SCALE) for mine, other in zip(own, came)
+    )
+    cols = first.shape[1]
+    return lax.dynamic_update_slice_in_dim(
+        jnp.concatenate([first, first], axis=1), second, (1 - (place[0] & 1)) * cols, 1
+    )
+
+
 def shards_ring(
     interface_stiffness,
     lower_factor,
@@ -130,17 +356,11 @@
     branches = lax.axis_size("subtree")
     tile = lax.axis_index("tile")
     branch = lax.axis_index("subtree")
-    z, x = tile // 2, tile % 2
-    y, core = branch // 2, branch % 2
+    place = jnp.stack([tile, branch]).astype(jnp.int32)
     stiffness = interface_stiffness[0]
     lower = lower_factor[0]
     upper = upper_factor[0]
-    rows, width = stiffness.shape
-    depth, cols = upper.shape
     mode_count = modes.shape[1]
-
-    def gray(i):
-        return i ^ (i >> 1)
 
     def over_z(block):
         step = [(gray(p) * 2 + a, gray((p + 1) % 4) * 2 + a) for p in range(4) for a in range(2)]
@@ -155,97 +375,60 @@
     def over_core(block):
         return lax.ppermute(block, "subtree", [(i, i ^ 1) for i in range(branches)])
 
-    from_z = [gray((gray(z) - k) % 4) for k in range(4)]
-    from_x = [x, 1 - x]
-
     chunk = modes.shape[0] // branches
-    mine = lax.dynamic_slice_in_dim(modes, branch * chunk, chunk, 0)
-    mode_z = [mine]
+    mode_z = [lax.dynamic_slice_in_dim(modes, branch * chunk, chunk, 0)]
     for _ in range(3):
         mode_z.append(over_z(mode_z[-1]))
     mode_own = jnp.stack(mode_z)
-    mode_other = over_x(mode_own)
-    quarter = jnp.zeros((4, 2, chunk, mode_count), modes.dtype)
-    for k in range(4):
-        for j, source in enumerate((mode_own, mode_other)):
-            quarter = lax.dynamic_update_slice(
-                quarter, source[k][None, None], (from_z[k], from_x[j], 0, 0)
-            )
-    quarter = quarter.reshape(tiles, chunk, mode_count)
-    across = over_y(quarter)
-    half = jnp.stack(
-        [jnp.where(y == 0, quarter, across), jnp.where(y == 0, across, quarter)], axis=1
-    )
-    beside = over_core(half)
-    all_modes = jnp.stack(
-        [jnp.where(core == 0, half, beside), jnp.where(core == 0, beside, half)], axis=2
-    ).reshape(tiles * modes.shape[0], mode_count)
+    quarter = jnp.concatenate([mode_own, over_x(mode_own)])
+    near = jnp.stack([quarter, over_y(quarter)])
+    beside = over_core(near)
 
     z1, x0 = lax.optimization_barrier((over_z(upper), over_x(upper)))
     z2, x1 = lax.optimization_barrier((over_z(z1), over_x(z1)))
     z3, x2 = lax.optimization_barrier((over_z(z2), over_x(z2)))
-    cut = depth // 2
+    cut = upper.shape[0] // 2
     x3_low, x3_high = over_x(z3[:cut]), over_z(x2[cut:])
 
-    def first_col(k, j):
-        return (from_z[k] * 2 + from_x[j]) * cols
-
-    def share(k, j, product):
-        return lax.dynamic_slice_in_dim(stiffness, first_col(k, j), cols, 1) - product
-
-    def times(left, right):
-        return jnp.dot(left, right, preferred_element_type=f32)
-
-    parts = [
-        [share(k, 0, times(lower, block)) for k, block in enumerate((upper, z1, z2, z3))],
-        [share(k, 1, times(lower, block)) for k, block in enumerate((x0, x1, x2))],
-    ]
-    parts[1].append(share(3, 1, times(lower[:, :cut], x3_low) + times(lower[:, cut:], x3_high)))
-
-    response = jnp.zeros((rows, mode_count), f32)
-    for j in range(2):
-        for k in range(4):
-            block_modes = lax.dynamic_slice_in_dim(all_modes, first_col(k, j), cols, 0)
-            response = response + jnp.dot(
-                parts[j][k],
-                block_modes.astype(f32),
-                precision=lax.Precision.HIGH,
-                preferred_element_type=f32,
-            )
-    reduced = jnp.einsum(
-        "rm,rc->mc",
-        modes.astype(f32),
-        response,
-        precision=lax.Precision.HIGH,
-        preferred_element_type=f32,
-    )
+    (p00,) = shares(place, stiffness, lower, [(0, 0, upper)], [None])
+    p01, p10 = shares(place, stiffness, lower, [(0, 1, z1), (1, 0, x0)], [None, None])
+    sent_a0, kept_a0, p11 = shares(place, stiffness, lower, [(0, 2, z2), (1, 1, x1)], [p00, None])
+    sent_b0, kept_b0, sent_a1, kept_a1 = shares(
+        place, stiffness, lower, [(0, 3, z3), (1, 2, x2)], [p01, p10]
+    )
+    response = respond(
+        place,
+        near,
+        beside,
+        [(1, 1, p11)],
+        [(0, 0, sent_a0, kept_a0), (0, 1, sent_b0, kept_b0), (1, 0, sent_a1, kept_a1)],
+    )
+    sent_b1, kept_b1, pieces = last_share(
+        place, stiffness, lower, x3_low, x3_high, p11, near, beside, response, modes
+    )
+
     mode_rows = mode_count // tiles
     mode_cols = mode_count // branches
-    pieces = reduced.reshape(tiles, mode_rows, branches, mode_cols).transpose(2, 0, 1, 3)
-    pieces = pieces.reshape(branches * tiles, mode_rows, mode_cols)
-    pieces = lax.all_to_all(pieces, ("subtree", "tile"), 0, 0)
-    stiff_block = jnp.sum(pieces, axis=0)
-
-    final = []
-    keep_first = [from_z[k] % 2 == core for k in range(2)]
-    kept_z = [jnp.where(keep_first[k], from_z[k], from_z[k + 2]) for k in range(2)]
-    stays = kept_z[0] // 2 == y
-    for j in range(2):
-        both = []
-        for k in range(2):
-            kept = jnp.where(keep_first[k], parts[j][k], parts[j][k + 2])
-            sent = jnp.where(keep_first[k], parts[j][k + 2], parts[j][k])
-            both.append(kept + over_core(sent))
-        sent = jnp.where(stays, both[1], both[0])
-        arrived = over_y((sent * SHARE_SCALE).astype(jnp.float16))
-        final.append(
-            jnp.where(stays, both[0], both[1]) + arrived.astype(f32) * (1.0 / SHARE_SCALE)
-        )
-    schur_out = jnp.concatenate(
-        [jnp.where(x == 0, final[0], final[1]), jnp.where(x == 0, final[1], final[0])], axis=1
-    )
-
-    picked = jnp.take(all_modes, gyro_rows, axis=0, mode="clip").astype(f32)
+    pieces = pieces.reshape(branches * tiles, mode_rows // 2, 2 * mode_cols)
+    summed = jnp.sum(lax.all_to_all(pieces, ("subtree", "tile"), 0, 0), axis=0)
+    stiff_block = jnp.concatenate([summed[:, :mode_cols], summed[:, mode_cols:]], axis=0)
+
+    own, came = [], []
+    for kept, sent in (
+        ((kept_a0, kept_b0), (sent_a0, sent_b0)),
+        ((kept_a1, kept_b1), (sent_a1, sent_b1)),
+    ):
+        gone, stayed = join(place, kept, [over_core(s) for s in sent])
+        own.append(stayed)
+        came.append(over_y(gone))
+    schur_out = finish(place, own, came)
+
+    row_tile, row_in = gyro_rows // modes.shape[0], gyro_rows % modes.shape[0]
+    dist = (row_in // chunk) ^ branch
+    turn = (gray(tile // 2) - gray(row_tile // 2)) & 3
+    held = ((dist & 1) * 2 + (dist >> 1)) * 8 + ((row_tile ^ tile) & 1) * 4 + turn
+    table = jnp.concatenate([near, beside]).reshape(tiles * modes.shape[0], mode_count)
+    picked = jnp.take(table, held * chunk + row_in % chunk, axis=0, mode="clip").astype(f32)
     gyro_block, spin_block = gyro_parts(
         picked,
         gyro_coupling,

time: 159 us -> 134 us (0.84)
  local copies, waits for them, and re-layouts: 42.7 us -> 12.8 us
  Pallas kernels: 0 us -> 20.1 us
  matrix products: 22.9 us -> 3.08 us
  waiting for transfers between devices: 48.6 us -> 56.4 us
  starting transfers between devices: 27.8 us -> 26.2 us
    dynamic_slice x9 -> x0, local copies, waits for them, and re-layouts: 24.2 us -> none  [share(): lax.dynamic_slice_in_dim(stiffness, first_col(k, j), cols, 1) - product]
    dot_general x18 -> x0, matrix products: 20.2 us -> none  [the longest x9 11.9 us: times(): return jnp.dot(left, right, preferred_element_type=f32)]
    pallas_call x0 -> x6, Pallas kernels: none -> 20.1 us  [the longest x4 9.94 us: shares(): call(body, (steps,), in_specs, [tile_spec] * outs, [jax.ShapeDtypeStruct(...]
    dynamic_update_slice x8 -> x0, local copies, waits for them, and re-layouts: 5.81 us -> none  [shards_ring(): lax.dynamic_update_slice(quarter, source[k][None, None], (from_z[k], from...]
    ppermute x7, waiting for transfers between devices: 20.4 us -> 25.4 us  [over_z(): return lax.ppermute(block, 'tile', step)]
    ppermute x3, waiting for transfers between devices: 21.2 us -> 24.8 us  [over_y(): return lax.ppermute(block, 'subtree', [(i, i ^ 2) for i in range(branches)])]
    concatenate x1 -> x3, other arithmetic: 0.17 us -> 3.15 us  [the longest x1 2.88 us: shards_ring(): jnp.concatenate([near, beside]).reshape(tiles * modes.shape[0], mode_count)]
    convert_element_type x2, other arithmetic: 7.54 us -> 4.63 us  [join(): (sent * SHARE_SCALE).astype(jnp.float16)]
  transfers between devices with their start and end apart: 21 -> 21, of which waited for: 9 -> 8; matrix products, arithmetic and copies ran while one was open for 46% -> 16% of each run, Pallas kernels for 0% -> 15%
where the time goes in v2:
time: 134 us; the launch traced here: 133 us
  waiting for transfers between devices  56.4 us (42%)
  starting transfers between devices  26.2 us (20%)
  Pallas kernels  20.1 us (15%)
  other arithmetic  13.9 us (10%)
  local copies, waits for them, and re-layouts  12.8 us (10%)
  matrix products  3.08 us (2%)
    ppermute x7, waiting for transfers between devices, over_z(): return lax.ppermute(block, 'tile', step)  25.4 us
    ppermute x3, waiting for transfers between devices, over_y(): return lax.ppermute(block, 'subtree', [(i, i ^ 2) for i in range(branches)])  24.8 us
    ppermute x7, starting transfers between devices, over_z(): return lax.ppermute(block, 'tile', step)  11.8 us
    pallas_call x4, Pallas kernels, shares(): call(body, (steps,), in_specs, [tile_spec] * outs, [jax.ShapeDtypeStruct(...  9.94 us
    unnamed x35, local copies, waits for them, and re-layouts  9.23 us
    ppermute x5, starting transfers between devices, over_x(): return lax.ppermute(block, 'tile', [(i, i ^ 1) for i in range(tiles)])  6.92 us
    pallas_call x1, Pallas kernels, respond(): call(body, (rows // step,), [whole(near.shape), whole(beside.shape)] + [t...  5.22 us
    ppermute x5, waiting for transfers between devices, over_x(): return lax.ppermute(block, 'tile', [(i, i ^ 1) for i in range(tiles)])  5.2 us
  transfers between devices with their start and end apart: 21, of which 8 were waited for; matrix products, arithmetic and copies ran while one was open for 16% of the time, Pallas kernels for 15%

profile of v2, /device:TPU:0, one launch (start us, length us, event | category | flops | bytes accessed | tf_op | source)
XLA Modules:
  0.0 133.4 jit_solution(13667824400741798047)
XLA Ops:
  1.5 3.1 %collective-permute-start.12 = (bf16[128,256]{1,0:T(8,128)(2,1)S(1)}, bf16[128,256]{1,0:T(8,128)(2,1)S(1)}, u32[]{:S(2)}, u32[]{:S(2)}) collective-permute-start(bf16[128,256]{1,0:T(8,128)(2,1)S(1)} %get-tuple-element.39), channel_id=1, source_target_pairs={{0,2},{1,3},{2,6},{3,7},{6,4},{7,5},{4,0},{5,1},{8,10},{9,11},{10,... | collective-permute-start | bytes 196616 | tf_op jit(solution)/shard_map/ppermute | solution.py:367
  4.6 3.3 %collective-permute-done.12 = bf16[128,256]{1,0:T(8,128)(2,1)S(1)} collective-permute-done((bf16[128,256]{1,0:T(8,128)(2,1)S(1)}, bf16[128,256]{1,0:T(8,128)(2,1)S(1)}, u32[]{:S(2)}, u32[]{:S(2)}) %collective-permute-start.12) | collective-permute-done | bytes 65568 | tf_op jit(solution)/shard_map/ppermute | solution.py:367
  9.1 3.3 %collective-permute-start = (bf16[512,512]{1,0:T(8,128)(2,1)}, bf16[512,512]{1,0:T(8,128)(2,1)S(1)}, u32[]{:S(2)}, u32[]{:S(2)}) collective-permute-start(bf16[512,512]{1,0:T(8,128)(2,1)} %bitcast.36), channel_id=1, source_target_pairs={{0,2},{1,3},{2,6},{3,7},{6,4},{7,5},{4,0},{5,1},{8,10},{9,11},{10,... | collective-permute-start | bytes 1572872 | tf_op jit(solution)/shard_map/ppermute | solution.py:367
  12.3 1.5 %collective-permute-start.1 = (bf16[512,512]{1,0:T(8,128)(2,1)}, bf16[512,512]{1,0:T(8,128)(2,1)S(1)}, u32[]{:S(2)}, u32[]{:S(2)}) collective-permute-start(bf16[512,512]{1,0:T(8,128)(2,1)} %bitcast.37), channel_id=1, source_target_pairs={{0,1},{1,0},{2,3},{3,2},{4,5},{5,4},{6,7},{7,6},{8,9},{9,8},{10,11... | collective-permute-start | bytes 1572872 | tf_op jit(solution)/shard_map/ppermute | solution.py:370
  14.9 9.9 %collective-permute-done.14 = bf16[128,256]{1,0:T(8,128)(2,1)S(1)} collective-permute-done((bf16[128,256]{1,0:T(8,128)(2,1)S(1)}, bf16[128,256]{1,0:T(8,128)(2,1)S(1)}, u32[]{:S(2)}, u32[]{:S(2)}) %collective-permute-start.14) | collective-permute-done | bytes 65568 | tf_op jit(solution)/shard_map/ppermute | solution.py:367
  24.8 1.6 %collective-permute-start.15 = (bf16[4,128,256]{2,1,0:T(8,128)(2,1)S(1)}, bf16[4,128,256]{2,1,0:T(8,128)(2,1)S(1)}, u32[]{:S(2)}, u32[]{:S(2)}) collective-permute-start(bf16[4,128,256]{2,1,0:T(8,128)(2,1)S(1)} %pad_maximum_fusion.3), channel_id=1, source_target_pairs={{0,1},{1,0},{2,3},{3,2},{4,5},{5,4},{6,7},{7,6},{8,9},{9,8},{10,11... | collective-permute-start | bytes 786440 | tf_op jit(solution)/shard_map/ppermute | solution.py:370
  26.4 5.2 %collective-permute-done.15 = bf16[4,128,256]{2,1,0:T(8,128)(2,1)S(1)} collective-permute-done((bf16[4,128,256]{2,1,0:T(8,128)(2,1)S(1)}, bf16[4,128,256]{2,1,0:T(8,128)(2,1)S(1)}, u32[]{:S(2)}, u32[]{:S(2)}) %collective-permute-start.15) | collective-permute-done | bytes 262176 | tf_op jit(solution)/shard_map/ppermute | solution.py:370
  31.6 1.3 %collective-permute-start.16 = (bf16[8,128,256]{2,1,0:T(8,128)(2,1)S(1)}, bf16[8,128,256]{2,1,0:T(8,128)(2,1)S(1)}, u32[]{:S(2)}, u32[]{:S(2)}) collective-permute-start(bf16[8,128,256]{2,1,0:T(8,128)(2,1)S(1)} %constant_dynamic-update-slice_fusion), channel_id=1, source_target_pairs={{0,16},{8,24},{16,0},{24,8},{1,17},{9,25},{17,1},{25,9},{2,18},{10... | collective-permute-start | bytes 1572872 | tf_op jit(solution)/shard_map/ppermute | solution.py:373
  34.3 1.5 %collective-permute-start.3 = (bf16[512,512]{1,0:T(8,128)(2,1)S(1)}, bf16[512,512]{1,0:T(8,128)(2,1)S(1)}, u32[]{:S(2)}, u32[]{:S(2)}) collective-permute-start(bf16[512,512]{1,0:T(8,128)(2,1)S(1)} %collective-permute-done.refs_3_), channel_id=1, source_target_pairs={{0,1},{1,0},{2,3},{3,2},{4,5},{5,4},{6,7},{7,6},{8,9},{9,8},{10,11... | collective-permute-start | bytes 1572872 | tf_op jit(solution)/shard_map/ppermute | solution.py:370
  35.8 7.3 %collective-permute-done.16 = bf16[8,128,256]{2,1,0:T(8,128)(2,1)S(1)} collective-permute-done((bf16[8,128,256]{2,1,0:T(8,128)(2,1)S(1)}, bf16[8,128,256]{2,1,0:T(8,128)(2,1)S(1)}, u32[]{:S(2)}, u32[]{:S(2)}) %collective-permute-start.16) | collective-permute-done | bytes 524320 | tf_op jit(solution)/shard_map/ppermute | solution.py:373
  44.3 2.5 %copy.10 = f32[512,512]{0,1:T(8,128)} copy(f32[512,512]{1,0:T(8,128)} %param.13) | data formatting | bytes 2097152 | tf_op args[5]
  46.9 3.4 %copy-done = f32[1,512,4096]{2,1,0:T(8,128)S(1)} copy-done((f32[1,512,4096]{2,1,0:T(8,128)S(1)}, f32[1,512,4096]{2,1,0:T(8,128)}, u32[]{:S(2)}) %copy-start) | copy-done | bytes 8388632
  51.6 1.3 collective-permute-start.6
  53.0 1.7 %shard_map.97 = (f32[512,512]{1,0:T(8,128)S(1)}, f32[512,512]{1,0:T(8,128)S(1)}) custom-call(s32[2]{0:T(128)S(1)} %pad_add_fusion.at, f32[512,4096]{1,0:T(8,128)S(1)} %bitcast.27, f32[512,4096]{1,0:T(8,128)S(1)} %bitcast.28, bf16[512,512]{1,0:T(8,128)(2,1)S(1)} %bitcast.32, bf16[512,512]{1,0:T(8,128)(2,1)S(1)} %collective-permute-done.refs_3_, ...), custom_call_target="tpu_custom_call" | custom-call | flops 536870912 | bytes 4194304 | tf_op jit(solution)/shard_map/pallas_call | solution.py:213
  54.7 12.2 %collective-permute-done.5.refs_3_ = bf16[512,512]{1,0:T(8,128)(2,1)S(1)} collective-permute-done((bf16[512,512]{1,0:T(8,128)(2,1)S(1)}, bf16[512,512]{1,0:T(8,128)(2,1)S(1)}, u32[]{:S(2)}, u32[]{:S(2)}) %collective-permute-start.5) | collective-permute-done | bytes 524320 | tf_op jit(solution)/shard_map/ppermute | solution.py:367
  68.0 1.8 %collective-permute-start.11 = (bf16[256,512]{1,0:T(8,128)(2,1)S(1)}, bf16[256,512]{1,0:T(8,128)(2,1)S(1)}, u32[]{:S(2)}, u32[]{:S(2)}) collective-permute-start(bf16[256,512]{1,0:T(8,128)(2,1)S(1)} %slice.13), channel_id=1, source_target_pairs={{0,2},{1,3},{2,6},{3,7},{6,4},{7,5},{4,0},{5,1},{8,10},{9,11},{10,... | collective-permute-start | bytes 786440 | tf_op jit(solution)/shard_map/ppermute | solution.py:367
  69.8 2.7 %shard_map.96 = (f32[512,512]{1,0:T(8,128)}, f32[512,512]{1,0:T(8,128)S(1)}, f32[512,512]{1,0:T(8,128)S(1)}) custom-call(s32[2]{0:T(128)S(1)} %pad_add_fusion.at, f32[512,4096]{1,0:T(8,128)S(1)} %bitcast.29, f32[512,4096]{1,0:T(8,128)S(1)} %bitcast.30, bf16[512,512]{1,0:T(8,128)(2,1)S(1)} %bitcast.33, bf16[512,512]{1,0:T(8,128)(2,1)S(1)} %collective-permute-done.2.refs_3_, ...), custom_call_target="tpu_custom_call" | custom-call | flops 536870912 | bytes 5242880 | tf_op jit(solution)/shard_map/pallas_call | solution.py:213
  72.4 4.3 %shard_map.98 = (f32[512,512]{1,0:T(8,128)}, f32[512,512]{1,0:T(8,128)S(1)}, f32[512,512]{1,0:T(8,128)}, f32[512,512]{1,0:T(8,128)S(1)}) custom-call(s32[2]{0:T(128)S(1)} %pad_add_fusion.at, f32[512,4096]{1,0:T(8,128)} %bitcast.23, f32[512,4096]{1,0:T(8,128)} %bitcast.24, bf16[512,512]{1,0:T(8,128)(2,1)S(1)} %bitcast.34, ...), custom_call_target="tpu_custom_call" | custom-call | flops 536870912 | bytes 6291456 | tf_op jit(solution)/shard_map/pallas_call | solution.py:213
  77.4 5.2 %shard_map.99.resp = f32[512,256]{1,0:T(8,128)S(1)} custom-call(s32[2]{0:T(128)S(1)} %pad_add_fusion.at, bf16[2,8,128,256]{3,2,1,0:T(8,128)(2,1)} %pad_maximum_fusion.2.near_ref, bf16[2,8,128,256]{3,2,1,0:T(8,128)(2,1)} %collective-permute-done.17.beside_ref, f32[512,512]{1,0:T(8,128)S(1)} %get-tuple-element.34.refs_0_.old_ref, ...), custom_call_target="tpu_custom_call" | custom-call | flops 1879048192 | bytes 7340032 | tf_op jit(solution)/shard_map/pallas_call | solution.py:252
  82.7 4.9 %shard_map.100 = (f32[512,512]{1,0:T(8,128)}, f32[512,512]{1,0:T(8,128)S(1)}, f32[4,128,128]{2,1,0:T(8,128)}) custom-call(s32[2]{0:T(128)S(1)} %pad_add_fusion.at, f32[512,4096]{1,0:T(8,128)} %bitcast.25, bf16[512,512]{1,0:T(8,128)(2,1)S(1)} %bitcast.35, bf16[256,512]{1,0:T(8,128)(2,1)S(1)} %collective-permute-done.10.lo, ...), custom_call_target="tpu_custom_call" | custom-call | flops 536870912 | bytes 4194304 | tf_op jit(solution)/shard_map/pallas_call | solution.py:305
  89.1 2.9 %all-to-all-start = ((f32[32,16,128]{2,1,0:T(8,128)}), f32[32,16,128]{2,1,0:T(8,128)S(1)}, u32[]{:S(2)}, u32[]{:S(2)}) async-start(f32[32,16,128]{2,1,0:T(8,128)} %bitcast.11), calls=%async_computation | async-start | bytes 524288 | tf_op jit(solution)/shard_map/all_to_all | solution.py:413
  92.0 2.9 %pad_maximum_fusion.1 = bf16[4,8,128,256]{3,2,1,0:T(8,128)(2,1)} fusion(bf16[2,8,128,256]{3,2,1,0:T(8,128)(2,1)} %collective-permute-done.17.beside_ref, bf16[1,8,128,256]{3,2,1,0:T(8,128)(2,1)} %bitcast.43, bf16[1,8,128,256]{3,2,1,0:T(8,128)(2,1)S(1)} %bitcast.41), kind=kLoop, calls=%fused_computation.2 | loop fusion | flops 2097152 | bytes 4194304 | tf_op jit(solution)/shard_map/concatenate | solution.py:430
  94.8 3.4 %gather_fusion = bf16[512,256]{1,0:T(8,128)(2,1)S(1)} fusion(bf16[4096,256]{1,0:T(8,128)(2,1)} %bitcast.39, s32[1024]{0:T(1024)S(1)} %pad_clamp_fusion), kind=kCustom, calls=%fused_computation | custom fusion | bytes 526336 | tf_op jit(solution)/shard_map/jit(_take)/gather | solution.py:431
  98.3 2.2 %fusion.1 = f32[512,64]{1,0:T(8,128)S(1)} fusion(f32[512,512]{1,0:T(8,128)} %param.13, f32[512,512]{0,1:T(8,128)} %copy.10, bf16[512,256]{1,0:T(8,128)(2,1)S(1)} %gather_fusion, s32[]{:T(128)S(6)} %select_n.77), kind=kOutput, calls=%fused_computation.6 | convolution fusion | flops 201850880 | bytes 2359300 | tf_op jit(solution)/shard_map/dot_general | solution.py:33
  102.6 2.5 %multiply_convert_fusion.1 = f16[512,512]{1,0:T(8,128)(2,1)S(1)} fusion(pred[]{:T(512)S(6)} %eq.12, f32[512,512]{1,0:T(8,128)} %copy-done.2, f32[512,512]{1,0:T(8,128)} %collective-permute-done.7, f32[512,512]{1,0:T(8,128)S(1)} %get-tuple-element.23.refs_2_, f32[512,512]{1,0:T(8,128)} %collective-permute-done.4), kind=kLoop, calls=%fused_computation.10 | loop fusion | flops 1310720 | bytes 4718593 | tf_op jit(solution)/shard_map/convert_element_type | solution.py:331
  106.4 2.2 %multiply_convert_fusion = f16[512,512]{1,0:T(8,128)(2,1)S(1)} fusion(pred[]{:T(512)S(6)} %eq.12, f32[512,512]{1,0:T(8,128)S(1)} %copy-done.5, f32[512,512]{1,0:T(8,128)} %collective-permute-done.18, f32[512,512]{1,0:T(8,128)S(1)} %get-tuple-element.32.refs_6_, f32[512,512]{1,0:T(8,128)} %collective-permute-done.9), kind=kLoop, calls=%fused_computation.8 | loop fusion | flops 1310720 | bytes 4718593 | tf_op jit(solution)/shard_map/convert_element_type | solution.py:331
  108.6 1.5 %collective-permute-start.19 = (f16[512,512]{1,0:T(8,128)(2,1)S(1)}, f16[512,512]{1,0:T(8,128)(2,1)S(1)}, u32[]{:S(2)}, u32[]{:S(2)}) collective-permute-start(f16[512,512]{1,0:T(8,128)(2,1)S(1)} %multiply_convert_fusion), channel_id=1, source_target_pairs={{0,16},{8,24},{16,0},{24,8},{1,17},{9,25},{17,1},{25,9},{2,18},{10... | collective-permute-start | bytes 1572872 | tf_op jit(solution)/shard_map/ppermute | solution.py:373
  110.1 9.9 %collective-permute-done.8 = f16[512,512]{1,0:T(8,128)(2,1)S(1)} collective-permute-done((f16[512,512]{1,0:T(8,128)(2,1)S(1)}, f16[512,512]{1,0:T(8,128)(2,1)S(1)}, u32[]{:S(2)}, u32[]{:S(2)}) %collective-permute-start.8) | collective-permute-done | bytes 524320 | tf_op jit(solution)/shard_map/ppermute | solution.py:373
  119.9 2.1 %multiply_add_fusion = f32[512,512]{1,0:T(8,128)S(1)} fusion(f16[512,512]{1,0:T(8,128)(2,1)S(1)} %collective-permute-done.8, pred[]{:T(512)S(6)} %eq.12, f32[512,512]{1,0:T(8,128)S(1)} %copy-done.3, f32[512,512]{1,0:T(8,128)} %collective-permute-done.7, f32[512,512]{1,0:T(8,128)S(1)} %get-tuple-element.23.refs_2_, f32[512,512]{1,0:T(8,128)} %collective-permute-done.4), kind=kLoop, calls=%fused_computation.9 | loop fusion | flops 1572864 | bytes 5767169 | tf_op jit(solution)/shard_map/add | solution.py:336
  122.3 7.6 %collective-permute-done.19 = f16[512,512]{1,0:T(8,128)(2,1)S(1)} collective-permute-done((f16[512,512]{1,0:T(8,128)(2,1)S(1)}, f16[512,512]{1,0:T(8,128)(2,1)S(1)}, u32[]{:S(2)}, u32[]{:S(2)}) %collective-permute-start.19) | collective-permute-done | bytes 524320 | tf_op jit(solution)/shard_map/ppermute | solution.py:373
  129.9 2.1 %add_dynamic-update-slice_fusion = f32[512,1024]{1,0:T(8,128)S(1)} fusion(f32[512,1024]{1,0:T(8,128)S(1)} %pad_maximum_fusion, s32[]{:T(128)S(6)} %select_n.69, f16[512,512]{1,0:T(8,128)(2,1)S(1)} %collective-permute-done.19, pred[]{:T(512)S(6)} %eq.12, f32[512,512]{1,0:T(8,128)S(1)} %copy-done.5, f32[512,512]{1,0:T(8,128)} %collective-permute-done.18, ...), kind=kLoop, calls=%fused_computation.7 | loop fusion | flops 1572864 | bytes 5767173 | tf_op jit(solution)/shard_map/dynamic_update_slice | solution.py:339
  132.1 1.3 copy-done.10
  (74 shorter events, 14.0 us)
Async XLA Ops:
  1.5 6.3 %collective-permute-start.12 = (bf16[128,256]{1,0:T(8,128)(2,1)S(1)}, bf16[128,256]{1,0:T(8,128)(2,1)S(1)}, u32[]{:S(2)}, u32[]{:S(2)}) collective-permute-start(bf16[128,256]{1,0:T(8,128)(2,1)S(1)} %get-tuple-element.39), channel_id=1, source_target_pairs={{0,2},{1,3},{2,6},{3,7},{6,4},{7,5},{4,0},{5,1},{8,10},{9,11},{10,... | collective-permute-start | bytes 196616 | tf_op jit(solution)/shard_map/ppermute | solution.py:367
  7.8 6.0 %collective-permute-start.13 = (bf16[128,256]{1,0:T(8,128)(2,1)S(1)}, bf16[128,256]{1,0:T(8,128)(2,1)S(1)}, u32[]{:S(2)}, u32[]{:S(2)}) collective-permute-start(bf16[128,256]{1,0:T(8,128)(2,1)S(1)} %collective-permute-done.12), channel_id=1, source_target_pairs={{0,2},{1,3},{2,6},{3,7},{6,4},{7,5},{4,0},{5,1},{8,10},{9,11},{10,... | collective-permute-start | bytes 196616 | tf_op jit(solution)/shard_map/ppermute | solution.py:367
  9.1 23.9 %collective-permute-start = (bf16[512,512]{1,0:T(8,128)(2,1)}, bf16[512,512]{1,0:T(8,128)(2,1)S(1)}, u32[]{:S(2)}, u32[]{:S(2)}) collective-permute-start(bf16[512,512]{1,0:T(8,128)(2,1)} %bitcast.36), channel_id=1, source_target_pairs={{0,2},{1,3},{2,6},{3,7},{6,4},{7,5},{4,0},{5,1},{8,10},{9,11},{10,... | collective-permute-start | bytes 1572872 | tf_op jit(solution)/shard_map/ppermute | solution.py:367
  12.3 20.7 %collective-permute-start.1 = (bf16[512,512]{1,0:T(8,128)(2,1)}, bf16[512,512]{1,0:T(8,128)(2,1)S(1)}, u32[]{:S(2)}, u32[]{:S(2)}) collective-permute-start(bf16[512,512]{1,0:T(8,128)(2,1)} %bitcast.37), channel_id=1, source_target_pairs={{0,1},{1,0},{2,3},{3,2},{4,5},{5,4},{6,7},{7,6},{8,9},{9,8},{10,11... | collective-permute-start | bytes 1572872 | tf_op jit(solution)/shard_map/ppermute | solution.py:370
  13.8 11.0 %collective-permute-start.14 = (bf16[128,256]{1,0:T(8,128)(2,1)S(1)}, bf16[128,256]{1,0:T(8,128)(2,1)S(1)}, u32[]{:S(2)}, u32[]{:S(2)}) collective-permute-start(bf16[128,256]{1,0:T(8,128)(2,1)S(1)} %collective-permute-done.13), channel_id=1, source_target_pairs={{0,2},{1,3},{2,6},{3,7},{6,4},{7,5},{4,0},{5,1},{8,10},{9,11},{10,... | collective-permute-start | bytes 196616 | tf_op jit(solution)/shard_map/ppermute | solution.py:367
  24.8 6.8 %collective-permute-start.15 = (bf16[4,128,256]{2,1,0:T(8,128)(2,1)S(1)}, bf16[4,128,256]{2,1,0:T(8,128)(2,1)S(1)}, u32[]{:S(2)}, u32[]{:S(2)}) collective-permute-start(bf16[4,128,256]{2,1,0:T(8,128)(2,1)S(1)} %pad_maximum_fusion.3), channel_id=1, source_target_pairs={{0,1},{1,0},{2,3},{3,2},{4,5},{5,4},{6,7},{7,6},{8,9},{9,8},{10,11... | collective-permute-start | bytes 786440 | tf_op jit(solution)/shard_map/ppermute | solution.py:370
  31.6 11.5 %copy-start.8 = (bf16[8,128,256]{2,1,0:T(8,128)(2,1)}, bf16[8,128,256]{2,1,0:T(8,128)(2,1)S(1)}, u32[]{:S(2)}) copy-start(bf16[8,128,256]{2,1,0:T(8,128)(2,1)S(1)} %constant_dynamic-update-slice_fusion) | copy-start | bytes 1572868
  31.6 11.5 %collective-permute-start.16 = (bf16[8,128,256]{2,1,0:T(8,128)(2,1)S(1)}, bf16[8,128,256]{2,1,0:T(8,128)(2,1)S(1)}, u32[]{:S(2)}, u32[]{:S(2)}) collective-permute-start(bf16[8,128,256]{2,1,0:T(8,128)(2,1)S(1)} %constant_dynamic-update-slice_fusion), channel_id=1, source_target_pairs={{0,16},{8,24},{16,0},{24,8},{1,17},{9,25},{17,1},{25,9},{2,18},{10... | collective-permute-start | bytes 1572872 | tf_op jit(solution)/shard_map/ppermute | solution.py:373
  33.0 18.5 %collective-permute-start.2 = (bf16[512,512]{1,0:T(8,128)(2,1)S(1)}, bf16[512,512]{1,0:T(8,128)(2,1)S(1)}, u32[]{:S(2)}, u32[]{:S(2)}) collective-permute-start(bf16[512,512]{1,0:T(8,128)(2,1)S(1)} %collective-permute-done.refs_3_), channel_id=1, source_target_pairs={{0,2},{1,3},{2,6},{3,7},{6,4},{7,5},{4,0},{5,1},{8,10},{9,11},{10,... | collective-permute-start | bytes 1572872 | tf_op jit(solution)/shard_map/ppermute | solution.py:367
  34.3 17.3 %collective-permute-start.3 = (bf16[512,512]{1,0:T(8,128)(2,1)S(1)}, bf16[512,512]{1,0:T(8,128)(2,1)S(1)}, u32[]{:S(2)}, u32[]{:S(2)}) collective-permute-start(bf16[512,512]{1,0:T(8,128)(2,1)S(1)} %collective-permute-done.refs_3_), channel_id=1, source_target_pairs={{0,1},{1,0},{2,3},{3,2},{4,5},{5,4},{6,7},{7,6},{8,9},{9,8},{10,11... | collective-permute-start | bytes 1572872 | tf_op jit(solution)/shard_map/ppermute | solution.py:370
  43.1 3.8 %copy-start.1 = (bf16[1,512,512]{2,1,0:T(8,128)(2,1)S(1)}, bf16[1,512,512]{2,1,0:T(8,128)(2,1)}, u32[]{:S(2)}) copy-start(bf16[1,512,512]{2,1,0:T(8,128)(2,1)} %param.9) | copy-start | bytes 1572868
  43.1 3.8 %copy-start.6 = (bf16[1,512,512]{2,1,0:T(8,128)(2,1)S(1)}, bf16[1,512,512]{2,1,0:T(8,128)(2,1)}, u32[]{:S(2)}) copy-start(bf16[1,512,512]{2,1,0:T(8,128)(2,1)} %param.10) | copy-start | bytes 1572868
  44.3 33.1 %collective-permute-start.17 = (bf16[2,8,128,256]{3,2,1,0:T(8,128)(2,1)}, bf16[2,8,128,256]{3,2,1,0:T(8,128)(2,1)}, u32[]{:S(2)}, u32[]{:S(2)}) collective-permute-start(bf16[2,8,128,256]{3,2,1,0:T(8,128)(2,1)} %pad_maximum_fusion.2.near_ref), channel_id=1, source_target_pairs={{0,8},{8,0},{16,24},{24,16},{1,9},{9,1},{17,25},{25,17},{2,10},{10... | collective-permute-start | bytes 3145736 | tf_op jit(solution)/shard_map/ppermute | solution.py:376
  46.9 3.4 %copy-start = (f32[1,512,4096]{2,1,0:T(8,128)S(1)}, f32[1,512,4096]{2,1,0:T(8,128)}, u32[]{:S(2)}) copy-start(f32[1,512,4096]{2,1,0:T(8,128)} %param.8) | copy-start | bytes 25165828
  50.3 2.7 %copy-start.14 = (s32[2]{0:T(128)S(1)}, s32[2]{0:T(128)}, u32[]{:S(2)}) copy-start(s32[2]{0:T(128)} %param.15) | copy-start | bytes 28
  51.6 15.3 %collective-permute-start.5 = (bf16[512,512]{1,0:T(8,128)(2,1)S(1)}, bf16[512,512]{1,0:T(8,128)(2,1)S(1)}, u32[]{:S(2)}, u32[]{:S(2)}) collective-permute-start(bf16[512,512]{1,0:T(8,128)(2,1)S(1)} %collective-permute-done.2.refs_3_), channel_id=1, source_target_pairs={{0,2},{1,3},{2,6},{3,7},{6,4},{7,5},{4,0},{5,1},{8,10},{9,11},{10,... | collective-permute-start | bytes 1572872 | tf_op jit(solution)/shard_map/ppermute | solution.py:367
  51.6 15.2 %collective-permute-start.6 = (bf16[512,512]{1,0:T(8,128)(2,1)S(1)}, bf16[512,512]{1,0:T(8,128)(2,1)S(1)}, u32[]{:S(2)}, u32[]{:S(2)}) collective-permute-start(bf16[512,512]{1,0:T(8,128)(2,1)S(1)} %collective-permute-done.2.refs_3_), channel_id=1, source_target_pairs={{0,1},{1,0},{2,3},{3,2},{4,5},{5,4},{6,7},{7,6},{8,9},{9,8},{10,11... | collective-permute-start | bytes 1572872 | tf_op jit(solution)/shard_map/ppermute | solution.py:370
  66.9 15.8 %collective-permute-start.10 = (bf16[256,512]{1,0:T(8,128)(2,1)S(1)}, bf16[256,512]{1,0:T(8,128)(2,1)S(1)}, u32[]{:S(2)}, u32[]{:S(2)}) collective-permute-start(bf16[256,512]{1,0:T(8,128)(2,1)S(1)} %slice.12), channel_id=1, source_target_pairs={{0,1},{1,0},{2,3},{3,2},{4,5},{5,4},{6,7},{7,6},{8,9},{9,8},{10,11... | collective-permute-start | bytes 786440 | tf_op jit(solution)/shard_map/ppermute | solution.py:370
  68.0 14.7 %collective-permute-start.11 = (bf16[256,512]{1,0:T(8,128)(2,1)S(1)}, bf16[256,512]{1,0:T(8,128)(2,1)S(1)}, u32[]{:S(2)}, u32[]{:S(2)}) collective-permute-start(bf16[256,512]{1,0:T(8,128)(2,1)S(1)} %slice.13), channel_id=1, source_target_pairs={{0,2},{1,3},{2,6},{3,7},{6,4},{7,5},{4,0},{5,1},{8,10},{9,11},{10,... | collective-permute-start | bytes 786440 | tf_op jit(solution)/shard_map/ppermute | solution.py:367
  72.4 30.1 %collective-permute-start.4 = (f32[512,512]{1,0:T(8,128)}, f32[512,512]{1,0:T(8,128)}, u32[]{:S(2)}, u32[]{:S(2)}) collective-permute-start(f32[512,512]{1,0:T(8,128)} %get-tuple-element.24.refs_1_), channel_id=1, source_target_pairs={{0,8},{8,0},{16,24},{24,16},{1,9},{9,1},{17,25},{25,17},{2,10},{10... | collective-permute-start | bytes 3145736 | tf_op jit(solution)/shard_map/ppermute | solution.py:376
  76.8 5.9 %copy-start.2 = (f32[512,512]{1,0:T(8,128)}, f32[512,512]{1,0:T(8,128)S(1)}, u32[]{:S(2)}) copy-start(f32[512,512]{1,0:T(8,128)S(1)} %get-tuple-element.30.refs_4_) | copy-start | bytes 3145732
  76.8 25.8 %collective-permute-start.7 = (f32[512,512]{1,0:T(8,128)}, f32[512,512]{1,0:T(8,128)}, u32[]{:S(2)}, u32[]{:S(2)}) collective-permute-start(f32[512,512]{1,0:T(8,128)} %get-tuple-element.31.refs_3_), channel_id=1, source_target_pairs={{0,8},{8,0},{16,24},{24,16},{1,9},{9,1},{17,25},{25,17},{2,10},{10... | collective-permute-start | bytes 3145736 | tf_op jit(solution)/shard_map/ppermute | solution.py:376
  77.3 29.1 %collective-permute-start.9 = (f32[512,512]{1,0:T(8,128)}, f32[512,512]{1,0:T(8,128)}, u32[]{:S(2)}, u32[]{:S(2)}) collective-permute-start(f32[512,512]{1,0:T(8,128)} %get-tuple-element.33.refs_5_), channel_id=1, source_target_pairs={{0,8},{8,0},{16,24},{24,16},{1,9},{9,1},{17,25},{25,17},{2,10},{10... | collective-permute-start | bytes 3145736 | tf_op jit(solution)/shard_map/ppermute | solution.py:376
  77.4 5.3 %copy-start.7 = (bf16[512,256]{1,0:T(8,128)(2,1)S(1)}, bf16[512,256]{1,0:T(8,128)(2,1)}, u32[]{:S(2)}) copy-start(bf16[512,256]{1,0:T(8,128)(2,1)} %mode.1) | copy-start | bytes 786436
  82.6 9.3 %copy-start.9 = (bf16[8,128,256]{2,1,0:T(8,128)(2,1)S(1)}, bf16[8,128,256]{2,1,0:T(8,128)(2,1)}, u32[]{:S(2)}) copy-start(bf16[8,128,256]{2,1,0:T(8,128)(2,1)} %copy-done.8) | copy-start | bytes 1572868
  88.6 17.8 %collective-permute-start.18 = (f32[512,512]{1,0:T(8,128)}, f32[512,512]{1,0:T(8,128)}, u32[]{:S(2)}, u32[]{:S(2)}) collective-permute-start(f32[512,512]{1,0:T(8,128)} %get-tuple-element.36), channel_id=1, source_target_pairs={{0,8},{8,0},{16,24},{24,16},{1,9},{9,1},{17,25},{25,17},{2,10},{10... | collective-permute-start | bytes 3145736 | tf_op jit(solution)/shard_map/ppermute | solution.py:376
  89.1 13.4 %all-to-all-start = ((f32[32,16,128]{2,1,0:T(8,128)}), f32[32,16,128]{2,1,0:T(8,128)S(1)}, u32[]{:S(2)}, u32[]{:S(2)}) async-start(f32[32,16,128]{2,1,0:T(8,128)} %bitcast.11), calls=%async_computation | async-start | bytes 524288 | tf_op jit(solution)/shard_map/all_to_all | solution.py:413
  94.8 6.1 %copy-start.12 = (f32[512]{0:T(512)S(1)}, f32[512]{0:T(512)}, u32[]{:S(2)}) copy-start(f32[512]{0:T(512)} %param.14) | copy-start | bytes 6148
  102.5 3.9 %copy-start.5 = (f32[512,512]{1,0:T(8,128)S(1)}, f32[512,512]{1,0:T(8,128)}, u32[]{:S(2)}) copy-start(f32[512,512]{1,0:T(8,128)} %copy-done.4) | copy-start | bytes 3145732
  105.0 14.9 %collective-permute-start.8 = (f16[512,512]{1,0:T(8,128)(2,1)S(1)}, f16[512,512]{1,0:T(8,128)(2,1)S(1)}, u32[]{:S(2)}, u32[]{:S(2)}) collective-permute-start(f16[512,512]{1,0:T(8,128)(2,1)S(1)} %multiply_convert_fusion.1), channel_id=1, source_target_pairs={{0,16},{8,24},{16,0},{24,8},{1,17},{9,25},{17,1},{25,9},{2,18},{10... | collective-permute-start | bytes 1572872 | tf_op jit(solution)/shard_map/ppermute | solution.py:373
  106.4 13.5 %copy-start.3 = (f32[512,512]{1,0:T(8,128)S(1)}, f32[512,512]{1,0:T(8,128)}, u32[]{:S(2)}) copy-start(f32[512,512]{1,0:T(8,128)} %copy-done.2) | copy-start | bytes 3145732
  108.6 21.3 %collective-permute-start.19 = (f16[512,512]{1,0:T(8,128)(2,1)S(1)}, f16[512,512]{1,0:T(8,128)(2,1)S(1)}, u32[]{:S(2)}, u32[]{:S(2)}) collective-permute-start(f16[512,512]{1,0:T(8,128)(2,1)S(1)} %multiply_convert_fusion), channel_id=1, source_target_pairs={{0,16},{8,24},{16,0},{24,8},{1,17},{9,25},{17,1},{25,9},{2,18},{10... | collective-permute-start | bytes 1572872 | tf_op jit(solution)/shard_map/ppermute | solution.py:373
  (4 other events, 6.2 us)

commit v3 on v1

--- a/solution.py
+++ b/solution.py
@@ -1,6 +1,8 @@
 import jax
 import jax.numpy as jnp
 from jax import lax
+from jax.experimental import pallas as pl
+from jax.experimental.pallas import tpu as pltpu
 from jax.sharding import PartitionSpec as P
 
 SPEED_STEPS = 64
@@ -9,6 +11,8 @@
 OMEGA_TOP = 2.0
 
 SHARE_SCALE = 32.0
+
+GRANT = 16 << 20
 
 
 def omegas(speed_index):
@@ -115,6 +119,214 @@
     return (schur_out, combine(stiff_block, gyro_block, spin_block, speed_index))
 
 
+def gray(i):
+    return i ^ (i >> 1)
+
+
+def ring_z(place, k):
+    return gray((gray(place[0] >> 1) + (4 - k)) & 3)
+
+
+def block_at(place, j, k):
+    return ring_z(place, k) * 2 + ((place[0] & 1) ^ j)
+
+
+def keeps(place, k):
+    return (ring_z(place, k) & 1) == (place[1] & 1)
+
+
+def stays(place):
+    return ((gray(place[0] >> 1) - gray(place[1])) & 1) == 0
+
+
+IN_VMEM = pl.BlockSpec(memory_space=pltpu.VMEM)
+
+
+def call(body, operands, outs, scratch=()):
+    return pl.pallas_call(
+        body,
+        out_shape=[jax.ShapeDtypeStruct(shape, dtype) for shape, dtype in outs],
+        in_specs=[pl.BlockSpec(memory_space=pltpu.SMEM)] + [IN_VMEM] * (len(operands) - 1),
+        out_specs=[IN_VMEM] * len(outs),
+        scratch_shapes=scratch,
+        compiler_params=pltpu.CompilerParams(vmem_limit_bytes=GRANT),
+        cost_estimate=pl.CostEstimate(flops=1 << 20, bytes_accessed=1 << 18, transcendentals=0),
+    )(*operands)
+
+
+def mul(left, right):
+    return jnp.dot(left, right, preferred_element_type=jnp.float32)
+
+
+def mul_wide(left, right):
+    high = left.astype(jnp.bfloat16)
+    low = (left - high.astype(jnp.float32)).astype(jnp.bfloat16)
+    return mul(high, right) + mul(low, right)
+
+
+ROW_STEPS = 4
+
+
+def shares(place, stiffness, lower, blocks):
+    rows = stiffness.shape[0]
+    depth = lower.shape[1]
+    cols = blocks[0][2][0].shape[1]
+    step = rows // ROW_STEPS
+    operands = [place, stiffness, lower]
+    outs = []
+    for _, _, pieces, old in blocks:
+        operands += list(pieces) + ([] if old is None else [old])
+        outs += [((rows, cols), jnp.float32)] * (1 if old is None else 2)
+
+    def body(at, stiff, low, *refs):
+        sources, targets = list(refs[: len(operands) - 3]), list(refs[len(operands) - 3 :])
+        for j, k, pieces, old in blocks:
+            uppers = [sources.pop(0) for _ in pieces]
+            before = None if old is None else sources.pop(0)
+            wanted = [targets.pop(0) for _ in range(1 if old is None else 2)]
+            first_col = pl.multiple_of(block_at(at, j, k) * cols, cols)
+            size = depth // len(pieces)
+
+            @pl.loop(0, ROW_STEPS)
+            def _(i):
+                part = pl.ds(pl.multiple_of(i * step, step), step)
+                value = stiff[part, pl.ds(first_col, cols)]
+                for n, ref in enumerate(uppers):
+                    value -= mul(low[part, n * size : (n + 1) * size], ref[:size, :])
+                if before is None:
+                    wanted[0][part, :] = value
+                else:
+                    sent, kept = wanted
+                    keep_old = keeps(at, k - 2)
+                    past = before[part, :]
+                    sent[part, :] = jnp.where(keep_old, value, past)
+                    kept[part, :] = jnp.where(keep_old, past, value)
+
+    return call(body, operands, outs)
+
+
+def fill_modes(at, target, near, beside, n):
+    half, width = near.shape[1], target.shape[1]
+    for other, source in enumerate((near, beside)):
+        first = pl.multiple_of(((at[1] & 1) ^ other) * 2 * half, 2 * half)
+        target[pl.ds(first, half), :] = source[n, :, :width]
+        target[pl.ds(first + half, half), :] = source[n, :, width:]
+
+
+def respond(place, groups, pairs, start, rows, mode_count):
+    cols = pairs[0][3].shape[1]
+    flat = [g for pair in groups for g in pair]
+    shares_in = [s for p in pairs for s in p[3:]]
+    plus = [] if start is None else [start]
+    step = rows // ROW_STEPS
+
+    def body(at, *refs):
+        group_refs = refs[: len(flat)]
+        share_refs = refs[len(flat) : len(flat) + len(shares_in)]
+        out, scratch = refs[-2], refs[-1]
+        for m, (older, newer, k, _, _) in enumerate(pairs):
+            keep_old = keeps(at, k)
+
+            def fill(slot, which):
+                group, n = which
+                fill_modes(at, scratch.at[slot], group_refs[2 * group], group_refs[2 * group + 1], n)
+
+            @pl.when(keep_old)
+            def _():
+                fill(2 * m, newer)
+                fill(2 * m + 1, older)
+
+            @pl.when(jnp.logical_not(keep_old))
+            def _():
+                fill(2 * m, older)
+                fill(2 * m + 1, newer)
+
+        @pl.loop(0, ROW_STEPS)
+        def _(i):
+            part = pl.ds(pl.multiple_of(i * step, step), step)
+            if plus:
+                total = refs[len(flat) + len(shares_in)][part, :]
+            else:
+                total = jnp.zeros((step, mode_count), jnp.float32)
+            for n in range(len(shares_in)):
+                total += mul_wide(share_refs[n][part, :], scratch[n])
+            out[part, :] = total
+
+    return call(
+        body,
+        [place] + flat + shares_in + plus,
+        [((rows, mode_count), jnp.float32)],
+        [pltpu.VMEM((len(shares_in), cols, mode_count), jnp.bfloat16)],
+    )[0]
+
+
+def reduce_modes(place, groups, pair, response, modes, branches, tiles):
+    mode_count = modes.shape[1]
+    group = mode_count // tiles // 2
+    older, newer, k, sent, kept = pair
+    rows, cols = sent.shape
+    flat = [g for both in groups for g in both]
+
+    def body(at, *refs):
+        group_refs = refs[: len(flat)]
+        sent_ref, kept_ref, resp, mode, pieces, scratch = refs[len(flat) :]
+        keep_old = keeps(at, k)
+
+        def fill(slot, which):
+            fill_modes(
+                at, scratch.at[slot], group_refs[2 * which[0]], group_refs[2 * which[0] + 1], which[1]
+            )
+
+        @pl.when(keep_old)
+        def _():
+            fill(0, newer)
+            fill(1, older)
+
+        @pl.when(jnp.logical_not(keep_old))
+        def _():
+            fill(0, older)
+            fill(1, newer)
+
+        total = resp[...] + mul_wide(sent_ref[...], scratch[0]) + mul_wide(kept_ref[...], scratch[1])
+        high = total.astype(jnp.bfloat16)
+        rest = (total - high.astype(jnp.float32)).astype(jnp.bfloat16)
+        across = (((0,), (0,)), ((), ()))
+        reduced = lax.dot_general(
+            mode[...], high, across, preferred_element_type=jnp.float32
+        ) + lax.dot_general(mode[...], rest, across, preferred_element_type=jnp.float32)
+        split = reduced.reshape(tiles, 2, group, mode_count)
+        upper = split[:, 0].reshape(tiles * group, mode_count)
+        under = split[:, 1].reshape(tiles * group, mode_count)
+        left = lax.broadcasted_iota(jnp.int32, (tiles * group, 128), 1) < 64
+        for half in range(branches // 2):
+            u = upper[:, 128 * half : 128 * half + 128]
+            v = under[:, 128 * half : 128 * half + 128]
+            pieces[2 * half] = jnp.where(left, u, pltpu.roll(v, 64, 1))
+            pieces[2 * half + 1] = jnp.where(left, pltpu.roll(u, 64, 1), v)
+
+    return call(
+        body,
+        [place] + flat + [sent, kept, response, modes],
+        [((branches, tiles * group, 128), jnp.float32)],
+        [pltpu.VMEM((2, cols, mode_count), jnp.bfloat16)],
+    )[0]
+
+
+def pick(which, arrays):
+    value = arrays[-1]
+    for n in range(len(arrays) - 2, -1, -1):
+        value = jnp.where(which == n, arrays[n], value)
+    return value
+
+
+def to_wire(value):
+    return (value * SHARE_SCALE).astype(jnp.float16)
+
+
+def from_wire(value):
+    return value.astype(jnp.float32) * (1.0 / SHARE_SCALE)
+
+
 def shards_ring(
     interface_stiffness,
     lower_factor,
@@ -130,21 +342,25 @@
     branches = lax.axis_size("subtree")
     tile = lax.axis_index("tile")
     branch = lax.axis_index("subtree")
-    z, x = tile // 2, tile % 2
-    y, core = branch // 2, branch % 2
+    place = jnp.stack([tile, branch]).astype(jnp.int32)
     stiffness = interface_stiffness[0]
     lower = lower_factor[0]
     upper = upper_factor[0]
-    rows, width = stiffness.shape
+    rows = stiffness.shape[0]
     depth, cols = upper.shape
     mode_count = modes.shape[1]
 
-    def gray(i):
-        return i ^ (i >> 1)
+    def ring_pairs(turn):
+        return [
+            (gray(p) * 2 + a, gray((p + 1) % 4) * 2 + a)
+            if turn
+            else (gray((p + 1) % 4) * 2 + 1 - a, gray(p) * 2 + a)
+            for p in range(4)
+            for a in range(2)
+        ]
 
     def over_z(block):
-        step = [(gray(p) * 2 + a, gray((p + 1) % 4) * 2 + a) for p in range(4) for a in range(2)]
-        return lax.ppermute(block, "tile", step)
+        return lax.ppermute(block, "tile", ring_pairs(True))
 
     def over_x(block):
         return lax.ppermute(block, "tile", [(i, i ^ 1) for i in range(tiles)])
@@ -155,97 +371,101 @@
     def over_core(block):
         return lax.ppermute(block, "subtree", [(i, i ^ 1) for i in range(branches)])
 
-    from_z = [gray((gray(z) - k) % 4) for k in range(4)]
-    from_x = [x, 1 - x]
-
-    chunk = modes.shape[0] // branches
-    mine = lax.dynamic_slice_in_dim(modes, branch * chunk, chunk, 0)
-    mode_z = [mine]
-    for _ in range(3):
-        mode_z.append(over_z(mode_z[-1]))
-    mode_own = jnp.stack(mode_z)
-    mode_other = over_x(mode_own)
-    quarter = jnp.zeros((4, 2, chunk, mode_count), modes.dtype)
-    for k in range(4):
-        for j, source in enumerate((mode_own, mode_other)):
-            quarter = lax.dynamic_update_slice(
-                quarter, source[k][None, None], (from_z[k], from_x[j], 0, 0)
-            )
-    quarter = quarter.reshape(tiles, chunk, mode_count)
-    across = over_y(quarter)
-    half = jnp.stack(
-        [jnp.where(y == 0, quarter, across), jnp.where(y == 0, across, quarter)], axis=1
-    )
-    beside = over_core(half)
-    all_modes = jnp.stack(
-        [jnp.where(core == 0, half, beside), jnp.where(core == 0, beside, half)], axis=2
-    ).reshape(tiles * modes.shape[0], mode_count)
-
-    z1, x0 = lax.optimization_barrier((over_z(upper), over_x(upper)))
+    def over_y_of(block, first):
+        route = [
+            (b * tiles + t, (b ^ 2) * tiles + t)
+            for b in range(branches)
+            for t in range(tiles)
+            if stays((t, b)) != first
+        ]
+        return lax.ppermute(block, ("subtree", "tile"), route)
+
+    chunk = modes.shape[0] // 2
+    mine = lax.dynamic_slice_in_dim(modes, (branch & 1) * chunk, chunk, 0)
+    mine = jnp.concatenate([mine[: chunk // 2], mine[chunk // 2 :]], axis=1)
+    load = jnp.concatenate([upper, mine], axis=0)
+    mode_far = lax.ppermute(mine, "tile", ring_pairs(False))
+    z1, x0 = lax.optimization_barrier((over_z(load), over_x(load)))
     z2, x1 = lax.optimization_barrier((over_z(z1), over_x(z1)))
     z3, x2 = lax.optimization_barrier((over_z(z2), over_x(z2)))
     cut = depth // 2
-    x3_low, x3_high = over_x(z3[:cut]), over_z(x2[cut:])
-
-    def first_col(k, j):
-        return (from_z[k] * 2 + from_x[j]) * cols
-
-    def share(k, j, product):
-        return lax.dynamic_slice_in_dim(stiffness, first_col(k, j), cols, 1) - product
-
-    def times(left, right):
-        return jnp.dot(left, right, preferred_element_type=f32)
-
-    parts = [
-        [share(k, 0, times(lower, block)) for k, block in enumerate((upper, z1, z2, z3))],
-        [share(k, 1, times(lower, block)) for k, block in enumerate((x0, x1, x2))],
-    ]
-    parts[1].append(share(3, 1, times(lower[:, :cut], x3_low) + times(lower[:, cut:], x3_high)))
-
-    response = jnp.zeros((rows, mode_count), f32)
-    for j in range(2):
-        for k in range(4):
-            block_modes = lax.dynamic_slice_in_dim(all_modes, first_col(k, j), cols, 0)
-            response = response + jnp.dot(
-                parts[j][k],
-                block_modes.astype(f32),
-                precision=lax.Precision.HIGH,
-                preferred_element_type=f32,
-            )
-    reduced = jnp.einsum(
-        "rm,rc->mc",
-        modes.astype(f32),
-        response,
-        precision=lax.Precision.HIGH,
-        preferred_element_type=f32,
-    )
+    x3_low, x3_high = over_x(z3[:cut]), over_z(x2[cut:depth])
+
+    def spread(pieces):
+        near = jnp.stack(pieces)
+        return near, over_core(near)
+
+    early = spread([mine, z1[depth:], x0[depth:], mode_far])
+    middle = spread([z2[depth:], x1[depth:]])
+    late = spread([z3[depth:], x2[depth:]])
+    early_n, middle_n, late_n = 0, 1, 2
+    groups = [early, middle, late]
+
+    (p00,) = shares(place, stiffness, lower, [(0, 0, [load], None)])
+    p01, p10 = shares(place, stiffness, lower, [(0, 1, [z1], None), (1, 0, [x0], None)])
+    sent_a0, kept_a0, p11 = shares(
+        place, stiffness, lower, [(0, 2, [z2], p00), (1, 1, [x1], None)]
+    )
+    sent_b0, kept_b0, sent_a1, kept_a1 = shares(
+        place, stiffness, lower, [(0, 3, [z3], p01), (1, 2, [x2], p10)]
+    )
+    chip_a0 = kept_a0 + over_core(sent_a0)
+    came_a0 = over_y_of(to_wire(chip_a0), True)
+    chip_b0 = kept_b0 + over_core(sent_b0)
+    wire_b0 = to_wire(chip_b0)
+    came_b0 = over_y_of(wire_b0, False)
+    chip_a1 = kept_a1 + over_core(sent_a1)
+    wire_a1 = to_wire(chip_a1)
+    came_a1 = over_y_of(wire_a1, True)
+
+    pair_a0 = ((early_n, 0), (middle_n, 0), 0, sent_a0, kept_a0)
+    pair_b0 = ((early_n, 1), (late_n, 0), 1, sent_b0, kept_b0)
+    pair_a1 = ((early_n, 2), (late_n, 1), 0, sent_a1, kept_a1)
+    response = respond(place, [early, middle], [pair_a0], None, rows, mode_count)
+    response = respond(place, groups, [pair_b0, pair_a1], response, rows, mode_count)
+    x3_low, x3_high, came_a0, _, _ = lax.optimization_barrier(
+        (x3_low, x3_high, came_a0, wire_b0, wire_a1)
+    )
+    sent_b1, kept_b1 = shares(place, stiffness, lower, [(1, 3, [x3_low, x3_high], p11)])
+
     mode_rows = mode_count // tiles
     mode_cols = mode_count // branches
-    pieces = reduced.reshape(tiles, mode_rows, branches, mode_cols).transpose(2, 0, 1, 3)
-    pieces = pieces.reshape(branches * tiles, mode_rows, mode_cols)
-    pieces = lax.all_to_all(pieces, ("subtree", "tile"), 0, 0)
-    stiff_block = jnp.sum(pieces, axis=0)
-
-    final = []
-    keep_first = [from_z[k] % 2 == core for k in range(2)]
-    kept_z = [jnp.where(keep_first[k], from_z[k], from_z[k + 2]) for k in range(2)]
-    stays = kept_z[0] // 2 == y
-    for j in range(2):
-        both = []
-        for k in range(2):
-            kept = jnp.where(keep_first[k], parts[j][k], parts[j][k + 2])
-            sent = jnp.where(keep_first[k], parts[j][k + 2], parts[j][k])
-            both.append(kept + over_core(sent))
-        sent = jnp.where(stays, both[1], both[0])
-        arrived = over_y((sent * SHARE_SCALE).astype(jnp.float16))
-        final.append(
-            jnp.where(stays, both[0], both[1]) + arrived.astype(f32) * (1.0 / SHARE_SCALE)
-        )
-    schur_out = jnp.concatenate(
-        [jnp.where(x == 0, final[0], final[1]), jnp.where(x == 0, final[1], final[0])], axis=1
-    )
-
-    picked = jnp.take(all_modes, gyro_rows, axis=0, mode="clip").astype(f32)
+    pair_b1 = ((0, 0), (0, 1), 1, sent_b1, kept_b1)
+    last_two = (
+        jnp.stack([middle[0][1], early[0][3]]),
+        jnp.stack([middle[1][1], early[1][3]]),
+    )
+    pieces = reduce_modes(place, [last_two], pair_b1, response, modes, branches, tiles)
+    pieces = pieces.reshape(branches * tiles, mode_rows // 2, 2 * mode_cols)
+    pieces, gyro_rows = lax.optimization_barrier((pieces, gyro_rows))
+    summed = jnp.sum(lax.all_to_all(pieces, ("subtree", "tile"), 0, 0), axis=0)
+    stiff_block = jnp.concatenate([summed[:, :mode_cols], summed[:, mode_cols:]], axis=0)
+
+    chip_b1 = kept_b1 + over_core(sent_b1)
+    wire_b1, came_a1, came_b0 = lax.optimization_barrier((to_wire(chip_b1), came_a1, came_b0))
+    came_b1 = over_y_of(wire_b1, False)
+    here = stays((tile, branch))
+    left = tile & 1
+    first = jnp.where(here, chip_a0 + from_wire(came_a0), chip_b0 + from_wire(came_b0))
+    ready = jnp.concatenate([first, first], axis=1)
+    second = jnp.where(here, chip_a1 + from_wire(came_a1), chip_b1 + from_wire(came_b1))
+    schur_out = lax.dynamic_update_slice_in_dim(ready, second, (1 - left) * cols, 1)
+
+    row_tile, row_in = gyro_rows // modes.shape[0], gyro_rows % modes.shape[0]
+    turn = (gray(tile // 2) - gray(row_tile // 2)) & 3
+    index = ((row_tile ^ tile) & 1) * 4 + turn
+    block = pick(index, [0, 1, 4, 6, 2, 5, 7, 3])
+    half_row = row_in % chunk
+    table = jnp.concatenate([g[side] for side in range(2) for g in groups]).reshape(
+        -1, 2 * mode_count
+    )
+    line = (((row_in // chunk) ^ branch) & 1) * 8 + block
+    wide = jnp.take(
+        table, line * (chunk // 2) + half_row % (chunk // 2), axis=0, mode="clip"
+    )
+    picked = jnp.where(
+        (half_row < chunk // 2)[:, None], wide[:, :mode_count], wide[:, mode_count:]
+    ).astype(f32)
     gyro_block, spin_block = gyro_parts(
         picked,
         gyro_coupling,

time: 159 us -> 110 us (0.69)
  local copies, waits for them, and re-layouts: 42.7 us -> 13 us
  waiting for transfers between devices: 48.6 us -> 27.5 us
  matrix products: 22.9 us -> 3.08 us
  Pallas kernels: 0 us -> 17.1 us
  starting transfers between devices: 27.8 us -> 32.8 us
    dynamic_slice x9 -> x0, local copies, waits for them, and re-layouts: 24.2 us -> none  [share(): lax.dynamic_slice_in_dim(stiffness, first_col(k, j), cols, 1) - product]
    ppermute x10 -> x9, waiting for transfers between devices: 41.6 us -> 20.5 us  [the longest x4 16.9 us: over_z(): return lax.ppermute(block, 'tile', ring_pairs(True))]
    dot_general x18 -> x0, matrix products: 20.2 us -> none  [the longest x9 11.9 us: times(): return jnp.dot(left, right, preferred_element_type=f32)]
    pallas_call x0 -> x8, Pallas kernels: none -> 17.1 us  [call(): pl.pallas_call(body, out_shape=[jax.ShapeDtypeStruct(shape, dtype) for sh...]
    dynamic_update_slice x8 -> x0, local copies, waits for them, and re-layouts: 5.81 us -> none  [shards_ring(): lax.dynamic_update_slice(quarter, source[k][None, None], (from_z[k], from...]
    ppermute x10 -> x9, starting transfers between devices: 17.6 us -> 22.5 us  [the longest x4 11.2 us: over_y_of(): return lax.ppermute(block, ('subtree', 'tile'), route)]
    ppermute x5 -> x4, waiting for transfers between devices: 7.05 us -> 3.54 us  [over_x(): return lax.ppermute(block, 'tile', [(i, i ^ 1) for i in range(tiles)])]
    all_to_all x1, waiting for transfers between devices: 0.01 us -> 3.44 us  [shards_ring(): summed = jnp.sum(lax.all_to_all(pieces, ('subtree', 'tile'), 0, 0), axis=0)]
  transfers between devices with their start and end apart: 21 -> 21, of which waited for: 9 -> 8; matrix products, arithmetic and copies ran while one was open for 46% -> 20% of each run, Pallas kernels for 0% -> 16%
where the time goes in v3:
time: 110 us; the launch traced here: 109 us
  starting transfers between devices  32.8 us (30%)
  waiting for transfers between devices  27.5 us (25%)
  Pallas kernels  17.1 us (16%)
  other arithmetic  14.4 us (13%)
  local copies, waits for them, and re-layouts  13 us (12%)
  matrix products  3.08 us (3%)
  between operations  1.25 us (1%)
    pallas_call x8, Pallas kernels, call(): pl.pallas_call(body, out_shape=[jax.ShapeDtypeStruct(shape, dtype) for sh...  17.1 us
    ppermute x4, waiting for transfers between devices, over_z(): return lax.ppermute(block, 'tile', ring_pairs(True))  16.9 us
    ppermute x4, starting transfers between devices, over_y_of(): return lax.ppermute(block, ('subtree', 'tile'), route)  11.2 us
    ppermute x4, starting transfers between devices, over_z(): return lax.ppermute(block, 'tile', ring_pairs(True))  10.2 us
    unnamed x48, local copies, waits for them, and re-layouts  7.96 us
    ppermute x4, starting transfers between devices, over_x(): return lax.ppermute(block, 'tile', [(i, i ^ 1) for i in range(tiles)])  5.97 us
    convert_element_type x4, other arithmetic, to_wire(): return (value * SHARE_SCALE).astype(jnp.float16)  5.82 us
    gather x1, local copies, waits for them, and re-layouts, shards_ring(): jnp.take(table, line * (chunk // 2) + half_row % (chunk // 2), axis=0, mo...  3.85 us
  transfers between devices with their start and end apart: 21, of which 8 were waited for; matrix products, arithmetic and copies ran while one was open for 20% of the time, Pallas kernels for 16%

profile of v3, /device:TPU:0, one launch (start us, length us, event | category | flops | bytes accessed | tf_op | source)
XLA Modules:
  0.0 109.2 jit_solution(13264796101612634090)
XLA Ops:
  2.8 3.1 %collective-permute-start = (bf16[640,512]{1,0:T(8,128)(2,1)S(1)}, bf16[640,512]{1,0:T(8,128)(2,1)S(1)}, u32[]{:S(2)}, u32[]{:S(2)}) collective-permute-start(bf16[640,512]{1,0:T(8,128)(2,1)S(1)} %maximum_maximum_fusion.refs_0_), channel_id=1, source_target_pairs={{0,2},{1,3},{2,6},{3,7},{6,4},{7,5},{4,0},{5,1},{8,10},{9,11},{10,... | collective-permute-start | bytes 1966088 | tf_op jit(solution)/shard_map/ppermute | solution.py:363
  5.9 1.5 %collective-permute-start.1 = (bf16[640,512]{1,0:T(8,128)(2,1)S(1)}, bf16[640,512]{1,0:T(8,128)(2,1)S(1)}, u32[]{:S(2)}, u32[]{:S(2)}) collective-permute-start(bf16[640,512]{1,0:T(8,128)(2,1)S(1)} %maximum_maximum_fusion.refs_0_), channel_id=1, source_target_pairs={{0,1},{1,0},{2,3},{3,2},{4,5},{5,4},{6,7},{7,6},{8,9},{9,8},{10,11... | collective-permute-start | bytes 1966088 | tf_op jit(solution)/shard_map/ppermute | solution.py:366
  10.6 3.4 %copy-done = f32[1,512,4096]{2,1,0:T(8,128)S(1)} copy-done((f32[1,512,4096]{2,1,0:T(8,128)S(1)}, f32[1,512,4096]{2,1,0:T(8,128)}, u32[]{:S(2)}) %copy-start) | copy-done | bytes 8388632
  14.0 1.5 %shard_map.95.refs_1_ = f32[512,512]{1,0:T(8,128)S(1)} custom-call(s32[2]{0:T(128)S(1)} %pad_add_fusion.at, f32[512,4096]{1,0:T(8,128)S(1)} %bitcast.42, bf16[512,512]{1,0:T(8,128)(2,1)S(1)} %bitcast.49, bf16[640,512]{1,0:T(8,128)(2,1)S(1)} %maximum_maximum_fusion.refs_0_), custom_call_target="tpu_custom_call" | custom-call | flops 1048576 | bytes 262144 | tf_op jit(solution)/shard_map/pallas_call | solution.py:146
  15.5 6.2 %collective-permute-done.refs_0_ = bf16[640,512]{1,0:T(8,128)(2,1)S(1)} collective-permute-done((bf16[640,512]{1,0:T(8,128)(2,1)S(1)}, bf16[640,512]{1,0:T(8,128)(2,1)S(1)}, u32[]{:S(2)}, u32[]{:S(2)}) %collective-permute-start) | collective-permute-done | bytes 655392 | tf_op jit(solution)/shard_map/ppermute | solution.py:363
  21.7 2.2 %collective-permute-done.1.refs_1_ = bf16[640,512]{1,0:T(8,128)(2,1)S(1)} collective-permute-done((bf16[640,512]{1,0:T(8,128)(2,1)S(1)}, bf16[640,512]{1,0:T(8,128)(2,1)S(1)}, u32[]{:S(2)}, u32[]{:S(2)}) %collective-permute-start.1) | collective-permute-done | bytes 655392 | tf_op jit(solution)/shard_map/ppermute | solution.py:366
  23.9 3.5 %collective-permute-start.2 = (bf16[640,512]{1,0:T(8,128)(2,1)S(1)}, bf16[640,512]{1,0:T(8,128)(2,1)S(1)}, u32[]{:S(2)}, u32[]{:S(2)}) collective-permute-start(bf16[640,512]{1,0:T(8,128)(2,1)S(1)} %collective-permute-done.refs_0_), channel_id=1, source_target_pairs={{0,2},{1,3},{2,6},{3,7},{6,4},{7,5},{4,0},{5,1},{8,10},{9,11},{10,... | collective-permute-start | bytes 1966088 | tf_op jit(solution)/shard_map/ppermute | solution.py:363
  27.5 1.5 %collective-permute-start.3 = (bf16[640,512]{1,0:T(8,128)(2,1)S(1)}, bf16[640,512]{1,0:T(8,128)(2,1)S(1)}, u32[]{:S(2)}, u32[]{:S(2)}) collective-permute-start(bf16[640,512]{1,0:T(8,128)(2,1)S(1)} %collective-permute-done.refs_0_), channel_id=1, source_target_pairs={{0,1},{1,0},{2,3},{3,2},{4,5},{5,4},{6,7},{7,6},{8,9},{9,8},{10,11... | collective-permute-start | bytes 1966088 | tf_op jit(solution)/shard_map/ppermute | solution.py:366
  30.1 2.4 %shard_map.97 = (f32[512,512]{1,0:T(8,128)S(1)}, f32[512,512]{1,0:T(8,128)S(1)}) custom-call(s32[2]{0:T(128)S(1)} %pad_add_fusion.at, f32[512,4096]{1,0:T(8,128)S(1)} %bitcast.43, bf16[512,512]{1,0:T(8,128)(2,1)S(1)} %bitcast.50, bf16[640,512]{1,0:T(8,128)(2,1)S(1)} %collective-permute-done.refs_0_, bf16[640,512]{1,0:T(8,128)(2,1)S(1)} %collective-permute-done.1.refs_1_), custom_call_target="tpu_custom_call" | custom-call | flops 1048576 | bytes 262144 | tf_op jit(solution)/shard_map/pallas_call | solution.py:146
  33.5 6.2 %collective-permute-done.2.refs_0_ = bf16[640,512]{1,0:T(8,128)(2,1)S(1)} collective-permute-done((bf16[640,512]{1,0:T(8,128)(2,1)S(1)}, bf16[640,512]{1,0:T(8,128)(2,1)S(1)}, u32[]{:S(2)}, u32[]{:S(2)}) %collective-permute-start.2) | collective-permute-done | bytes 655392 | tf_op jit(solution)/shard_map/ppermute | solution.py:363
  40.4 2.1 %collective-permute-start.5 = (bf16[640,512]{1,0:T(8,128)(2,1)S(1)}, bf16[640,512]{1,0:T(8,128)(2,1)S(1)}, u32[]{:S(2)}, u32[]{:S(2)}) collective-permute-start(bf16[640,512]{1,0:T(8,128)(2,1)S(1)} %collective-permute-done.2.refs_0_), channel_id=1, source_target_pairs={{0,2},{1,3},{2,6},{3,7},{6,4},{7,5},{4,0},{5,1},{8,10},{9,11},{10,... | collective-permute-start | bytes 1966088 | tf_op jit(solution)/shard_map/ppermute | solution.py:363
  42.5 1.5 %collective-permute-start.6 = (bf16[640,512]{1,0:T(8,128)(2,1)S(1)}, bf16[640,512]{1,0:T(8,128)(2,1)S(1)}, u32[]{:S(2)}, u32[]{:S(2)}) collective-permute-start(bf16[640,512]{1,0:T(8,128)(2,1)S(1)} %collective-permute-done.2.refs_0_), channel_id=1, source_target_pairs={{0,1},{1,0},{2,3},{3,2},{4,5},{5,4},{6,7},{7,6},{8,9},{9,8},{10,11... | collective-permute-start | bytes 1966088 | tf_op jit(solution)/shard_map/ppermute | solution.py:366
  45.0 2.4 %shard_map.96 = (f32[512,512]{1,0:T(8,128)S(1)}, f32[512,512]{1,0:T(8,128)S(1)}, f32[512,512]{1,0:T(8,128)S(1)}) custom-call(s32[2]{0:T(128)S(1)} %pad_add_fusion.at, f32[512,4096]{1,0:T(8,128)S(1)} %bitcast.44, bf16[512,512]{1,0:T(8,128)(2,1)S(1)} %bitcast.51, bf16[640,512]{1,0:T(8,128)(2,1)S(1)} %collective-permute-done.2.refs_0_, ...), custom_call_target="tpu_custom_call" | custom-call | flops 1048576 | bytes 262144 | tf_op jit(solution)/shard_map/pallas_call | solution.py:146
  48.1 1.8 %shard_map.100.refs_10_ = f32[512,256]{1,0:T(8,128)S(1)} custom-call(s32[2]{0:T(128)S(1)} %pad_add_fusion.at, bf16[4,128,512]{2,1,0:T(8,128)(2,1)S(1)} %pad_maximum_fusion.1.refs_0_, bf16[4,128,512]{2,1,0:T(8,128)(2,1)S(1)} %collective-permute-done.18.refs_1_, bf16[2,128,512]{2,1,0:T(8,128)(2,1)S(1)} %get-tuple-element.63.refs_2_, ...), custom_call_target="tpu_custom_call" | custom-call | flops 1048576 | bytes 262144 | tf_op jit(solution)/shard_map/pallas_call | solution.py:146
  50.0 4.5 %collective-permute-done.5.refs_0_ = bf16[640,512]{1,0:T(8,128)(2,1)S(1)} collective-permute-done((bf16[640,512]{1,0:T(8,128)(2,1)S(1)}, bf16[640,512]{1,0:T(8,128)(2,1)S(1)}, u32[]{:S(2)}, u32[]{:S(2)}) %collective-permute-start.5) | collective-permute-done | bytes 655392 | tf_op jit(solution)/shard_map/ppermute | solution.py:363
  55.3 2.5 %shard_map.98 = (f32[512,512]{1,0:T(8,128)S(1)}, f32[512,512]{1,0:T(8,128)S(1)}, f32[512,512]{1,0:T(8,128)S(1)}, f32[512,512]{1,0:T(8,128)S(1)}) custom-call(s32[2]{0:T(128)S(1)} %pad_add_fusion.at, f32[512,4096]{1,0:T(8,128)S(1)} %bitcast.47, bf16[512,512]{1,0:T(8,128)(2,1)S(1)} %bitcast.52, bf16[640,512]{1,0:T(8,128)(2,1)S(1)} %collective-permute-done.5.refs_0_, ...), custom_call_target="tpu_custom_call" | custom-call | flops 1048576 | bytes 262144 | tf_op jit(solution)/shard_map/pallas_call | solution.py:146
  58.4 1.5 %collective-permute-start.7 = (bf16[256,512]{1,0:T(8,128)(2,1)S(1)}, bf16[256,512]{1,0:T(8,128)(2,1)S(1)}, u32[]{:S(2)}, u32[]{:S(2)}) collective-permute-start(bf16[256,512]{1,0:T(8,128)(2,1)S(1)} %slice.50), channel_id=1, source_target_pairs={{0,1},{1,0},{2,3},{3,2},{4,5},{5,4},{6,7},{7,6},{8,9},{9,8},{10,11... | collective-permute-start | bytes 786440 | tf_op jit(solution)/shard_map/ppermute | solution.py:366
  60.0 1.5 %collective-permute-start.8 = (bf16[256,512]{1,0:T(8,128)(2,1)S(1)}, bf16[256,512]{1,0:T(8,128)(2,1)S(1)}, u32[]{:S(2)}, u32[]{:S(2)}) collective-permute-start(bf16[256,512]{1,0:T(8,128)(2,1)S(1)} %slice.51), channel_id=1, source_target_pairs={{0,2},{1,3},{2,6},{3,7},{6,4},{7,5},{4,0},{5,1},{8,10},{9,11},{10,... | collective-permute-start | bytes 786440 | tf_op jit(solution)/shard_map/ppermute | solution.py:363
  61.5 2.4 %shard_map.101.refs_4_ = f32[512,256]{1,0:T(8,128)S(1)} custom-call(s32[2]{0:T(128)S(1)} %pad_add_fusion.at, bf16[4,128,512]{2,1,0:T(8,128)(2,1)S(1)} %pad_maximum_fusion.1.refs_0_, bf16[4,128,512]{2,1,0:T(8,128)(2,1)S(1)} %collective-permute-done.18.refs_1_, bf16[2,128,512]{2,1,0:T(8,128)(2,1)S(1)} %get-tuple-element.63.refs_2_, ...), custom_call_target="tpu_custom_call" | custom-call | flops 1048576 | bytes 262144 | tf_op jit(solution)/shard_map/pallas_call | solution.py:146
  64.0 1.5 %multiply_convert_fusion.3 = (f16[512,512]{1,0:T(8,128)(2,1)S(1)}, f32[512,512]{1,0:T(8,128)}) fusion(f32[512,512]{1,0:T(8,128)S(1)} %get-tuple-element.30.refs_5_, f32[512,512]{1,0:T(8,128)S(1)} %collective-permute-done.4), kind=kLoop, calls=%fused_computation.10 | loop fusion | flops 786432 | bytes 3670016 | tf_op jit(solution)/shard_map/convert_element_type | solution.py:323
  70.9 6.2 %collective-permute-start.14 = (f16[512,512]{1,0:T(8,128)(2,1)}, f16[512,512]{1,0:T(8,128)(2,1)}, u32[]{:S(2)}, u32[]{:S(2)}) collective-permute-start(f16[512,512]{1,0:T(8,128)(2,1)} %get-tuple-element.56), channel_id=1, source_target_pairs={{0,16},{1,17},{6,22},{7,23},{10,26},{11,27},{12,28},{13,29},{18,2}... | collective-permute-start | bytes 1572872 | tf_op jit(solution)/shard_map/ppermute | solution.py:381
  78.0 1.5 %shard_map.99 = (f32[512,512]{1,0:T(8,128)S(1)}, f32[512,512]{1,0:T(8,128)S(1)}) custom-call(s32[2]{0:T(128)S(1)} %pad_add_fusion.at, f32[512,4096]{1,0:T(8,128)S(1)} %bitcast.48, bf16[512,512]{1,0:T(8,128)(2,1)S(1)} %bitcast.53, bf16[256,512]{1,0:T(8,128)(2,1)S(1)} %collective-permute-done.7.refs_0_, bf16[256,512]{1,0:T(8,128)(2,1)S(1)} %collective-permute-done.8.refs_1_, ...), custom_call_target="tpu_custom_call" | custom-call | flops 1048576 | bytes 262144 | tf_op jit(solution)/shard_map/pallas_call | solution.py:146
  79.6 2.5 %shard_map.102 = f32[4,128,128]{2,1,0:T(8,128)} custom-call(s32[2]{0:T(128)S(1)} %pad_add_fusion.at, bf16[2,128,512]{2,1,0:T(8,128)(2,1)S(1)} %get-tuple-element.62.refs_0_, bf16[2,128,512]{2,1,0:T(8,128)(2,1)S(1)} %pad_maximum_fusion.4.refs_1_, f32[512,512]{1,0:T(8,128)S(1)} %get-tuple-element.46.refs_2_, f32[512,512]{1,0:T(8,128)S(1)} %get-tuple-element.45.refs_3_, ...), custom_call_target="tpu_custom_call" | custom-call | flops 1048576 | bytes 262144 | tf_op jit(solution)/shard_map/pallas_call | solution.py:146
  82.1 2.9 %all-to-all-start = ((f32[32,16,128]{2,1,0:T(8,128)}), f32[32,16,128]{2,1,0:T(8,128)S(1)}, u32[]{:S(2)}, u32[]{:S(2)}) async-start(f32[32,16,128]{2,1,0:T(8,128)} %bitcast.13), calls=%async_computation | async-start | bytes 524288 | tf_op jit(solution)/shard_map/all_to_all | solution.py:441
  85.1 3.9 %gather_fusion = bf16[512,512]{1,0:T(8,128)(2,1)S(1)} fusion(bf16[2048,512]{1,0:T(8,128)(2,1)} %bitcast.54, s32[1024]{0:T(1024)S(1)} %pad_clamp_fusion), kind=kCustom, calls=%fused_computation | custom fusion | bytes 1050624 | tf_op jit(solution)/shard_map/jit(_take)/gather | solution.py:463
  89.6 2.2 %fusion.1 = f32[512,64]{1,0:T(8,128)S(1)} fusion(f32[512,512]{1,0:T(8,128)} %param.13, f32[512,512]{0,1:T(8,128)} %copy.10, bf16[512,256]{1,0:T(8,128)(2,1)S(1)} %slice_select_fusion, s32[]{:T(128)S(6)} %select_n.102), kind=kOutput, calls=%fused_computation.4 | convolution fusion | flops 201850880 | bytes 2359300 | tf_op jit(solution)/shard_map/dot_general | solution.py:35
  92.2 3.4 %all-to-all-done = f32[32,16,128]{2,1,0:T(8,128)S(1)} async-done(((f32[32,16,128]{2,1,0:T(8,128)}), f32[32,16,128]{2,1,0:T(8,128)S(1)}, u32[]{:S(2)}, u32[]{:S(2)}) %all-to-all-start) | async-done | bytes 262176 | tf_op jit(solution)/shard_map/all_to_all | solution.py:441
  95.8 1.5 %multiply_convert_fusion = (f16[512,512]{1,0:T(8,128)(2,1)S(1)}, f32[512,512]{1,0:T(8,128)S(1)}) fusion(f32[512,512]{1,0:T(8,128)S(1)} %get-tuple-element.45.refs_3_, f32[512,512]{1,0:T(8,128)} %collective-permute-done.12), kind=kLoop, calls=%fused_computation.7 | loop fusion | flops 786432 | bytes 3670016 | tf_op jit(solution)/shard_map/convert_element_type | solution.py:323
  97.3 2.5 %collective-permute-start.15 = (f16[512,512]{1,0:T(8,128)(2,1)S(1)}, f16[512,512]{1,0:T(8,128)(2,1)S(1)}, u32[]{:S(2)}, u32[]{:S(2)}) collective-permute-start(f16[512,512]{1,0:T(8,128)(2,1)S(1)} %get-tuple-element.49), channel_id=1, source_target_pairs={{0,16},{1,17},{6,22},{7,23},{10,26},{11,27},{12,28},{13,29},{18,2}... | collective-permute-start | bytes 1572872 | tf_op jit(solution)/shard_map/ppermute | solution.py:381
  100.5 2.0 %add_select_fusion = f32[512,512]{1,0:T(8,128)S(1)} fusion(f32[512,512]{1,0:T(8,128)} %get-tuple-element.57, f16[512,512]{1,0:T(8,128)(2,1)} %collective-permute-done.14, f32[512,512]{1,0:T(8,128)} %get-tuple-element.59, f16[512,512]{1,0:T(8,128)(2,1)S(1)} %copy-done.12, pred[]{:T(512)S(6)} %eq.34), kind=kLoop, calls=%fused_computation.6 | loop fusion | flops 1835008 | bytes 4194305 | tf_op jit(solution)/shard_map/jit(_where)/select_n | solution.py:449
  102.8 3.6 %collective-permute-done.15 = f16[512,512]{1,0:T(8,128)(2,1)S(1)} collective-permute-done((f16[512,512]{1,0:T(8,128)(2,1)S(1)}, f16[512,512]{1,0:T(8,128)(2,1)S(1)}, u32[]{:S(2)}, u32[]{:S(2)}) %collective-permute-start.15) | collective-permute-done | bytes 524320 | tf_op jit(solution)/shard_map/ppermute | solution.py:381
  106.4 1.5 %select_dynamic-update-slice_fusion = f32[512,1024]{1,0:T(8,128)S(1)} fusion(f32[512,1024]{1,0:T(8,128)S(1)} %pad_maximum_fusion, s32[]{:T(128)S(6)} %select_n.85, f32[512,512]{1,0:T(8,128)S(1)} %get-tuple-element.53, f16[512,512]{1,0:T(8,128)(2,1)S(1)} %collective-permute-done.15, f32[512,512]{1,0:T(8,128)S(1)} %copy-done.4, ...), kind=kLoop, calls=%fused_computation.5 | loop fusion | flops 1835008 | bytes 4194309 | tf_op jit(solution)/shard_map/dynamic_update_slice | solution.py:452
  (104 shorter events, 21.1 us)
Async XLA Ops:
  0.6 8.5 %copy-start.5 = (f32[512,512]{1,0:T(8,128)S(1)}, f32[512,512]{1,0:T(8,128)}, u32[]{:S(2)}) copy-start(f32[512,512]{1,0:T(8,128)} %param.13) | copy-start | bytes 3145732
  0.6 9.9 %copy-start.1 = (bf16[1,512,512]{2,1,0:T(8,128)(2,1)S(1)}, bf16[1,512,512]{2,1,0:T(8,128)(2,1)}, u32[]{:S(2)}) copy-start(bf16[1,512,512]{2,1,0:T(8,128)(2,1)} %param.9) | copy-start | bytes 1572868
  1.7 5.7 %copy-start.7 = (bf16[128,256]{1,0:T(8,128)(2,1)}, bf16[128,256]{1,0:T(8,128)(2,1)S(1)}, u32[]{:S(2)}) copy-start(bf16[128,256]{1,0:T(8,128)(2,1)S(1)} %get-tuple-element.60) | copy-start | bytes 196612
  1.7 6.4 %copy-start.9 = (bf16[128,256]{1,0:T(8,128)(2,1)}, bf16[128,256]{1,0:T(8,128)(2,1)S(1)}, u32[]{:S(2)}) copy-start(bf16[128,256]{1,0:T(8,128)(2,1)S(1)} %get-tuple-element.61) | copy-start | bytes 196612
  2.8 18.9 %collective-permute-start = (bf16[640,512]{1,0:T(8,128)(2,1)S(1)}, bf16[640,512]{1,0:T(8,128)(2,1)S(1)}, u32[]{:S(2)}, u32[]{:S(2)}) collective-permute-start(bf16[640,512]{1,0:T(8,128)(2,1)S(1)} %maximum_maximum_fusion.refs_0_), channel_id=1, source_target_pairs={{0,2},{1,3},{2,6},{3,7},{6,4},{7,5},{4,0},{5,1},{8,10},{9,11},{10,... | collective-permute-start | bytes 1966088 | tf_op jit(solution)/shard_map/ppermute | solution.py:363
  5.9 18.0 %collective-permute-start.1 = (bf16[640,512]{1,0:T(8,128)(2,1)S(1)}, bf16[640,512]{1,0:T(8,128)(2,1)S(1)}, u32[]{:S(2)}, u32[]{:S(2)}) collective-permute-start(bf16[640,512]{1,0:T(8,128)(2,1)S(1)} %maximum_maximum_fusion.refs_0_), channel_id=1, source_target_pairs={{0,1},{1,0},{2,3},{3,2},{4,5},{5,4},{6,7},{7,6},{8,9},{9,8},{10,11... | collective-permute-start | bytes 1966088 | tf_op jit(solution)/shard_map/ppermute | solution.py:366
  8.1 20.9 %collective-permute-start.16 = (bf16[128,512]{1,0:T(8,128)(2,1)}, bf16[128,512]{1,0:T(8,128)(2,1)}, u32[]{:S(2)}, u32[]{:S(2)}) collective-permute-start(bf16[128,512]{1,0:T(8,128)(2,1)} %get-tuple-element.65), channel_id=1, source_target_pairs={{3,0},{2,1},{7,2},{6,3},{5,6},{4,7},{1,4},{0,5},{11,8},{10,9},{15,... | collective-permute-start | bytes 393224 | tf_op jit(solution)/shard_map/ppermute | solution.py:387
  14.0 15.0 %copy-start.13 = (bf16[1,128,512]{2,1,0:T(8,128)(2,1)S(1)}, bf16[1,128,512]{2,1,0:T(8,128)(2,1)}, u32[]{:S(2)}) copy-start(bf16[1,128,512]{2,1,0:T(8,128)(2,1)} %get-tuple-element.64) | copy-start | bytes 393220
  23.9 15.7 %collective-permute-start.2 = (bf16[640,512]{1,0:T(8,128)(2,1)S(1)}, bf16[640,512]{1,0:T(8,128)(2,1)S(1)}, u32[]{:S(2)}, u32[]{:S(2)}) collective-permute-start(bf16[640,512]{1,0:T(8,128)(2,1)S(1)} %collective-permute-done.refs_0_), channel_id=1, source_target_pairs={{0,2},{1,3},{2,6},{3,7},{6,4},{7,5},{4,0},{5,1},{8,10},{9,11},{10,... | collective-permute-start | bytes 1966088 | tf_op jit(solution)/shard_map/ppermute | solution.py:363
  27.5 12.9 %collective-permute-start.3 = (bf16[640,512]{1,0:T(8,128)(2,1)S(1)}, bf16[640,512]{1,0:T(8,128)(2,1)S(1)}, u32[]{:S(2)}, u32[]{:S(2)}) collective-permute-start(bf16[640,512]{1,0:T(8,128)(2,1)S(1)} %collective-permute-done.refs_0_), channel_id=1, source_target_pairs={{0,1},{1,0},{2,3},{3,2},{4,5},{5,4},{6,7},{7,6},{8,9},{9,8},{10,11... | collective-permute-start | bytes 1966088 | tf_op jit(solution)/shard_map/ppermute | solution.py:366
  30.0 3.5 %collective-permute-start.18 = (bf16[4,128,512]{2,1,0:T(8,128)(2,1)S(1)}, bf16[4,128,512]{2,1,0:T(8,128)(2,1)S(1)}, u32[]{:S(2)}, u32[]{:S(2)}) collective-permute-start(bf16[4,128,512]{2,1,0:T(8,128)(2,1)S(1)} %pad_maximum_fusion.1.refs_0_), channel_id=1, source_target_pairs={{0,8},{8,0},{16,24},{24,16},{1,9},{9,1},{17,25},{25,17},{2,10},{10... | collective-permute-start | bytes 1572872 | tf_op jit(solution)/shard_map/ppermute | solution.py:372
  40.4 14.1 %collective-permute-start.5 = (bf16[640,512]{1,0:T(8,128)(2,1)S(1)}, bf16[640,512]{1,0:T(8,128)(2,1)S(1)}, u32[]{:S(2)}, u32[]{:S(2)}) collective-permute-start(bf16[640,512]{1,0:T(8,128)(2,1)S(1)} %collective-permute-done.2.refs_0_), channel_id=1, source_target_pairs={{0,2},{1,3},{2,6},{3,7},{6,4},{7,5},{4,0},{5,1},{8,10},{9,11},{10,... | collective-permute-start | bytes 1966088 | tf_op jit(solution)/shard_map/ppermute | solution.py:363
  42.5 12.6 %collective-permute-start.6 = (bf16[640,512]{1,0:T(8,128)(2,1)S(1)}, bf16[640,512]{1,0:T(8,128)(2,1)S(1)}, u32[]{:S(2)}, u32[]{:S(2)}) collective-permute-start(bf16[640,512]{1,0:T(8,128)(2,1)S(1)} %collective-permute-done.2.refs_0_), channel_id=1, source_target_pairs={{0,1},{1,0},{2,3},{3,2},{4,5},{5,4},{6,7},{7,6},{8,9},{9,8},{10,11... | collective-permute-start | bytes 1966088 | tf_op jit(solution)/shard_map/ppermute | solution.py:366
  44.9 10.3 %slice-start = ((s8[8388608]{0:T(1024)(128)(4,1)}), s8[4194304]{0:T(1024)(128)(4,1)S(1)}, s32[]{:S(2)}) async-start(s8[8388608]{0:T(1024)(128)(4,1)} %bitcast.45), calls=%async_computation.1 | async-start | bytes 8388608
  45.0 10.3 %slice-start.1 = ((s8[8388608]{0:T(1024)(128)(4,1)}), s8[4194304]{0:T(1024)(128)(4,1)S(1)}, s32[]{:S(2)}) async-start(s8[8388608]{0:T(1024)(128)(4,1)} %bitcast.45), calls=%async_computation.2 | async-start | bytes 8388608
  45.0 3.1 %collective-permute-start.17 = (bf16[2,128,512]{2,1,0:T(8,128)(2,1)S(1)}, bf16[2,128,512]{2,1,0:T(8,128)(2,1)S(1)}, u32[]{:S(2)}, u32[]{:S(2)}) collective-permute-start(bf16[2,128,512]{2,1,0:T(8,128)(2,1)S(1)} %get-tuple-element.63.refs_2_), channel_id=1, source_target_pairs={{0,8},{8,0},{16,24},{24,16},{1,9},{9,1},{17,25},{25,17},{2,10},{10... | collective-permute-start | bytes 786440 | tf_op jit(solution)/shard_map/ppermute | solution.py:372
  47.5 16.5 %collective-permute-start.4 = (f32[512,512]{1,0:T(8,128)S(1)}, f32[512,512]{1,0:T(8,128)S(1)}, u32[]{:S(2)}, u32[]{:S(2)}) collective-permute-start(f32[512,512]{1,0:T(8,128)S(1)} %get-tuple-element.31.refs_4_), channel_id=1, source_target_pairs={{0,8},{8,0},{16,24},{24,16},{1,9},{9,1},{17,25},{25,17},{2,10},{10... | collective-permute-start | bytes 3145736 | tf_op jit(solution)/shard_map/ppermute | solution.py:372
  55.2 4.8 %collective-permute-start.19 = (bf16[2,128,512]{2,1,0:T(8,128)(2,1)S(1)}, bf16[2,128,512]{2,1,0:T(8,128)(2,1)S(1)}, u32[]{:S(2)}, u32[]{:S(2)}) collective-permute-start(bf16[2,128,512]{2,1,0:T(8,128)(2,1)S(1)} %pad_maximum_fusion.5.refs_4_), channel_id=1, source_target_pairs={{0,8},{8,0},{16,24},{24,16},{1,9},{9,1},{17,25},{25,17},{2,10},{10... | collective-permute-start | bytes 786440 | tf_op jit(solution)/shard_map/ppermute | solution.py:372
  57.7 9.0 %collective-permute-start.11 = (f32[512,512]{1,0:T(8,128)S(1)}, f32[512,512]{1,0:T(8,128)S(1)}, u32[]{:S(2)}, u32[]{:S(2)}) collective-permute-start(f32[512,512]{1,0:T(8,128)S(1)} %get-tuple-element.40.refs_8_), channel_id=1, source_target_pairs={{0,8},{8,0},{16,24},{24,16},{1,9},{9,1},{17,25},{25,17},{2,10},{10... | collective-permute-start | bytes 3145736 | tf_op jit(solution)/shard_map/ppermute | solution.py:372
  58.3 11.2 %collective-permute-start.10 = (f32[512,512]{1,0:T(8,128)S(1)}, f32[512,512]{1,0:T(8,128)S(1)}, u32[]{:S(2)}, u32[]{:S(2)}) collective-permute-start(f32[512,512]{1,0:T(8,128)S(1)} %get-tuple-element.38.refs_6_), channel_id=1, source_target_pairs={{0,8},{8,0},{16,24},{24,16},{1,9},{9,1},{17,25},{25,17},{2,10},{10... | collective-permute-start | bytes 3145736 | tf_op jit(solution)/shard_map/ppermute | solution.py:372
  58.4 18.8 %collective-permute-start.7 = (bf16[256,512]{1,0:T(8,128)(2,1)S(1)}, bf16[256,512]{1,0:T(8,128)(2,1)S(1)}, u32[]{:S(2)}, u32[]{:S(2)}) collective-permute-start(bf16[256,512]{1,0:T(8,128)(2,1)S(1)} %slice.50), channel_id=1, source_target_pairs={{0,1},{1,0},{2,3},{3,2},{4,5},{5,4},{6,7},{7,6},{8,9},{9,8},{10,11... | collective-permute-start | bytes 786440 | tf_op jit(solution)/shard_map/ppermute | solution.py:366
  60.0 17.1 %collective-permute-start.8 = (bf16[256,512]{1,0:T(8,128)(2,1)S(1)}, bf16[256,512]{1,0:T(8,128)(2,1)S(1)}, u32[]{:S(2)}, u32[]{:S(2)}) collective-permute-start(bf16[256,512]{1,0:T(8,128)(2,1)S(1)} %slice.51), channel_id=1, source_target_pairs={{0,2},{1,3},{2,6},{3,7},{6,4},{7,5},{4,0},{5,1},{8,10},{9,11},{10,... | collective-permute-start | bytes 786440 | tf_op jit(solution)/shard_map/ppermute | solution.py:363
  64.0 4.2 %copy-start.3 = (bf16[16,128,512]{2,1,0:T(8,128)(2,1)}, bf16[16,128,512]{2,1,0:T(8,128)(2,1)S(1)}, u32[]{:S(2)}) copy-start(bf16[16,128,512]{2,1,0:T(8,128)(2,1)S(1)} %constant_dynamic-update-slice_fusion) | copy-start | bytes 6291460
  65.4 11.7 %collective-permute-start.9 = (f16[512,512]{1,0:T(8,128)(2,1)S(1)}, f16[512,512]{1,0:T(8,128)(2,1)S(1)}, u32[]{:S(2)}, u32[]{:S(2)}) collective-permute-start(f16[512,512]{1,0:T(8,128)(2,1)S(1)} %get-tuple-element.58), channel_id=1, source_target_pairs={{2,18},{3,19},{4,20},{5,21},{8,24},{9,25},{14,30},{15,31},{16,0},{... | collective-permute-start | bytes 1572872 | tf_op jit(solution)/shard_map/ppermute | solution.py:381
  68.2 29.1 %collective-permute-start.13 = (f16[512,512]{1,0:T(8,128)(2,1)}, f16[512,512]{1,0:T(8,128)(2,1)}, u32[]{:S(2)}, u32[]{:S(2)}) collective-permute-start(f16[512,512]{1,0:T(8,128)(2,1)} %get-tuple-element.54), channel_id=1, source_target_pairs={{2,18},{3,19},{4,20},{5,21},{8,24},{9,25},{14,30},{15,31},{16,0},{... | collective-permute-start | bytes 1572872 | tf_op jit(solution)/shard_map/ppermute | solution.py:381
  70.9 26.4 %collective-permute-start.14 = (f16[512,512]{1,0:T(8,128)(2,1)}, f16[512,512]{1,0:T(8,128)(2,1)}, u32[]{:S(2)}, u32[]{:S(2)}) collective-permute-start(f16[512,512]{1,0:T(8,128)(2,1)} %get-tuple-element.56), channel_id=1, source_target_pairs={{0,16},{1,17},{6,22},{7,23},{10,26},{11,27},{12,28},{13,29},{18,2}... | collective-permute-start | bytes 1572872 | tf_op jit(solution)/shard_map/ppermute | solution.py:381
  79.5 16.3 %collective-permute-start.12 = (f32[512,512]{1,0:T(8,128)S(1)}, f32[512,512]{1,0:T(8,128)}, u32[]{:S(2)}, u32[]{:S(2)}) collective-permute-start(f32[512,512]{1,0:T(8,128)S(1)} %get-tuple-element.46.refs_2_), channel_id=1, source_target_pairs={{0,8},{8,0},{16,24},{24,16},{1,9},{9,1},{17,25},{25,17},{2,10},{10... | collective-permute-start | bytes 3145736 | tf_op jit(solution)/shard_map/ppermute | solution.py:372
  79.6 5.4 %copy-start.14 = (s32[512]{0:T(512)S(1)}, s32[512]{0:T(512)}, u32[]{:S(2)}) copy-start(s32[512]{0:T(512)} %param.12) | copy-start | bytes 6148
  82.1 13.5 %all-to-all-start = ((f32[32,16,128]{2,1,0:T(8,128)}), f32[32,16,128]{2,1,0:T(8,128)S(1)}, u32[]{:S(2)}, u32[]{:S(2)}) async-start(f32[32,16,128]{2,1,0:T(8,128)} %bitcast.13), calls=%async_computation | async-start | bytes 524288 | tf_op jit(solution)/shard_map/all_to_all | solution.py:441
  85.1 4.0 %copy-start.15 = (f32[512]{0:T(512)S(1)}, f32[512]{0:T(512)}, u32[]{:S(2)}) copy-start(f32[512]{0:T(512)} %param.14) | copy-start | bytes 6148
  92.2 8.3 %copy-start.12 = (f16[512,512]{1,0:T(8,128)(2,1)S(1)}, f16[512,512]{1,0:T(8,128)(2,1)}, u32[]{:S(2)}) copy-start(f16[512,512]{1,0:T(8,128)(2,1)} %copy-done.11) | copy-start | bytes 1572868
  97.3 9.1 %collective-permute-start.15 = (f16[512,512]{1,0:T(8,128)(2,1)S(1)}, f16[512,512]{1,0:T(8,128)(2,1)S(1)}, u32[]{:S(2)}, u32[]{:S(2)}) collective-permute-start(f16[512,512]{1,0:T(8,128)(2,1)S(1)} %get-tuple-element.49), channel_id=1, source_target_pairs={{0,16},{1,17},{6,22},{7,23},{10,26},{11,27},{12,28},{13,29},{18,2}... | collective-permute-start | bytes 1572872 | tf_op jit(solution)/shard_map/ppermute | solution.py:381
  (8 other events, 15.7 us)

commit v4 on v3

--- a/solution.py
+++ b/solution.py
@@ -150,7 +150,7 @@
         out_specs=[IN_VMEM] * len(outs),
         scratch_shapes=scratch,
         compiler_params=pltpu.CompilerParams(vmem_limit_bytes=GRANT),
-        cost_estimate=pl.CostEstimate(flops=1 << 20, bytes_accessed=1 << 18, transcendentals=0),
+        cost_estimate=pl.CostEstimate(flops=1 << 31, bytes_accessed=1 << 20, transcendentals=0),
     )(*operands)
 
 

time: 110 us -> 109 us (level)
    unnamed x48 -> x44, local copies, waits for them, and re-layouts: 7.96 us -> 7.1 us
where the time goes in v4:
time: 109 us; the launch traced here: 108 us
  starting transfers between devices  32.7 us (30%)
  waiting for transfers between devices  26.7 us (24%)
  Pallas kernels  17.2 us (16%)
  other arithmetic  15.1 us (14%)
  local copies, waits for them, and re-layouts  12.1 us (11%)
  matrix products  3.08 us (3%)
  between operations  1.26 us (1%)
    pallas_call x8, Pallas kernels, call(): pl.pallas_call(body, out_shape=[jax.ShapeDtypeStruct(shape, dtype) for sh...  17.2 us
    ppermute x4, waiting for transfers between devices, over_z(): return lax.ppermute(block, 'tile', ring_pairs(True))  16.1 us
    ppermute x4, starting transfers between devices, over_y_of(): return lax.ppermute(block, ('subtree', 'tile'), route)  11.2 us
    ppermute x4, starting transfers between devices, over_z(): return lax.ppermute(block, 'tile', ring_pairs(True))  10.2 us
    unnamed x44, local copies, waits for them, and re-layouts  7.1 us
    ppermute x4, starting transfers between devices, over_x(): return lax.ppermute(block, 'tile', [(i, i ^ 1) for i in range(tiles)])  5.97 us
    convert_element_type x4, other arithmetic, to_wire(): return (value * SHARE_SCALE).astype(jnp.float16)  5.59 us
    gather x1, local copies, waits for them, and re-layouts, shards_ring(): jnp.take(table, line * (chunk // 2) + half_row % (chunk // 2), axis=0, mo...  3.85 us
  transfers between devices with their start and end apart: 21, of which 8 were waited for; matrix products, arithmetic and copies ran while one was open for 20% of the time, Pallas kernels for 16%

profile of v4, /device:TPU:0, one launch (start us, length us, event | category | flops | bytes accessed | tf_op | source)
XLA Modules:
  0.0 108.1 jit_solution(4099961659835507994)
XLA Ops:
  2.8 3.1 %collective-permute-start = (bf16[640,512]{1,0:T(8,128)(2,1)S(1)}, bf16[640,512]{1,0:T(8,128)(2,1)S(1)}, u32[]{:S(2)}, u32[]{:S(2)}) collective-permute-start(bf16[640,512]{1,0:T(8,128)(2,1)S(1)} %maximum_maximum_fusion.refs_0_), channel_id=1, source_target_pairs={{0,2},{1,3},{2,6},{3,7},{6,4},{7,5},{4,0},{5,1},{8,10},{9,11},{10,... | collective-permute-start | bytes 1966088 | tf_op jit(solution)/shard_map/ppermute | solution.py:363
  5.9 1.5 %collective-permute-start.1 = (bf16[640,512]{1,0:T(8,128)(2,1)S(1)}, bf16[640,512]{1,0:T(8,128)(2,1)S(1)}, u32[]{:S(2)}, u32[]{:S(2)}) collective-permute-start(bf16[640,512]{1,0:T(8,128)(2,1)S(1)} %maximum_maximum_fusion.refs_0_), channel_id=1, source_target_pairs={{0,1},{1,0},{2,3},{3,2},{4,5},{5,4},{6,7},{7,6},{8,9},{9,8},{10,11... | collective-permute-start | bytes 1966088 | tf_op jit(solution)/shard_map/ppermute | solution.py:366
  11.4 3.4 %copy-done = f32[1,512,4096]{2,1,0:T(8,128)S(1)} copy-done((f32[1,512,4096]{2,1,0:T(8,128)S(1)}, f32[1,512,4096]{2,1,0:T(8,128)}, u32[]{:S(2)}) %copy-start) | copy-done | bytes 8388632
  14.8 1.5 %shard_map.95.refs_1_ = f32[512,512]{1,0:T(8,128)S(1)} custom-call(s32[2]{0:T(128)S(1)} %pad_add_fusion.at, f32[512,4096]{1,0:T(8,128)S(1)} %bitcast.42, bf16[512,512]{1,0:T(8,128)(2,1)S(1)} %bitcast.49, bf16[640,512]{1,0:T(8,128)(2,1)S(1)} %maximum_maximum_fusion.refs_0_), custom_call_target="tpu_custom_call" | custom-call | flops 2147483648 | bytes 1048576 | tf_op jit(solution)/shard_map/pallas_call | solution.py:146
  16.3 5.4 %collective-permute-done.refs_0_ = bf16[640,512]{1,0:T(8,128)(2,1)S(1)} collective-permute-done((bf16[640,512]{1,0:T(8,128)(2,1)S(1)}, bf16[640,512]{1,0:T(8,128)(2,1)S(1)}, u32[]{:S(2)}, u32[]{:S(2)}) %collective-permute-start) | collective-permute-done | bytes 655392 | tf_op jit(solution)/shard_map/ppermute | solution.py:363
  21.7 2.2 %collective-permute-done.1.refs_1_ = bf16[640,512]{1,0:T(8,128)(2,1)S(1)} collective-permute-done((bf16[640,512]{1,0:T(8,128)(2,1)S(1)}, bf16[640,512]{1,0:T(8,128)(2,1)S(1)}, u32[]{:S(2)}, u32[]{:S(2)}) %collective-permute-start.1) | collective-permute-done | bytes 655392 | tf_op jit(solution)/shard_map/ppermute | solution.py:366
  23.9 3.5 %collective-permute-start.2 = (bf16[640,512]{1,0:T(8,128)(2,1)S(1)}, bf16[640,512]{1,0:T(8,128)(2,1)S(1)}, u32[]{:S(2)}, u32[]{:S(2)}) collective-permute-start(bf16[640,512]{1,0:T(8,128)(2,1)S(1)} %collective-permute-done.refs_0_), channel_id=1, source_target_pairs={{0,2},{1,3},{2,6},{3,7},{6,4},{7,5},{4,0},{5,1},{8,10},{9,11},{10,... | collective-permute-start | bytes 1966088 | tf_op jit(solution)/shard_map/ppermute | solution.py:363
  27.5 1.5 %collective-permute-start.3 = (bf16[640,512]{1,0:T(8,128)(2,1)S(1)}, bf16[640,512]{1,0:T(8,128)(2,1)S(1)}, u32[]{:S(2)}, u32[]{:S(2)}) collective-permute-start(bf16[640,512]{1,0:T(8,128)(2,1)S(1)} %collective-permute-done.refs_0_), channel_id=1, source_target_pairs={{0,1},{1,0},{2,3},{3,2},{4,5},{5,4},{6,7},{7,6},{8,9},{9,8},{10,11... | collective-permute-start | bytes 1966088 | tf_op jit(solution)/shard_map/ppermute | solution.py:366
  30.1 2.4 %shard_map.97 = (f32[512,512]{1,0:T(8,128)S(1)}, f32[512,512]{1,0:T(8,128)S(1)}) custom-call(s32[2]{0:T(128)S(1)} %pad_add_fusion.at, f32[512,4096]{1,0:T(8,128)S(1)} %bitcast.43, bf16[512,512]{1,0:T(8,128)(2,1)S(1)} %bitcast.50, bf16[640,512]{1,0:T(8,128)(2,1)S(1)} %collective-permute-done.refs_0_, bf16[640,512]{1,0:T(8,128)(2,1)S(1)} %collective-permute-done.1.refs_1_), custom_call_target="tpu_custom_call" | custom-call | flops 2147483648 | bytes 1048576 | tf_op jit(solution)/shard_map/pallas_call | solution.py:146
  33.5 6.2 %collective-permute-done.2.refs_0_ = bf16[640,512]{1,0:T(8,128)(2,1)S(1)} collective-permute-done((bf16[640,512]{1,0:T(8,128)(2,1)S(1)}, bf16[640,512]{1,0:T(8,128)(2,1)S(1)}, u32[]{:S(2)}, u32[]{:S(2)}) %collective-permute-start.2) | collective-permute-done | bytes 655392 | tf_op jit(solution)/shard_map/ppermute | solution.py:363
  40.4 2.1 %collective-permute-start.5 = (bf16[640,512]{1,0:T(8,128)(2,1)S(1)}, bf16[640,512]{1,0:T(8,128)(2,1)S(1)}, u32[]{:S(2)}, u32[]{:S(2)}) collective-permute-start(bf16[640,512]{1,0:T(8,128)(2,1)S(1)} %collective-permute-done.2.refs_0_), channel_id=1, source_target_pairs={{0,2},{1,3},{2,6},{3,7},{6,4},{7,5},{4,0},{5,1},{8,10},{9,11},{10,... | collective-permute-start | bytes 1966088 | tf_op jit(solution)/shard_map/ppermute | solution.py:363
  42.5 1.5 %collective-permute-start.6 = (bf16[640,512]{1,0:T(8,128)(2,1)S(1)}, bf16[640,512]{1,0:T(8,128)(2,1)S(1)}, u32[]{:S(2)}, u32[]{:S(2)}) collective-permute-start(bf16[640,512]{1,0:T(8,128)(2,1)S(1)} %collective-permute-done.2.refs_0_), channel_id=1, source_target_pairs={{0,1},{1,0},{2,3},{3,2},{4,5},{5,4},{6,7},{7,6},{8,9},{9,8},{10,11... | collective-permute-start | bytes 1966088 | tf_op jit(solution)/shard_map/ppermute | solution.py:366
  45.0 2.4 %shard_map.96 = (f32[512,512]{1,0:T(8,128)S(1)}, f32[512,512]{1,0:T(8,128)S(1)}, f32[512,512]{1,0:T(8,128)S(1)}) custom-call(s32[2]{0:T(128)S(1)} %pad_add_fusion.at, f32[512,4096]{1,0:T(8,128)S(1)} %bitcast.44, bf16[512,512]{1,0:T(8,128)(2,1)S(1)} %bitcast.51, bf16[640,512]{1,0:T(8,128)(2,1)S(1)} %collective-permute-done.2.refs_0_, ...), custom_call_target="tpu_custom_call" | custom-call | flops 2147483648 | bytes 1048576 | tf_op jit(solution)/shard_map/pallas_call | solution.py:146
  48.1 1.8 %shard_map.100.refs_10_ = f32[512,256]{1,0:T(8,128)S(1)} custom-call(s32[2]{0:T(128)S(1)} %pad_add_fusion.at, bf16[4,128,512]{2,1,0:T(8,128)(2,1)S(1)} %pad_maximum_fusion.1.refs_0_, bf16[4,128,512]{2,1,0:T(8,128)(2,1)S(1)} %collective-permute-done.18.refs_1_, bf16[2,128,512]{2,1,0:T(8,128)(2,1)S(1)} %get-tuple-element.63.refs_2_, ...), custom_call_target="tpu_custom_call" | custom-call | flops 2147483648 | bytes 1048576 | tf_op jit(solution)/shard_map/pallas_call | solution.py:146
  50.0 4.5 %collective-permute-done.5.refs_0_ = bf16[640,512]{1,0:T(8,128)(2,1)S(1)} collective-permute-done((bf16[640,512]{1,0:T(8,128)(2,1)S(1)}, bf16[640,512]{1,0:T(8,128)(2,1)S(1)}, u32[]{:S(2)}, u32[]{:S(2)}) %collective-permute-start.5) | collective-permute-done | bytes 655392 | tf_op jit(solution)/shard_map/ppermute | solution.py:363
  55.3 2.5 %shard_map.98 = (f32[512,512]{1,0:T(8,128)S(1)}, f32[512,512]{1,0:T(8,128)S(1)}, f32[512,512]{1,0:T(8,128)S(1)}, f32[512,512]{1,0:T(8,128)S(1)}) custom-call(s32[2]{0:T(128)S(1)} %pad_add_fusion.at, f32[512,4096]{1,0:T(8,128)S(1)} %bitcast.47, bf16[512,512]{1,0:T(8,128)(2,1)S(1)} %bitcast.52, bf16[640,512]{1,0:T(8,128)(2,1)S(1)} %collective-permute-done.5.refs_0_, ...), custom_call_target="tpu_custom_call" | custom-call | flops 2147483648 | bytes 1048576 | tf_op jit(solution)/shard_map/pallas_call | solution.py:146
  58.3 1.5 %collective-permute-start.7 = (bf16[256,512]{1,0:T(8,128)(2,1)S(1)}, bf16[256,512]{1,0:T(8,128)(2,1)S(1)}, u32[]{:S(2)}, u32[]{:S(2)}) collective-permute-start(bf16[256,512]{1,0:T(8,128)(2,1)S(1)} %slice.50), channel_id=1, source_target_pairs={{0,1},{1,0},{2,3},{3,2},{4,5},{5,4},{6,7},{7,6},{8,9},{9,8},{10,11... | collective-permute-start | bytes 786440 | tf_op jit(solution)/shard_map/ppermute | solution.py:366
  60.0 1.5 %collective-permute-start.8 = (bf16[256,512]{1,0:T(8,128)(2,1)S(1)}, bf16[256,512]{1,0:T(8,128)(2,1)S(1)}, u32[]{:S(2)}, u32[]{:S(2)}) collective-permute-start(bf16[256,512]{1,0:T(8,128)(2,1)S(1)} %slice.51), channel_id=1, source_target_pairs={{0,2},{1,3},{2,6},{3,7},{6,4},{7,5},{4,0},{5,1},{8,10},{9,11},{10,... | collective-permute-start | bytes 786440 | tf_op jit(solution)/shard_map/ppermute | solution.py:363
  61.5 2.4 %shard_map.101.refs_4_ = f32[512,256]{1,0:T(8,128)S(1)} custom-call(s32[2]{0:T(128)S(1)} %pad_add_fusion.at, bf16[4,128,512]{2,1,0:T(8,128)(2,1)S(1)} %pad_maximum_fusion.1.refs_0_, bf16[4,128,512]{2,1,0:T(8,128)(2,1)S(1)} %collective-permute-done.18.refs_1_, bf16[2,128,512]{2,1,0:T(8,128)(2,1)S(1)} %get-tuple-element.63.refs_2_, ...), custom_call_target="tpu_custom_call" | custom-call | flops 2147483648 | bytes 1048576 | tf_op jit(solution)/shard_map/pallas_call | solution.py:146
  66.5 1.4 %multiply_convert_fusion.1 = (f16[512,512]{1,0:T(8,128)(2,1)}, f32[512,512]{1,0:T(8,128)}) fusion(f32[512,512]{1,0:T(8,128)S(1)} %get-tuple-element.39.refs_9_, f32[512,512]{1,0:T(8,128)S(1)} %collective-permute-done.11), kind=kLoop, calls=%fused_computation.8 | loop fusion | flops 786432 | bytes 3670016 | tf_op jit(solution)/shard_map/convert_element_type | solution.py:323
  70.7 6.2 %collective-permute-start.14 = (f16[512,512]{1,0:T(8,128)(2,1)}, f16[512,512]{1,0:T(8,128)(2,1)}, u32[]{:S(2)}, u32[]{:S(2)}) collective-permute-start(f16[512,512]{1,0:T(8,128)(2,1)} %get-tuple-element.56), channel_id=1, source_target_pairs={{0,16},{1,17},{6,22},{7,23},{10,26},{11,27},{12,28},{13,29},{18,2}... | collective-permute-start | bytes 1572872 | tf_op jit(solution)/shard_map/ppermute | solution.py:381
  76.9 1.5 %shard_map.99 = (f32[512,512]{1,0:T(8,128)S(1)}, f32[512,512]{1,0:T(8,128)S(1)}) custom-call(s32[2]{0:T(128)S(1)} %pad_add_fusion.at, f32[512,4096]{1,0:T(8,128)S(1)} %bitcast.48, bf16[512,512]{1,0:T(8,128)(2,1)S(1)} %bitcast.53, bf16[256,512]{1,0:T(8,128)(2,1)S(1)} %collective-permute-done.7.refs_0_, bf16[256,512]{1,0:T(8,128)(2,1)S(1)} %collective-permute-done.8.refs_1_, ...), custom_call_target="tpu_custom_call" | custom-call | flops 2147483648 | bytes 1048576 | tf_op jit(solution)/shard_map/pallas_call | solution.py:146
  78.5 2.6 %shard_map.102 = f32[4,128,128]{2,1,0:T(8,128)} custom-call(s32[2]{0:T(128)S(1)} %pad_add_fusion.at, bf16[2,128,512]{2,1,0:T(8,128)(2,1)S(1)} %get-tuple-element.62.refs_0_, bf16[2,128,512]{2,1,0:T(8,128)(2,1)S(1)} %pad_maximum_fusion.4.refs_1_, f32[512,512]{1,0:T(8,128)S(1)} %get-tuple-element.46.refs_2_, f32[512,512]{1,0:T(8,128)S(1)} %get-tuple-element.45.refs_3_, ...), custom_call_target="tpu_custom_call" | custom-call | flops 2147483648 | bytes 1048576 | tf_op jit(solution)/shard_map/pallas_call | solution.py:146
  81.1 2.9 %all-to-all-start = ((f32[32,16,128]{2,1,0:T(8,128)}), f32[32,16,128]{2,1,0:T(8,128)S(1)}, u32[]{:S(2)}, u32[]{:S(2)}) async-start(f32[32,16,128]{2,1,0:T(8,128)} %bitcast.13), calls=%async_computation | async-start | bytes 524288 | tf_op jit(solution)/shard_map/all_to_all | solution.py:441
  84.0 3.9 %gather_fusion = bf16[512,512]{1,0:T(8,128)(2,1)S(1)} fusion(bf16[2048,512]{1,0:T(8,128)(2,1)} %bitcast.54, s32[1024]{0:T(1024)S(1)} %pad_clamp_fusion), kind=kCustom, calls=%fused_computation | custom fusion | bytes 1050624 | tf_op jit(solution)/shard_map/jit(_take)/gather | solution.py:463
  88.5 2.2 %fusion.1 = f32[512,64]{1,0:T(8,128)S(1)} fusion(f32[512,512]{1,0:T(8,128)} %param.13, f32[512,512]{0,1:T(8,128)} %copy.10, bf16[512,256]{1,0:T(8,128)(2,1)S(1)} %slice_select_fusion, s32[]{:T(128)S(6)} %select_n.102), kind=kOutput, calls=%fused_computation.4 | convolution fusion | flops 201850880 | bytes 2359300 | tf_op jit(solution)/shard_map/dot_general | solution.py:35
  91.1 3.4 %all-to-all-done = f32[32,16,128]{2,1,0:T(8,128)S(1)} async-done(((f32[32,16,128]{2,1,0:T(8,128)}), f32[32,16,128]{2,1,0:T(8,128)S(1)}, u32[]{:S(2)}, u32[]{:S(2)}) %all-to-all-start) | async-done | bytes 262176 | tf_op jit(solution)/shard_map/all_to_all | solution.py:441
  94.7 1.5 %multiply_convert_fusion = (f16[512,512]{1,0:T(8,128)(2,1)S(1)}, f32[512,512]{1,0:T(8,128)S(1)}) fusion(f32[512,512]{1,0:T(8,128)S(1)} %get-tuple-element.45.refs_3_, f32[512,512]{1,0:T(8,128)} %collective-permute-done.12), kind=kLoop, calls=%fused_computation.7 | loop fusion | flops 786432 | bytes 3670016 | tf_op jit(solution)/shard_map/convert_element_type | solution.py:323
  96.2 2.5 %collective-permute-start.15 = (f16[512,512]{1,0:T(8,128)(2,1)S(1)}, f16[512,512]{1,0:T(8,128)(2,1)S(1)}, u32[]{:S(2)}, u32[]{:S(2)}) collective-permute-start(f16[512,512]{1,0:T(8,128)(2,1)S(1)} %get-tuple-element.49), channel_id=1, source_target_pairs={{0,16},{1,17},{6,22},{7,23},{10,26},{11,27},{12,28},{13,29},{18,2}... | collective-permute-start | bytes 1572872 | tf_op jit(solution)/shard_map/ppermute | solution.py:381
  99.4 2.0 %add_select_fusion = f32[512,512]{1,0:T(8,128)S(1)} fusion(f32[512,512]{1,0:T(8,128)} %get-tuple-element.57, f16[512,512]{1,0:T(8,128)(2,1)} %collective-permute-done.14, f32[512,512]{1,0:T(8,128)} %get-tuple-element.59, f16[512,512]{1,0:T(8,128)(2,1)S(1)} %copy-done.10, pred[]{:T(512)S(6)} %eq.34), kind=kLoop, calls=%fused_computation.6 | loop fusion | flops 1835008 | bytes 4194305 | tf_op jit(solution)/shard_map/jit(_where)/select_n | solution.py:449
  101.7 3.6 %collective-permute-done.15 = f16[512,512]{1,0:T(8,128)(2,1)S(1)} collective-permute-done((f16[512,512]{1,0:T(8,128)(2,1)S(1)}, f16[512,512]{1,0:T(8,128)(2,1)S(1)}, u32[]{:S(2)}, u32[]{:S(2)}) %collective-permute-start.15) | collective-permute-done | bytes 524320 | tf_op jit(solution)/shard_map/ppermute | solution.py:381
  105.3 1.5 %select_dynamic-update-slice_fusion = f32[512,1024]{1,0:T(8,128)S(1)} fusion(f32[512,1024]{1,0:T(8,128)S(1)} %pad_maximum_fusion, s32[]{:T(128)S(6)} %select_n.85, f32[512,512]{1,0:T(8,128)S(1)} %get-tuple-element.53, f16[512,512]{1,0:T(8,128)(2,1)S(1)} %collective-permute-done.15, f32[512,512]{1,0:T(8,128)S(1)} %copy-done.4, ...), kind=kLoop, calls=%fused_computation.5 | loop fusion | flops 1835008 | bytes 4194309 | tf_op jit(solution)/shard_map/dynamic_update_slice | solution.py:452
  (100 shorter events, 20.8 us)
Async XLA Ops:
  0.6 8.5 %copy-start.5 = (f32[512,512]{1,0:T(8,128)S(1)}, f32[512,512]{1,0:T(8,128)}, u32[]{:S(2)}) copy-start(f32[512,512]{1,0:T(8,128)} %param.13) | copy-start | bytes 3145732
  1.6 5.8 %copy-start.7 = (bf16[128,256]{1,0:T(8,128)(2,1)}, bf16[128,256]{1,0:T(8,128)(2,1)S(1)}, u32[]{:S(2)}) copy-start(bf16[128,256]{1,0:T(8,128)(2,1)S(1)} %get-tuple-element.60) | copy-start | bytes 196612
  1.6 6.5 %copy-start.8 = (bf16[128,256]{1,0:T(8,128)(2,1)}, bf16[128,256]{1,0:T(8,128)(2,1)S(1)}, u32[]{:S(2)}) copy-start(bf16[128,256]{1,0:T(8,128)(2,1)S(1)} %get-tuple-element.61) | copy-start | bytes 196612
  1.6 9.8 %copy-start.1 = (bf16[1,512,512]{2,1,0:T(8,128)(2,1)S(1)}, bf16[1,512,512]{2,1,0:T(8,128)(2,1)}, u32[]{:S(2)}) copy-start(bf16[1,512,512]{2,1,0:T(8,128)(2,1)} %param.9) | copy-start | bytes 1572868
  2.8 18.9 %collective-permute-start = (bf16[640,512]{1,0:T(8,128)(2,1)S(1)}, bf16[640,512]{1,0:T(8,128)(2,1)S(1)}, u32[]{:S(2)}, u32[]{:S(2)}) collective-permute-start(bf16[640,512]{1,0:T(8,128)(2,1)S(1)} %maximum_maximum_fusion.refs_0_), channel_id=1, source_target_pairs={{0,2},{1,3},{2,6},{3,7},{6,4},{7,5},{4,0},{5,1},{8,10},{9,11},{10,... | collective-permute-start | bytes 1966088 | tf_op jit(solution)/shard_map/ppermute | solution.py:363
  5.9 18.0 %collective-permute-start.1 = (bf16[640,512]{1,0:T(8,128)(2,1)S(1)}, bf16[640,512]{1,0:T(8,128)(2,1)S(1)}, u32[]{:S(2)}, u32[]{:S(2)}) collective-permute-start(bf16[640,512]{1,0:T(8,128)(2,1)S(1)} %maximum_maximum_fusion.refs_0_), channel_id=1, source_target_pairs={{0,1},{1,0},{2,3},{3,2},{4,5},{5,4},{6,7},{7,6},{8,9},{9,8},{10,11... | collective-permute-start | bytes 1966088 | tf_op jit(solution)/shard_map/ppermute | solution.py:366
  8.1 20.9 %collective-permute-start.16 = (bf16[128,512]{1,0:T(8,128)(2,1)}, bf16[128,512]{1,0:T(8,128)(2,1)}, u32[]{:S(2)}, u32[]{:S(2)}) collective-permute-start(bf16[128,512]{1,0:T(8,128)(2,1)} %get-tuple-element.65), channel_id=1, source_target_pairs={{3,0},{2,1},{7,2},{6,3},{5,6},{4,7},{1,4},{0,5},{11,8},{10,9},{15,... | collective-permute-start | bytes 393224 | tf_op jit(solution)/shard_map/ppermute | solution.py:387
  14.8 14.2 %copy-start.11 = (bf16[1,128,512]{2,1,0:T(8,128)(2,1)S(1)}, bf16[1,128,512]{2,1,0:T(8,128)(2,1)}, u32[]{:S(2)}) copy-start(bf16[1,128,512]{2,1,0:T(8,128)(2,1)} %get-tuple-element.64) | copy-start | bytes 393220
  23.9 15.7 %collective-permute-start.2 = (bf16[640,512]{1,0:T(8,128)(2,1)S(1)}, bf16[640,512]{1,0:T(8,128)(2,1)S(1)}, u32[]{:S(2)}, u32[]{:S(2)}) collective-permute-start(bf16[640,512]{1,0:T(8,128)(2,1)S(1)} %collective-permute-done.refs_0_), channel_id=1, source_target_pairs={{0,2},{1,3},{2,6},{3,7},{6,4},{7,5},{4,0},{5,1},{8,10},{9,11},{10,... | collective-permute-start | bytes 1966088 | tf_op jit(solution)/shard_map/ppermute | solution.py:363
  27.5 12.9 %collective-permute-start.3 = (bf16[640,512]{1,0:T(8,128)(2,1)S(1)}, bf16[640,512]{1,0:T(8,128)(2,1)S(1)}, u32[]{:S(2)}, u32[]{:S(2)}) collective-permute-start(bf16[640,512]{1,0:T(8,128)(2,1)S(1)} %collective-permute-done.refs_0_), channel_id=1, source_target_pairs={{0,1},{1,0},{2,3},{3,2},{4,5},{5,4},{6,7},{7,6},{8,9},{9,8},{10,11... | collective-permute-start | bytes 1966088 | tf_op jit(solution)/shard_map/ppermute | solution.py:366
  30.0 3.5 %collective-permute-start.18 = (bf16[4,128,512]{2,1,0:T(8,128)(2,1)S(1)}, bf16[4,128,512]{2,1,0:T(8,128)(2,1)S(1)}, u32[]{:S(2)}, u32[]{:S(2)}) collective-permute-start(bf16[4,128,512]{2,1,0:T(8,128)(2,1)S(1)} %pad_maximum_fusion.1.refs_0_), channel_id=1, source_target_pairs={{0,8},{8,0},{16,24},{24,16},{1,9},{9,1},{17,25},{25,17},{2,10},{10... | collective-permute-start | bytes 1572872 | tf_op jit(solution)/shard_map/ppermute | solution.py:372
  40.4 14.1 %collective-permute-start.5 = (bf16[640,512]{1,0:T(8,128)(2,1)S(1)}, bf16[640,512]{1,0:T(8,128)(2,1)S(1)}, u32[]{:S(2)}, u32[]{:S(2)}) collective-permute-start(bf16[640,512]{1,0:T(8,128)(2,1)S(1)} %collective-permute-done.2.refs_0_), channel_id=1, source_target_pairs={{0,2},{1,3},{2,6},{3,7},{6,4},{7,5},{4,0},{5,1},{8,10},{9,11},{10,... | collective-permute-start | bytes 1966088 | tf_op jit(solution)/shard_map/ppermute | solution.py:363
  42.5 12.6 %collective-permute-start.6 = (bf16[640,512]{1,0:T(8,128)(2,1)S(1)}, bf16[640,512]{1,0:T(8,128)(2,1)S(1)}, u32[]{:S(2)}, u32[]{:S(2)}) collective-permute-start(bf16[640,512]{1,0:T(8,128)(2,1)S(1)} %collective-permute-done.2.refs_0_), channel_id=1, source_target_pairs={{0,1},{1,0},{2,3},{3,2},{4,5},{5,4},{6,7},{7,6},{8,9},{9,8},{10,11... | collective-permute-start | bytes 1966088 | tf_op jit(solution)/shard_map/ppermute | solution.py:366
  44.9 3.1 %collective-permute-start.17 = (bf16[2,128,512]{2,1,0:T(8,128)(2,1)S(1)}, bf16[2,128,512]{2,1,0:T(8,128)(2,1)S(1)}, u32[]{:S(2)}, u32[]{:S(2)}) collective-permute-start(bf16[2,128,512]{2,1,0:T(8,128)(2,1)S(1)} %get-tuple-element.63.refs_2_), channel_id=1, source_target_pairs={{0,8},{8,0},{16,24},{24,16},{1,9},{9,1},{17,25},{25,17},{2,10},{10... | collective-permute-start | bytes 786440 | tf_op jit(solution)/shard_map/ppermute | solution.py:372
  45.0 10.2 %slice-start = ((s8[8388608]{0:T(1024)(128)(4,1)}), s8[4194304]{0:T(1024)(128)(4,1)S(1)}, s32[]{:S(2)}) async-start(s8[8388608]{0:T(1024)(128)(4,1)} %bitcast.45), calls=%async_computation.1 | async-start | bytes 8388608
  47.5 7.8 %slice-start.1 = ((s8[8388608]{0:T(1024)(128)(4,1)}), s8[4194304]{0:T(1024)(128)(4,1)S(1)}, s32[]{:S(2)}) async-start(s8[8388608]{0:T(1024)(128)(4,1)} %bitcast.45), calls=%async_computation.2 | async-start | bytes 8388608
  47.5 16.5 %collective-permute-start.4 = (f32[512,512]{1,0:T(8,128)S(1)}, f32[512,512]{1,0:T(8,128)S(1)}, u32[]{:S(2)}, u32[]{:S(2)}) collective-permute-start(f32[512,512]{1,0:T(8,128)S(1)} %get-tuple-element.31.refs_4_), channel_id=1, source_target_pairs={{0,8},{8,0},{16,24},{24,16},{1,9},{9,1},{17,25},{25,17},{2,10},{10... | collective-permute-start | bytes 3145736 | tf_op jit(solution)/shard_map/ppermute | solution.py:372
  55.2 4.8 %collective-permute-start.19 = (bf16[2,128,512]{2,1,0:T(8,128)(2,1)S(1)}, bf16[2,128,512]{2,1,0:T(8,128)(2,1)S(1)}, u32[]{:S(2)}, u32[]{:S(2)}) collective-permute-start(bf16[2,128,512]{2,1,0:T(8,128)(2,1)S(1)} %pad_maximum_fusion.5.refs_4_), channel_id=1, source_target_pairs={{0,8},{8,0},{16,24},{24,16},{1,9},{9,1},{17,25},{25,17},{2,10},{10... | collective-permute-start | bytes 786440 | tf_op jit(solution)/shard_map/ppermute | solution.py:372
  57.7 8.8 %collective-permute-start.11 = (f32[512,512]{1,0:T(8,128)S(1)}, f32[512,512]{1,0:T(8,128)S(1)}, u32[]{:S(2)}, u32[]{:S(2)}) collective-permute-start(f32[512,512]{1,0:T(8,128)S(1)} %get-tuple-element.40.refs_8_), channel_id=1, source_target_pairs={{0,8},{8,0},{16,24},{24,16},{1,9},{9,1},{17,25},{25,17},{2,10},{10... | collective-permute-start | bytes 3145736 | tf_op jit(solution)/shard_map/ppermute | solution.py:372
  58.3 11.0 %collective-permute-start.10 = (f32[512,512]{1,0:T(8,128)S(1)}, f32[512,512]{1,0:T(8,128)S(1)}, u32[]{:S(2)}, u32[]{:S(2)}) collective-permute-start(f32[512,512]{1,0:T(8,128)S(1)} %get-tuple-element.38.refs_6_), channel_id=1, source_target_pairs={{0,8},{8,0},{16,24},{24,16},{1,9},{9,1},{17,25},{25,17},{2,10},{10... | collective-permute-start | bytes 3145736 | tf_op jit(solution)/shard_map/ppermute | solution.py:372
  58.3 18.5 %collective-permute-start.7 = (bf16[256,512]{1,0:T(8,128)(2,1)S(1)}, bf16[256,512]{1,0:T(8,128)(2,1)S(1)}, u32[]{:S(2)}, u32[]{:S(2)}) collective-permute-start(bf16[256,512]{1,0:T(8,128)(2,1)S(1)} %slice.50), channel_id=1, source_target_pairs={{0,1},{1,0},{2,3},{3,2},{4,5},{5,4},{6,7},{7,6},{8,9},{9,8},{10,11... | collective-permute-start | bytes 786440 | tf_op jit(solution)/shard_map/ppermute | solution.py:366
  60.0 16.9 %collective-permute-start.8 = (bf16[256,512]{1,0:T(8,128)(2,1)S(1)}, bf16[256,512]{1,0:T(8,128)(2,1)S(1)}, u32[]{:S(2)}, u32[]{:S(2)}) collective-permute-start(bf16[256,512]{1,0:T(8,128)(2,1)S(1)} %slice.51), channel_id=1, source_target_pairs={{0,2},{1,3},{2,6},{3,7},{6,4},{7,5},{4,0},{5,1},{8,10},{9,11},{10,... | collective-permute-start | bytes 786440 | tf_op jit(solution)/shard_map/ppermute | solution.py:363
  65.2 11.6 %collective-permute-start.9 = (f16[512,512]{1,0:T(8,128)(2,1)S(1)}, f16[512,512]{1,0:T(8,128)(2,1)S(1)}, u32[]{:S(2)}, u32[]{:S(2)}) collective-permute-start(f16[512,512]{1,0:T(8,128)(2,1)S(1)} %get-tuple-element.58), channel_id=1, source_target_pairs={{2,18},{3,19},{4,20},{5,21},{8,24},{9,25},{14,30},{15,31},{16,0},{... | collective-permute-start | bytes 1572872 | tf_op jit(solution)/shard_map/ppermute | solution.py:381
  67.9 28.3 %collective-permute-start.13 = (f16[512,512]{1,0:T(8,128)(2,1)}, f16[512,512]{1,0:T(8,128)(2,1)}, u32[]{:S(2)}, u32[]{:S(2)}) collective-permute-start(f16[512,512]{1,0:T(8,128)(2,1)} %get-tuple-element.54), channel_id=1, source_target_pairs={{2,18},{3,19},{4,20},{5,21},{8,24},{9,25},{14,30},{15,31},{16,0},{... | collective-permute-start | bytes 1572872 | tf_op jit(solution)/shard_map/ppermute | solution.py:381
  70.7 25.5 %collective-permute-start.14 = (f16[512,512]{1,0:T(8,128)(2,1)}, f16[512,512]{1,0:T(8,128)(2,1)}, u32[]{:S(2)}, u32[]{:S(2)}) collective-permute-start(f16[512,512]{1,0:T(8,128)(2,1)} %get-tuple-element.56), channel_id=1, source_target_pairs={{0,16},{1,17},{6,22},{7,23},{10,26},{11,27},{12,28},{13,29},{18,2}... | collective-permute-start | bytes 1572872 | tf_op jit(solution)/shard_map/ppermute | solution.py:381
  78.4 16.3 %collective-permute-start.12 = (f32[512,512]{1,0:T(8,128)S(1)}, f32[512,512]{1,0:T(8,128)}, u32[]{:S(2)}, u32[]{:S(2)}) collective-permute-start(f32[512,512]{1,0:T(8,128)S(1)} %get-tuple-element.46.refs_2_), channel_id=1, source_target_pairs={{0,8},{8,0},{16,24},{24,16},{1,9},{9,1},{17,25},{25,17},{2,10},{10... | collective-permute-start | bytes 3145736 | tf_op jit(solution)/shard_map/ppermute | solution.py:372
  78.5 5.4 %copy-start.12 = (s32[512]{0:T(512)S(1)}, s32[512]{0:T(512)}, u32[]{:S(2)}) copy-start(s32[512]{0:T(512)} %param.12) | copy-start | bytes 6148
  81.1 13.5 %all-to-all-start = ((f32[32,16,128]{2,1,0:T(8,128)}), f32[32,16,128]{2,1,0:T(8,128)S(1)}, u32[]{:S(2)}, u32[]{:S(2)}) async-start(f32[32,16,128]{2,1,0:T(8,128)} %bitcast.13), calls=%async_computation | async-start | bytes 524288 | tf_op jit(solution)/shard_map/all_to_all | solution.py:441
  84.0 4.0 %copy-start.13 = (f32[512]{0:T(512)S(1)}, f32[512]{0:T(512)}, u32[]{:S(2)}) copy-start(f32[512]{0:T(512)} %param.14) | copy-start | bytes 6148
  91.1 8.3 %copy-start.10 = (f16[512,512]{1,0:T(8,128)(2,1)S(1)}, f16[512,512]{1,0:T(8,128)(2,1)}, u32[]{:S(2)}) copy-start(f16[512,512]{1,0:T(8,128)(2,1)} %copy-done.9) | copy-start | bytes 1572868
  96.2 9.1 %collective-permute-start.15 = (f16[512,512]{1,0:T(8,128)(2,1)S(1)}, f16[512,512]{1,0:T(8,128)(2,1)S(1)}, u32[]{:S(2)}, u32[]{:S(2)}) collective-permute-start(f16[512,512]{1,0:T(8,128)(2,1)S(1)} %get-tuple-element.49), channel_id=1, source_target_pairs={{0,16},{1,17},{6,22},{7,23},{10,26},{11,27},{12,28},{13,29},{18,2}... | collective-permute-start | bytes 1572872 | tf_op jit(solution)/shard_map/ppermute | solution.py:381
  101.4 3.9 %copy-start.4 = (f32[512,512]{1,0:T(8,128)S(1)}, f32[512,512]{1,0:T(8,128)}, u32[]{:S(2)}) copy-start(f32[512,512]{1,0:T(8,128)} %get-tuple-element.55) | copy-start | bytes 3145732
  (6 other events, 11.8 us)

commit v5 on v4

--- a/solution.py
+++ b/solution.py
@@ -164,7 +164,7 @@
     return mul(high, right) + mul(low, right)
 
 
-ROW_STEPS = 4
+ROW_STEPS = 2
 
 
 def shares(place, stiffness, lower, blocks):

time: 109 us -> 107 us (0.982)
  Pallas kernels: 17.2 us -> 13.7 us
  waiting for transfers between devices: 26.7 us -> 28.8 us
    pallas_call x8, Pallas kernels: 17.2 us -> 13.7 us  [call(): pl.pallas_call(body, out_shape=[jax.ShapeDtypeStruct(shape, dtype) for sh...]
    ppermute x4, waiting for transfers between devices: 16.1 us -> 18.1 us  [over_z(): return lax.ppermute(block, 'tile', ring_pairs(True))]
  transfers between devices with their start and end apart: 21 -> 21, of which waited for: 8 -> 8; matrix products, arithmetic and copies ran while one was open for 20% -> 21% of each run, Pallas kernels for 16% -> 13%
where the time goes in v5:
time: 107 us
  starting transfers between devices  32.7 us (31%)
  waiting for transfers between devices  28.8 us (27%)
  other arithmetic  15.1 us (14%)
  Pallas kernels  13.7 us (13%)
  local copies, waits for them, and re-layouts  12.1 us (11%)
  matrix products  3.08 us (3%)
  between operations  1.26 us (1%)
    ppermute x4, waiting for transfers between devices, over_z(): return lax.ppermute(block, 'tile', ring_pairs(True))  18.1 us
    pallas_call x8, Pallas kernels, call(): pl.pallas_call(body, out_shape=[jax.ShapeDtypeStruct(shape, dtype) for sh...  13.7 us
    ppermute x4, starting transfers between devices, over_y_of(): return lax.ppermute(block, ('subtree', 'tile'), route)  11.2 us
    ppermute x4, starting transfers between devices, over_z(): return lax.ppermute(block, 'tile', ring_pairs(True))  10.2 us
    unnamed x44, local copies, waits for them, and re-layouts  7.1 us
    ppermute x4, starting transfers between devices, over_x(): return lax.ppermute(block, 'tile', [(i, i ^ 1) for i in range(tiles)])  5.96 us
    convert_element_type x4, other arithmetic, to_wire(): return (value * SHARE_SCALE).astype(jnp.float16)  5.59 us
    gather x1, local copies, waits for them, and re-layouts, shards_ring(): jnp.take(table, line * (chunk // 2) + half_row % (chunk // 2), axis=0, mo...  3.85 us
  transfers between devices with their start and end apart: 21, of which 8 were waited for; matrix products, arithmetic and copies ran while one was open for 21% of the time, Pallas kernels for 13%

profile of v5, /device:TPU:0, one launch (start us, length us, event | category | flops | bytes accessed | tf_op | source)
XLA Modules:
  0.0 106.8 jit_solution(15226839576698761019)
XLA Ops:
  2.8 3.1 %collective-permute-start = (bf16[640,512]{1,0:T(8,128)(2,1)S(1)}, bf16[640,512]{1,0:T(8,128)(2,1)S(1)}, u32[]{:S(2)}, u32[]{:S(2)}) collective-permute-start(bf16[640,512]{1,0:T(8,128)(2,1)S(1)} %maximum_maximum_fusion.refs_0_), channel_id=1, source_target_pairs={{0,2},{1,3},{2,6},{3,7},{6,4},{7,5},{4,0},{5,1},{8,10},{9,11},{10,... | collective-permute-start | bytes 1966088 | tf_op jit(solution)/shard_map/ppermute | solution.py:363
  5.9 1.5 %collective-permute-start.1 = (bf16[640,512]{1,0:T(8,128)(2,1)S(1)}, bf16[640,512]{1,0:T(8,128)(2,1)S(1)}, u32[]{:S(2)}, u32[]{:S(2)}) collective-permute-start(bf16[640,512]{1,0:T(8,128)(2,1)S(1)} %maximum_maximum_fusion.refs_0_), channel_id=1, source_target_pairs={{0,1},{1,0},{2,3},{3,2},{4,5},{5,4},{6,7},{7,6},{8,9},{9,8},{10,11... | collective-permute-start | bytes 1966088 | tf_op jit(solution)/shard_map/ppermute | solution.py:366
  11.4 3.4 %copy-done = f32[1,512,4096]{2,1,0:T(8,128)S(1)} copy-done((f32[1,512,4096]{2,1,0:T(8,128)S(1)}, f32[1,512,4096]{2,1,0:T(8,128)}, u32[]{:S(2)}) %copy-start) | copy-done | bytes 8388632
  16.0 5.7 %collective-permute-done.refs_0_ = bf16[640,512]{1,0:T(8,128)(2,1)S(1)} collective-permute-done((bf16[640,512]{1,0:T(8,128)(2,1)S(1)}, bf16[640,512]{1,0:T(8,128)(2,1)S(1)}, u32[]{:S(2)}, u32[]{:S(2)}) %collective-permute-start) | collective-permute-done | bytes 655392 | tf_op jit(solution)/shard_map/ppermute | solution.py:363
  21.7 2.2 %collective-permute-done.1.refs_1_ = bf16[640,512]{1,0:T(8,128)(2,1)S(1)} collective-permute-done((bf16[640,512]{1,0:T(8,128)(2,1)S(1)}, bf16[640,512]{1,0:T(8,128)(2,1)S(1)}, u32[]{:S(2)}, u32[]{:S(2)}) %collective-permute-start.1) | collective-permute-done | bytes 655392 | tf_op jit(solution)/shard_map/ppermute | solution.py:366
  23.9 3.5 %collective-permute-start.2 = (bf16[640,512]{1,0:T(8,128)(2,1)S(1)}, bf16[640,512]{1,0:T(8,128)(2,1)S(1)}, u32[]{:S(2)}, u32[]{:S(2)}) collective-permute-start(bf16[640,512]{1,0:T(8,128)(2,1)S(1)} %collective-permute-done.refs_0_), channel_id=1, source_target_pairs={{0,2},{1,3},{2,6},{3,7},{6,4},{7,5},{4,0},{5,1},{8,10},{9,11},{10,... | collective-permute-start | bytes 1966088 | tf_op jit(solution)/shard_map/ppermute | solution.py:363
  27.5 1.5 %collective-permute-start.3 = (bf16[640,512]{1,0:T(8,128)(2,1)S(1)}, bf16[640,512]{1,0:T(8,128)(2,1)S(1)}, u32[]{:S(2)}, u32[]{:S(2)}) collective-permute-start(bf16[640,512]{1,0:T(8,128)(2,1)S(1)} %collective-permute-done.refs_0_), channel_id=1, source_target_pairs={{0,1},{1,0},{2,3},{3,2},{4,5},{5,4},{6,7},{7,6},{8,9},{9,8},{10,11... | collective-permute-start | bytes 1966088 | tf_op jit(solution)/shard_map/ppermute | solution.py:366
  30.1 1.8 %shard_map.97 = (f32[512,512]{1,0:T(8,128)S(1)}, f32[512,512]{1,0:T(8,128)S(1)}) custom-call(s32[2]{0:T(128)S(1)} %pad_add_fusion.at, f32[512,4096]{1,0:T(8,128)S(1)} %bitcast.43, bf16[512,512]{1,0:T(8,128)(2,1)S(1)} %bitcast.50, bf16[640,512]{1,0:T(8,128)(2,1)S(1)} %collective-permute-done.refs_0_, bf16[640,512]{1,0:T(8,128)(2,1)S(1)} %collective-permute-done.1.refs_1_), custom_call_target="tpu_custom_call" | custom-call | flops 2147483648 | bytes 1048576 | tf_op jit(solution)/shard_map/pallas_call | solution.py:146
  32.8 6.8 %collective-permute-done.2.refs_0_ = bf16[640,512]{1,0:T(8,128)(2,1)S(1)} collective-permute-done((bf16[640,512]{1,0:T(8,128)(2,1)S(1)}, bf16[640,512]{1,0:T(8,128)(2,1)S(1)}, u32[]{:S(2)}, u32[]{:S(2)}) %collective-permute-start.2) | collective-permute-done | bytes 655392 | tf_op jit(solution)/shard_map/ppermute | solution.py:363
  40.4 2.1 %collective-permute-start.5 = (bf16[640,512]{1,0:T(8,128)(2,1)S(1)}, bf16[640,512]{1,0:T(8,128)(2,1)S(1)}, u32[]{:S(2)}, u32[]{:S(2)}) collective-permute-start(bf16[640,512]{1,0:T(8,128)(2,1)S(1)} %collective-permute-done.2.refs_0_), channel_id=1, source_target_pairs={{0,2},{1,3},{2,6},{3,7},{6,4},{7,5},{4,0},{5,1},{8,10},{9,11},{10,... | collective-permute-start | bytes 1966088 | tf_op jit(solution)/shard_map/ppermute | solution.py:363
  42.5 1.5 %collective-permute-start.6 = (bf16[640,512]{1,0:T(8,128)(2,1)S(1)}, bf16[640,512]{1,0:T(8,128)(2,1)S(1)}, u32[]{:S(2)}, u32[]{:S(2)}) collective-permute-start(bf16[640,512]{1,0:T(8,128)(2,1)S(1)} %collective-permute-done.2.refs_0_), channel_id=1, source_target_pairs={{0,1},{1,0},{2,3},{3,2},{4,5},{5,4},{6,7},{7,6},{8,9},{9,8},{10,11... | collective-permute-start | bytes 1966088 | tf_op jit(solution)/shard_map/ppermute | solution.py:366
  45.0 1.8 %shard_map.96 = (f32[512,512]{1,0:T(8,128)S(1)}, f32[512,512]{1,0:T(8,128)S(1)}, f32[512,512]{1,0:T(8,128)S(1)}) custom-call(s32[2]{0:T(128)S(1)} %pad_add_fusion.at, f32[512,4096]{1,0:T(8,128)S(1)} %bitcast.44, bf16[512,512]{1,0:T(8,128)(2,1)S(1)} %bitcast.51, bf16[640,512]{1,0:T(8,128)(2,1)S(1)} %collective-permute-done.2.refs_0_, ...), custom_call_target="tpu_custom_call" | custom-call | flops 2147483648 | bytes 1048576 | tf_op jit(solution)/shard_map/pallas_call | solution.py:146
  47.5 1.5 %shard_map.100.refs_10_ = f32[512,256]{1,0:T(8,128)S(1)} custom-call(s32[2]{0:T(128)S(1)} %pad_add_fusion.at, bf16[4,128,512]{2,1,0:T(8,128)(2,1)S(1)} %pad_maximum_fusion.1.refs_0_, bf16[4,128,512]{2,1,0:T(8,128)(2,1)S(1)} %collective-permute-done.18.refs_1_, bf16[2,128,512]{2,1,0:T(8,128)(2,1)S(1)} %get-tuple-element.63.refs_2_, ...), custom_call_target="tpu_custom_call" | custom-call | flops 2147483648 | bytes 1048576 | tf_op jit(solution)/shard_map/pallas_call | solution.py:146
  48.9 5.5 %collective-permute-done.5.refs_0_ = bf16[640,512]{1,0:T(8,128)(2,1)S(1)} collective-permute-done((bf16[640,512]{1,0:T(8,128)(2,1)S(1)}, bf16[640,512]{1,0:T(8,128)(2,1)S(1)}, u32[]{:S(2)}, u32[]{:S(2)}) %collective-permute-start.5) | collective-permute-done | bytes 655392 | tf_op jit(solution)/shard_map/ppermute | solution.py:363
  55.3 1.8 %shard_map.98 = (f32[512,512]{1,0:T(8,128)S(1)}, f32[512,512]{1,0:T(8,128)S(1)}, f32[512,512]{1,0:T(8,128)S(1)}, f32[512,512]{1,0:T(8,128)S(1)}) custom-call(s32[2]{0:T(128)S(1)} %pad_add_fusion.at, f32[512,4096]{1,0:T(8,128)S(1)} %bitcast.47, bf16[512,512]{1,0:T(8,128)(2,1)S(1)} %bitcast.52, bf16[640,512]{1,0:T(8,128)(2,1)S(1)} %collective-permute-done.5.refs_0_, ...), custom_call_target="tpu_custom_call" | custom-call | flops 2147483648 | bytes 1048576 | tf_op jit(solution)/shard_map/pallas_call | solution.py:146
  57.7 1.5 %collective-permute-start.7 = (bf16[256,512]{1,0:T(8,128)(2,1)S(1)}, bf16[256,512]{1,0:T(8,128)(2,1)S(1)}, u32[]{:S(2)}, u32[]{:S(2)}) collective-permute-start(bf16[256,512]{1,0:T(8,128)(2,1)S(1)} %slice.50), channel_id=1, source_target_pairs={{0,1},{1,0},{2,3},{3,2},{4,5},{5,4},{6,7},{7,6},{8,9},{9,8},{10,11... | collective-permute-start | bytes 786440 | tf_op jit(solution)/shard_map/ppermute | solution.py:366
  59.3 1.5 %collective-permute-start.8 = (bf16[256,512]{1,0:T(8,128)(2,1)S(1)}, bf16[256,512]{1,0:T(8,128)(2,1)S(1)}, u32[]{:S(2)}, u32[]{:S(2)}) collective-permute-start(bf16[256,512]{1,0:T(8,128)(2,1)S(1)} %slice.51), channel_id=1, source_target_pairs={{0,2},{1,3},{2,6},{3,7},{6,4},{7,5},{4,0},{5,1},{8,10},{9,11},{10,... | collective-permute-start | bytes 786440 | tf_op jit(solution)/shard_map/ppermute | solution.py:363
  60.8 2.1 %shard_map.101.refs_4_ = f32[512,256]{1,0:T(8,128)S(1)} custom-call(s32[2]{0:T(128)S(1)} %pad_add_fusion.at, bf16[4,128,512]{2,1,0:T(8,128)(2,1)S(1)} %pad_maximum_fusion.1.refs_0_, bf16[4,128,512]{2,1,0:T(8,128)(2,1)S(1)} %collective-permute-done.18.refs_1_, bf16[2,128,512]{2,1,0:T(8,128)(2,1)S(1)} %get-tuple-element.63.refs_2_, ...), custom_call_target="tpu_custom_call" | custom-call | flops 2147483648 | bytes 1048576 | tf_op jit(solution)/shard_map/pallas_call | solution.py:146
  65.5 1.4 %multiply_convert_fusion.1 = (f16[512,512]{1,0:T(8,128)(2,1)}, f32[512,512]{1,0:T(8,128)}) fusion(f32[512,512]{1,0:T(8,128)S(1)} %get-tuple-element.39.refs_9_, f32[512,512]{1,0:T(8,128)S(1)} %collective-permute-done.11), kind=kLoop, calls=%fused_computation.8 | loop fusion | flops 786432 | bytes 3670016 | tf_op jit(solution)/shard_map/convert_element_type | solution.py:323
  68.2 1.4 %multiply_convert_fusion.2 = (f16[512,512]{1,0:T(8,128)(2,1)}, f32[512,512]{1,0:T(8,128)}) fusion(f32[512,512]{1,0:T(8,128)S(1)} %get-tuple-element.37.refs_7_, f32[512,512]{1,0:T(8,128)S(1)} %collective-permute-done.10), kind=kLoop, calls=%fused_computation.9 | loop fusion | flops 786432 | bytes 3670016 | tf_op jit(solution)/shard_map/convert_element_type | solution.py:323
  69.6 6.2 %collective-permute-start.14 = (f16[512,512]{1,0:T(8,128)(2,1)}, f16[512,512]{1,0:T(8,128)(2,1)}, u32[]{:S(2)}, u32[]{:S(2)}) collective-permute-start(f16[512,512]{1,0:T(8,128)(2,1)} %get-tuple-element.56), channel_id=1, source_target_pairs={{0,16},{1,17},{6,22},{7,23},{10,26},{11,27},{12,28},{13,29},{18,2}... | collective-permute-start | bytes 1572872 | tf_op jit(solution)/shard_map/ppermute | solution.py:381
  77.1 2.6 %shard_map.102 = f32[4,128,128]{2,1,0:T(8,128)} custom-call(s32[2]{0:T(128)S(1)} %pad_add_fusion.at, bf16[2,128,512]{2,1,0:T(8,128)(2,1)S(1)} %get-tuple-element.62.refs_0_, bf16[2,128,512]{2,1,0:T(8,128)(2,1)S(1)} %pad_maximum_fusion.4.refs_1_, f32[512,512]{1,0:T(8,128)S(1)} %get-tuple-element.46.refs_2_, f32[512,512]{1,0:T(8,128)S(1)} %get-tuple-element.45.refs_3_, ...), custom_call_target="tpu_custom_call" | custom-call | flops 2147483648 | bytes 1048576 | tf_op jit(solution)/shard_map/pallas_call | solution.py:146
  79.7 2.9 %all-to-all-start = ((f32[32,16,128]{2,1,0:T(8,128)}), f32[32,16,128]{2,1,0:T(8,128)S(1)}, u32[]{:S(2)}, u32[]{:S(2)}) async-start(f32[32,16,128]{2,1,0:T(8,128)} %bitcast.13), calls=%async_computation | async-start | bytes 524288 | tf_op jit(solution)/shard_map/all_to_all | solution.py:441
  82.7 3.9 %gather_fusion = bf16[512,512]{1,0:T(8,128)(2,1)S(1)} fusion(bf16[2048,512]{1,0:T(8,128)(2,1)} %bitcast.54, s32[1024]{0:T(1024)S(1)} %pad_clamp_fusion), kind=kCustom, calls=%fused_computation | custom fusion | bytes 1050624 | tf_op jit(solution)/shard_map/jit(_take)/gather | solution.py:463
  87.1 2.2 %fusion.1 = f32[512,64]{1,0:T(8,128)S(1)} fusion(f32[512,512]{1,0:T(8,128)} %param.13, f32[512,512]{0,1:T(8,128)} %copy.10, bf16[512,256]{1,0:T(8,128)(2,1)S(1)} %slice_select_fusion, s32[]{:T(128)S(6)} %select_n.102), kind=kOutput, calls=%fused_computation.4 | convolution fusion | flops 201850880 | bytes 2359300 | tf_op jit(solution)/shard_map/dot_general | solution.py:35
  89.8 3.4 %all-to-all-done = f32[32,16,128]{2,1,0:T(8,128)S(1)} async-done(((f32[32,16,128]{2,1,0:T(8,128)}), f32[32,16,128]{2,1,0:T(8,128)S(1)}, u32[]{:S(2)}, u32[]{:S(2)}) %all-to-all-start) | async-done | bytes 262176 | tf_op jit(solution)/shard_map/all_to_all | solution.py:441
  93.3 1.5 %multiply_convert_fusion = (f16[512,512]{1,0:T(8,128)(2,1)S(1)}, f32[512,512]{1,0:T(8,128)S(1)}) fusion(f32[512,512]{1,0:T(8,128)S(1)} %get-tuple-element.45.refs_3_, f32[512,512]{1,0:T(8,128)} %collective-permute-done.12), kind=kLoop, calls=%fused_computation.7 | loop fusion | flops 786432 | bytes 3670016 | tf_op jit(solution)/shard_map/convert_element_type | solution.py:323
  94.8 2.5 %collective-permute-start.15 = (f16[512,512]{1,0:T(8,128)(2,1)S(1)}, f16[512,512]{1,0:T(8,128)(2,1)S(1)}, u32[]{:S(2)}, u32[]{:S(2)}) collective-permute-start(f16[512,512]{1,0:T(8,128)(2,1)S(1)} %get-tuple-element.49), channel_id=1, source_target_pairs={{0,16},{1,17},{6,22},{7,23},{10,26},{11,27},{12,28},{13,29},{18,2}... | collective-permute-start | bytes 1572872 | tf_op jit(solution)/shard_map/ppermute | solution.py:381
  98.0 2.0 %add_select_fusion = f32[512,512]{1,0:T(8,128)S(1)} fusion(f32[512,512]{1,0:T(8,128)} %get-tuple-element.57, f16[512,512]{1,0:T(8,128)(2,1)} %collective-permute-done.14, f32[512,512]{1,0:T(8,128)} %get-tuple-element.59, f16[512,512]{1,0:T(8,128)(2,1)S(1)} %copy-done.10, pred[]{:T(512)S(6)} %eq.34), kind=kLoop, calls=%fused_computation.6 | loop fusion | flops 1835008 | bytes 4194305 | tf_op jit(solution)/shard_map/jit(_where)/select_n | solution.py:449
  100.3 3.6 %collective-permute-done.15 = f16[512,512]{1,0:T(8,128)(2,1)S(1)} collective-permute-done((f16[512,512]{1,0:T(8,128)(2,1)S(1)}, f16[512,512]{1,0:T(8,128)(2,1)S(1)}, u32[]{:S(2)}, u32[]{:S(2)}) %collective-permute-start.15) | collective-permute-done | bytes 524320 | tf_op jit(solution)/shard_map/ppermute | solution.py:381
  104.0 1.5 %select_dynamic-update-slice_fusion = f32[512,1024]{1,0:T(8,128)S(1)} fusion(f32[512,1024]{1,0:T(8,128)S(1)} %pad_maximum_fusion, s32[]{:T(128)S(6)} %select_n.85, f32[512,512]{1,0:T(8,128)S(1)} %get-tuple-element.53, f16[512,512]{1,0:T(8,128)(2,1)S(1)} %collective-permute-done.15, f32[512,512]{1,0:T(8,128)S(1)} %copy-done.4, ...), kind=kLoop, calls=%fused_computation.5 | loop fusion | flops 1835008 | bytes 4194309 | tf_op jit(solution)/shard_map/dynamic_update_slice | solution.py:452
  105.5 1.3 %copy-done.6 = f32[512,1024]{1,0:T(8,128)} copy-done((f32[512,1024]{1,0:T(8,128)}, f32[512,1024]{1,0:T(8,128)S(1)}, u32[]{:S(2)}) %copy-start.6) | copy-done | bytes 2097176
  (100 shorter events, 20.4 us)
Async XLA Ops:
  0.6 8.5 %copy-start.5 = (f32[512,512]{1,0:T(8,128)S(1)}, f32[512,512]{1,0:T(8,128)}, u32[]{:S(2)}) copy-start(f32[512,512]{1,0:T(8,128)} %param.13) | copy-start | bytes 3145732
  1.6 5.8 %copy-start.7 = (bf16[128,256]{1,0:T(8,128)(2,1)}, bf16[128,256]{1,0:T(8,128)(2,1)S(1)}, u32[]{:S(2)}) copy-start(bf16[128,256]{1,0:T(8,128)(2,1)S(1)} %get-tuple-element.60) | copy-start | bytes 196612
  1.6 6.5 %copy-start.8 = (bf16[128,256]{1,0:T(8,128)(2,1)}, bf16[128,256]{1,0:T(8,128)(2,1)S(1)}, u32[]{:S(2)}) copy-start(bf16[128,256]{1,0:T(8,128)(2,1)S(1)} %get-tuple-element.61) | copy-start | bytes 196612
  1.6 9.8 %copy-start.1 = (bf16[1,512,512]{2,1,0:T(8,128)(2,1)S(1)}, bf16[1,512,512]{2,1,0:T(8,128)(2,1)}, u32[]{:S(2)}) copy-start(bf16[1,512,512]{2,1,0:T(8,128)(2,1)} %param.9) | copy-start | bytes 1572868
  2.8 18.9 %collective-permute-start = (bf16[640,512]{1,0:T(8,128)(2,1)S(1)}, bf16[640,512]{1,0:T(8,128)(2,1)S(1)}, u32[]{:S(2)}, u32[]{:S(2)}) collective-permute-start(bf16[640,512]{1,0:T(8,128)(2,1)S(1)} %maximum_maximum_fusion.refs_0_), channel_id=1, source_target_pairs={{0,2},{1,3},{2,6},{3,7},{6,4},{7,5},{4,0},{5,1},{8,10},{9,11},{10,... | collective-permute-start | bytes 1966088 | tf_op jit(solution)/shard_map/ppermute | solution.py:363
  5.9 18.0 %collective-permute-start.1 = (bf16[640,512]{1,0:T(8,128)(2,1)S(1)}, bf16[640,512]{1,0:T(8,128)(2,1)S(1)}, u32[]{:S(2)}, u32[]{:S(2)}) collective-permute-start(bf16[640,512]{1,0:T(8,128)(2,1)S(1)} %maximum_maximum_fusion.refs_0_), channel_id=1, source_target_pairs={{0,1},{1,0},{2,3},{3,2},{4,5},{5,4},{6,7},{7,6},{8,9},{9,8},{10,11... | collective-permute-start | bytes 1966088 | tf_op jit(solution)/shard_map/ppermute | solution.py:366
  8.1 20.9 %collective-permute-start.16 = (bf16[128,512]{1,0:T(8,128)(2,1)}, bf16[128,512]{1,0:T(8,128)(2,1)}, u32[]{:S(2)}, u32[]{:S(2)}) collective-permute-start(bf16[128,512]{1,0:T(8,128)(2,1)} %get-tuple-element.65), channel_id=1, source_target_pairs={{3,0},{2,1},{7,2},{6,3},{5,6},{4,7},{1,4},{0,5},{11,8},{10,9},{15,... | collective-permute-start | bytes 393224 | tf_op jit(solution)/shard_map/ppermute | solution.py:387
  14.8 14.2 %copy-start.11 = (bf16[1,128,512]{2,1,0:T(8,128)(2,1)S(1)}, bf16[1,128,512]{2,1,0:T(8,128)(2,1)}, u32[]{:S(2)}) copy-start(bf16[1,128,512]{2,1,0:T(8,128)(2,1)} %get-tuple-element.64) | copy-start | bytes 393220
  23.9 15.7 %collective-permute-start.2 = (bf16[640,512]{1,0:T(8,128)(2,1)S(1)}, bf16[640,512]{1,0:T(8,128)(2,1)S(1)}, u32[]{:S(2)}, u32[]{:S(2)}) collective-permute-start(bf16[640,512]{1,0:T(8,128)(2,1)S(1)} %collective-permute-done.refs_0_), channel_id=1, source_target_pairs={{0,2},{1,3},{2,6},{3,7},{6,4},{7,5},{4,0},{5,1},{8,10},{9,11},{10,... | collective-permute-start | bytes 1966088 | tf_op jit(solution)/shard_map/ppermute | solution.py:363
  27.5 12.9 %collective-permute-start.3 = (bf16[640,512]{1,0:T(8,128)(2,1)S(1)}, bf16[640,512]{1,0:T(8,128)(2,1)S(1)}, u32[]{:S(2)}, u32[]{:S(2)}) collective-permute-start(bf16[640,512]{1,0:T(8,128)(2,1)S(1)} %collective-permute-done.refs_0_), channel_id=1, source_target_pairs={{0,1},{1,0},{2,3},{3,2},{4,5},{5,4},{6,7},{7,6},{8,9},{9,8},{10,11... | collective-permute-start | bytes 1966088 | tf_op jit(solution)/shard_map/ppermute | solution.py:366
  30.0 2.8 %collective-permute-start.18 = (bf16[4,128,512]{2,1,0:T(8,128)(2,1)S(1)}, bf16[4,128,512]{2,1,0:T(8,128)(2,1)S(1)}, u32[]{:S(2)}, u32[]{:S(2)}) collective-permute-start(bf16[4,128,512]{2,1,0:T(8,128)(2,1)S(1)} %pad_maximum_fusion.1.refs_0_), channel_id=1, source_target_pairs={{0,8},{8,0},{16,24},{24,16},{1,9},{9,1},{17,25},{25,17},{2,10},{10... | collective-permute-start | bytes 1572872 | tf_op jit(solution)/shard_map/ppermute | solution.py:372
  40.4 14.1 %collective-permute-start.5 = (bf16[640,512]{1,0:T(8,128)(2,1)S(1)}, bf16[640,512]{1,0:T(8,128)(2,1)S(1)}, u32[]{:S(2)}, u32[]{:S(2)}) collective-permute-start(bf16[640,512]{1,0:T(8,128)(2,1)S(1)} %collective-permute-done.2.refs_0_), channel_id=1, source_target_pairs={{0,2},{1,3},{2,6},{3,7},{6,4},{7,5},{4,0},{5,1},{8,10},{9,11},{10,... | collective-permute-start | bytes 1966088 | tf_op jit(solution)/shard_map/ppermute | solution.py:363
  42.5 12.6 %collective-permute-start.6 = (bf16[640,512]{1,0:T(8,128)(2,1)S(1)}, bf16[640,512]{1,0:T(8,128)(2,1)S(1)}, u32[]{:S(2)}, u32[]{:S(2)}) collective-permute-start(bf16[640,512]{1,0:T(8,128)(2,1)S(1)} %collective-permute-done.2.refs_0_), channel_id=1, source_target_pairs={{0,1},{1,0},{2,3},{3,2},{4,5},{5,4},{6,7},{7,6},{8,9},{9,8},{10,11... | collective-permute-start | bytes 1966088 | tf_op jit(solution)/shard_map/ppermute | solution.py:366
  44.9 2.5 %collective-permute-start.17 = (bf16[2,128,512]{2,1,0:T(8,128)(2,1)S(1)}, bf16[2,128,512]{2,1,0:T(8,128)(2,1)S(1)}, u32[]{:S(2)}, u32[]{:S(2)}) collective-permute-start(bf16[2,128,512]{2,1,0:T(8,128)(2,1)S(1)} %get-tuple-element.63.refs_2_), channel_id=1, source_target_pairs={{0,8},{8,0},{16,24},{24,16},{1,9},{9,1},{17,25},{25,17},{2,10},{10... | collective-permute-start | bytes 786440 | tf_op jit(solution)/shard_map/ppermute | solution.py:372
  45.0 10.2 %slice-start = ((s8[8388608]{0:T(1024)(128)(4,1)}), s8[4194304]{0:T(1024)(128)(4,1)S(1)}, s32[]{:S(2)}) async-start(s8[8388608]{0:T(1024)(128)(4,1)} %bitcast.45), calls=%async_computation.1 | async-start | bytes 8388608
  46.8 8.5 %slice-start.1 = ((s8[8388608]{0:T(1024)(128)(4,1)}), s8[4194304]{0:T(1024)(128)(4,1)S(1)}, s32[]{:S(2)}) async-start(s8[8388608]{0:T(1024)(128)(4,1)} %bitcast.45), calls=%async_computation.2 | async-start | bytes 8388608
  46.8 16.1 %collective-permute-start.4 = (f32[512,512]{1,0:T(8,128)S(1)}, f32[512,512]{1,0:T(8,128)S(1)}, u32[]{:S(2)}, u32[]{:S(2)}) collective-permute-start(f32[512,512]{1,0:T(8,128)S(1)} %get-tuple-element.31.refs_4_), channel_id=1, source_target_pairs={{0,8},{8,0},{16,24},{24,16},{1,9},{9,1},{17,25},{25,17},{2,10},{10... | collective-permute-start | bytes 3145736 | tf_op jit(solution)/shard_map/ppermute | solution.py:372
  55.2 4.1 %collective-permute-start.19 = (bf16[2,128,512]{2,1,0:T(8,128)(2,1)S(1)}, bf16[2,128,512]{2,1,0:T(8,128)(2,1)S(1)}, u32[]{:S(2)}, u32[]{:S(2)}) collective-permute-start(bf16[2,128,512]{2,1,0:T(8,128)(2,1)S(1)} %pad_maximum_fusion.5.refs_4_), channel_id=1, source_target_pairs={{0,8},{8,0},{16,24},{24,16},{1,9},{9,1},{17,25},{25,17},{2,10},{10... | collective-permute-start | bytes 786440 | tf_op jit(solution)/shard_map/ppermute | solution.py:372
  57.0 8.4 %collective-permute-start.11 = (f32[512,512]{1,0:T(8,128)S(1)}, f32[512,512]{1,0:T(8,128)S(1)}, u32[]{:S(2)}, u32[]{:S(2)}) collective-permute-start(f32[512,512]{1,0:T(8,128)S(1)} %get-tuple-element.40.refs_8_), channel_id=1, source_target_pairs={{0,8},{8,0},{16,24},{24,16},{1,9},{9,1},{17,25},{25,17},{2,10},{10... | collective-permute-start | bytes 3145736 | tf_op jit(solution)/shard_map/ppermute | solution.py:372
  57.6 10.6 %collective-permute-start.10 = (f32[512,512]{1,0:T(8,128)S(1)}, f32[512,512]{1,0:T(8,128)S(1)}, u32[]{:S(2)}, u32[]{:S(2)}) collective-permute-start(f32[512,512]{1,0:T(8,128)S(1)} %get-tuple-element.38.refs_6_), channel_id=1, source_target_pairs={{0,8},{8,0},{16,24},{24,16},{1,9},{9,1},{17,25},{25,17},{2,10},{10... | collective-permute-start | bytes 3145736 | tf_op jit(solution)/shard_map/ppermute | solution.py:372
  57.7 18.1 %collective-permute-start.7 = (bf16[256,512]{1,0:T(8,128)(2,1)S(1)}, bf16[256,512]{1,0:T(8,128)(2,1)S(1)}, u32[]{:S(2)}, u32[]{:S(2)}) collective-permute-start(bf16[256,512]{1,0:T(8,128)(2,1)S(1)} %slice.50), channel_id=1, source_target_pairs={{0,1},{1,0},{2,3},{3,2},{4,5},{5,4},{6,7},{7,6},{8,9},{9,8},{10,11... | collective-permute-start | bytes 786440 | tf_op jit(solution)/shard_map/ppermute | solution.py:366
  59.3 16.5 %collective-permute-start.8 = (bf16[256,512]{1,0:T(8,128)(2,1)S(1)}, bf16[256,512]{1,0:T(8,128)(2,1)S(1)}, u32[]{:S(2)}, u32[]{:S(2)}) collective-permute-start(bf16[256,512]{1,0:T(8,128)(2,1)S(1)} %slice.51), channel_id=1, source_target_pairs={{0,2},{1,3},{2,6},{3,7},{6,4},{7,5},{4,0},{5,1},{8,10},{9,11},{10,... | collective-permute-start | bytes 786440 | tf_op jit(solution)/shard_map/ppermute | solution.py:363
  64.2 11.6 %collective-permute-start.9 = (f16[512,512]{1,0:T(8,128)(2,1)S(1)}, f16[512,512]{1,0:T(8,128)(2,1)S(1)}, u32[]{:S(2)}, u32[]{:S(2)}) collective-permute-start(f16[512,512]{1,0:T(8,128)(2,1)S(1)} %get-tuple-element.58), channel_id=1, source_target_pairs={{2,18},{3,19},{4,20},{5,21},{8,24},{9,25},{14,30},{15,31},{16,0},{... | collective-permute-start | bytes 1572872 | tf_op jit(solution)/shard_map/ppermute | solution.py:381
  66.9 27.9 %collective-permute-start.13 = (f16[512,512]{1,0:T(8,128)(2,1)}, f16[512,512]{1,0:T(8,128)(2,1)}, u32[]{:S(2)}, u32[]{:S(2)}) collective-permute-start(f16[512,512]{1,0:T(8,128)(2,1)} %get-tuple-element.54), channel_id=1, source_target_pairs={{2,18},{3,19},{4,20},{5,21},{8,24},{9,25},{14,30},{15,31},{16,0},{... | collective-permute-start | bytes 1572872 | tf_op jit(solution)/shard_map/ppermute | solution.py:381
  69.6 25.2 %collective-permute-start.14 = (f16[512,512]{1,0:T(8,128)(2,1)}, f16[512,512]{1,0:T(8,128)(2,1)}, u32[]{:S(2)}, u32[]{:S(2)}) collective-permute-start(f16[512,512]{1,0:T(8,128)(2,1)} %get-tuple-element.56), channel_id=1, source_target_pairs={{0,16},{1,17},{6,22},{7,23},{10,26},{11,27},{12,28},{13,29},{18,2}... | collective-permute-start | bytes 1572872 | tf_op jit(solution)/shard_map/ppermute | solution.py:381
  77.0 16.3 %collective-permute-start.12 = (f32[512,512]{1,0:T(8,128)S(1)}, f32[512,512]{1,0:T(8,128)}, u32[]{:S(2)}, u32[]{:S(2)}) collective-permute-start(f32[512,512]{1,0:T(8,128)S(1)} %get-tuple-element.46.refs_2_), channel_id=1, source_target_pairs={{0,8},{8,0},{16,24},{24,16},{1,9},{9,1},{17,25},{25,17},{2,10},{10... | collective-permute-start | bytes 3145736 | tf_op jit(solution)/shard_map/ppermute | solution.py:372
  77.1 5.4 %copy-start.12 = (s32[512]{0:T(512)S(1)}, s32[512]{0:T(512)}, u32[]{:S(2)}) copy-start(s32[512]{0:T(512)} %param.12) | copy-start | bytes 6148
  79.7 13.5 %all-to-all-start = ((f32[32,16,128]{2,1,0:T(8,128)}), f32[32,16,128]{2,1,0:T(8,128)S(1)}, u32[]{:S(2)}, u32[]{:S(2)}) async-start(f32[32,16,128]{2,1,0:T(8,128)} %bitcast.13), calls=%async_computation | async-start | bytes 524288 | tf_op jit(solution)/shard_map/all_to_all | solution.py:441
  82.6 4.0 %copy-start.13 = (f32[512]{0:T(512)S(1)}, f32[512]{0:T(512)}, u32[]{:S(2)}) copy-start(f32[512]{0:T(512)} %param.14) | copy-start | bytes 6148
  89.8 8.3 %copy-start.10 = (f16[512,512]{1,0:T(8,128)(2,1)S(1)}, f16[512,512]{1,0:T(8,128)(2,1)}, u32[]{:S(2)}) copy-start(f16[512,512]{1,0:T(8,128)(2,1)} %copy-done.9) | copy-start | bytes 1572868
  94.8 9.1 %collective-permute-start.15 = (f16[512,512]{1,0:T(8,128)(2,1)S(1)}, f16[512,512]{1,0:T(8,128)(2,1)S(1)}, u32[]{:S(2)}, u32[]{:S(2)}) collective-permute-start(f16[512,512]{1,0:T(8,128)(2,1)S(1)} %get-tuple-element.49), channel_id=1, source_target_pairs={{0,16},{1,17},{6,22},{7,23},{10,26},{11,27},{12,28},{13,29},{18,2}... | collective-permute-start | bytes 1572872 | tf_op jit(solution)/shard_map/ppermute | solution.py:381
  100.0 3.9 %copy-start.4 = (f32[512,512]{1,0:T(8,128)S(1)}, f32[512,512]{1,0:T(8,128)}, u32[]{:S(2)}) copy-start(f32[512,512]{1,0:T(8,128)} %get-tuple-element.55) | copy-start | bytes 3145732
  (6 other events, 10.5 us)
